TPU v7x, 32 devices: a whole 2x2x4 slice. The times are simulated.
32 devices in a mesh: groups: 2 (over y), seq: 4 (over z), head: 2 (over x), sub: 2 (over core).
Axes of the slice: x: 2, y: 2, z: 4, core: 2. Of those that a mesh axis runs over, the one named last changes fastest.
Arguments:
- token_values: bfloat16 [16384, 5120], P(('groups', 'seq', 'sub'), 'head'), parts along dimension 0, may hold values from -6 to 6
- gate_values: bfloat16 [16384, 5120], P(('groups', 'seq', 'sub'), 'head'), parts along dimension 0, may hold values from -80 to 80
- state_input: bfloat16 [16384, 128], P(('groups', 'seq', 'sub')), parts along dimension 0, may hold values from -6 to 6
- state_readout: bfloat16 [16384, 128], P(('groups', 'seq', 'sub')), parts along dimension 0, may hold values from -6 to 6
- step_raw: float32 [80, 8192], P('head', ('seq', 'sub')), may hold values from -3 to 16
- step_bias: float32 [80], P('head'), may hold values from -16 to -3
- decay_log: float32 [80], P('head'), may hold values from 0 to 2.78
- skip_gain: float32 [80], P('head'), may hold values from 0.5 to 2
- norm_gain: float32 [5120], P('head'), may hold values from 0.5 to 1.5
- document_ids: int32 [16384], P(('groups', 'seq', 'sub')), parts along dimension 0, may hold values from 0 to 8191, as said below
- live_blocks: int32 [16], P(('groups', 'seq', 'sub')), parts along dimension 0, may hold values from 1 to 4, as said below
Outputs:
- normalized: bfloat16 [16384, 5120], P(('groups', 'seq', 'sub'), 'head'), parts along dimension 0
There are 2 independent parts, one for each index of `groups`. A program takes and returns all parts, laid end to end along the dimension named above; an argument that names none is the same for every part. Nothing has to cross between parts.
Inputs may be any that keep to these rules, and one draw needn't show every extreme that they name: `document_ids`: never falling along the sequence, 0 at the first position, 8191 at the last, and unchanged over the padding positions that follow a shard's live blocks. `live_blocks`: the number of live blocks of 256 positions at the start of each shard of 1024 positions; the rest of a shard is padding; some shard has 4 and some has 1.
All inputs are finite; a program needn't handle non-finite values.
Results may differ from a plain program's by a relative error of at most 0.003.
Values sent between devices are 32-bit elements; how exact they have to be, the bound alone decides.
No kernel may reach another device: no remote copies, remote signals or barrier semaphores. Data moves between devices by JAX's collectives and lax.ppermute only.
A program may use at most 192 MiB of HBM per device.

v0:
```python
import functools
import math

import jax
import jax.numpy as jnp
import numpy as np
from jax import lax
from jax.experimental import pallas as pl
from jax.experimental.pallas import tpu as pltpu
from jax.sharding import PartitionSpec as P

BLOCK = 256
LANES = 128
LOG2E = math.log2(math.e)
F32 = jnp.float32
BF16 = jnp.bfloat16


def dot(a, b, contract=((1,), (0,))):
    return lax.dot_general(a, b, (contract, ((), ())), preferred_element_type=F32)


def two_parts(value):
    high = value.astype(BF16)
    low = (value - high.astype(F32)).astype(BF16)
    return high, low


def pick_row(ref, base, count, k, cols):
    row = ref[base : base + 1, cols]
    for j in range(1, count):
        row = jnp.where(k == j, ref[base + j : base + j + 1, cols], row)
    return row


def softplus(v):
    u = jnp.exp(-jnp.abs(v))
    s = u / (2.0 + u)
    q = s * s
    series = jnp.full_like(q, 1.0 / 17.0)
    for odd in (15, 13, 11, 9, 7, 5, 3, 1):
        series = series * q + 1.0 / odd
    return jnp.maximum(v, 0.0) + 2.0 * s * series


def state_kernel(
    heads,
    live_ref,
    docs_ref,
    sub_ref,
    raw_ref,
    par_ref,
    doc_row_ref,
    skip_ref,
    hot_ref,
    x_ref,
    b_ref,
    g_ref,
    col_ref,
    enter_ref,
    own_ref,
    aux_ref,
    sent_ref,
    row_ref,
    pack,
    decay_col,
    state,
    scal,
):
    k = pl.program_id(0)
    length = raw_ref.shape[1]
    count = length // BLOCK
    channels = x_ref.shape[1]
    tiles = channels // LANES
    ends = [docs_ref[j * BLOCK + BLOCK - 1] for j in range(count)]

    @pl.when(k == 0)
    def _():
        rows = raw_ref.shape[0]
        lane = lax.broadcasted_iota(jnp.int32, (1, length), 1)
        step = softplus(raw_ref[...] + par_ref[:, 0:1])
        step = jnp.where(lane < live_ref[0] * BLOCK, step, 0.0)
        cum = (-LOG2E * jnp.exp(par_ref[:, 1:2])) * step
        within = jnp.bitwise_and(lane, BLOCK - 1)
        shift = 1
        while shift < BLOCK:
            cum = cum + jnp.where(within >= shift, pltpu.roll(cum, shift, 1), 0.0)
            shift *= 2
        g = cum - jnp.where(step > 0.0, LOG2E * jnp.log(step), -1e30)
        for h in range(rows):
            g_ref[h] = g[h : h + 1, :]
        pack[...] = jnp.zeros_like(pack)
        pack[0:rows, :] = cum
        pack[LANES - 1 : LANES, :] = doc_row_ref[...].astype(F32)
        col_ref[...] = pack[...].T
        pack[LANES - 1 : LANES, :] = jnp.zeros((1, length), F32)
        for j in range(count):
            piece = slice(j * BLOCK, (j + 1) * BLOCK)
            last = cum[:, (j + 1) * BLOCK - 1 : (j + 1) * BLOCK]
            same = doc_row_ref[:, piece] == ends[j]
            pack[0:rows, piece] = jnp.where(
                same, step[:, piece] * jnp.exp2(last - cum[:, piece]), 0.0
            )
        high, low = two_parts(pack[...].T)
        decay_col[:, 0:LANES] = high
        decay_col[:, LANES:] = low
        head_lane = lax.broadcasted_iota(jnp.int32, (1, LANES), 1) < heads
        before = jnp.zeros((1, LANES), F32)
        scal[...] = jnp.zeros_like(scal)
        for j in range(count):
            end = jnp.where(head_lane, col_ref[(j + 1) * BLOCK - 1 : (j + 1) * BLOCK, :], 0.0)
            scal[j : j + 1, :] = jnp.where(head_lane, jnp.exp2(end), 0.0)
            scal[count + j : count + j + 1, :] = jnp.where(head_lane, jnp.exp2(before), 0.0)
            before = before + end
        scal[2 * count : 2 * count + 1, :] = jnp.where(head_lane, jnp.exp2(before), 0.0)
        scal[2 * count + 1 : 2 * count + 2, :] = skip_ref[...]
        high, low = two_parts(scal[...])
        hot = hot_ref[...]
        row_ref[...] = dot(high, hot) + dot(low, hot)
        state[...] = jnp.zeros_like(state)

    start = pl.multiple_of(k * BLOCK, BLOCK)
    end_doc = docs_ref[k * BLOCK + BLOCK - 1]
    prior_doc = docs_ref[jnp.maximum(k * BLOCK - 1, 0)]
    link = jnp.where(end_doc == prior_doc, 1.0, 0.0)
    decay = decay_col[pl.ds(start, BLOCK), :]
    inputs_t = b_ref[...].T
    wide = chunk_of(channels, 512)
    for c in range(0, channels, wide):
        cols = slice(c, c + wide)
        old = state[:, cols]
        enter_ref[0, :, cols] = old
        hot = hot_ref[:, cols]
        grown = dot(decay, jnp.concatenate([hot, hot], axis=0))
        scaled = (x_ref[:, cols].astype(F32) * grown).astype(BF16)
        passage = pick_row(row_ref, 0, count, k, cols) * link
        state[:, cols] = passage * old + dot(inputs_t, scaled)

    @pl.when(k == pl.num_programs(0) - 1)
    def _():
        half = state.shape[0] // 2
        full = jnp.where(ends[count - 1] == docs_ref[0], 1.0, 0.0)
        mine = pl.multiple_of(sub_ref[0] * half, half)
        theirs = pl.multiple_of((1 - sub_ref[0]) * half, half)
        aux_ref[...] = jnp.zeros_like(aux_ref)
        for j in range(tiles):
            cols = slice(j * LANES, (j + 1) * LANES)
            own_ref[j] = state[pl.ds(mine, half), cols]
            sent_ref[j * half : (j + 1) * half, :] = state[pl.ds(theirs, half), cols]
            aux_ref[j : j + 1, :] = row_ref[2 * count : 2 * count + 1, cols] * full
        aux_ref[tiles : tiles + 1, :] = jnp.full((1, LANES), docs_ref[0].astype(F32))
        aux_ref[tiles + 1 : tiles + 2, :] = jnp.full((1, LANES), docs_ref[length - 1].astype(F32))
        sent_ref[tiles * half :, :] = aux_ref[...]


def inner_kernel(
    heads,
    width,
    first_tile,
    count,
    live_ref,
    docs_ref,
    x_ref,
    z_ref,
    b_ref,
    c_ref,
    g_ref,
    col_ref,
    doc_row_ref,
    enter_ref,
    row_ref,
    hot_ref,
    *refs,
):
    y_ref, f_ref, affinity, turned, entry, passed = refs[-6:]
    k = pl.program_id(0)
    half = BLOCK // 2
    per_tile = LANES // width

    @pl.when(k >= live_ref[0])
    def _():
        y_ref[...] = jnp.zeros_like(y_ref)
        f_ref[...] = jnp.zeros_like(f_ref)

    @pl.when(k < live_ref[0])
    def _():
        readout = c_ref[...]
        doc_col = col_ref[:, LANES - 1 : LANES]
        doc_row = doc_row_ref[...].astype(F32)
        t = lax.broadcasted_iota(jnp.int32, (BLOCK, BLOCK), 0)
        s = lax.broadcasted_iota(jnp.int32, (BLOCK, BLOCK), 1)
        affinity[...] = jnp.where(
            (t >= s) & (doc_col == doc_row), dot(readout, b_ref[...], ((1,), (1,))), 0.0
        )
        prior_doc = docs_ref[jnp.maximum(k * BLOCK - 1, 0)]
        lane = lax.broadcasted_iota(jnp.int32, (1, LANES), 1)
        linked = (doc_col == prior_doc.astype(F32)) & (lane < heads)
        high, low = two_parts(jnp.where(linked, jnp.exp2(col_ref[...]), 0.0))
        entry[:, 0:LANES] = high
        entry[:, LANES:] = low
        turned[...] = pltpu.roll(
            col_ref[...], (LANES - first_tile * per_tile) % LANES, 1
        )
        reaches = jnp.where(prior_doc == docs_ref[0], 1.0, 0.0)
        passed[0:1, :] = pick_row(row_ref, count, count, k, slice(None)) * reaches
        twice = jnp.concatenate([readout, readout], axis=1)

        def tile(j, rest):
            cols = pl.ds(pl.multiple_of(j * LANES, LANES), LANES)
            x = x_ref[:, cols]
            columns = turned[...]
            tops, bottoms, masked = [], [], []
            for i in range(per_tile):
                cum = jnp.broadcast_to(columns[:, i : i + 1], (BLOCK, LANES))
                g = g_ref[(first_tile + j) * per_tile + i]
                left, right = g[:, :half], g[:, half:]
                top = jnp.exp2(jnp.minimum(cum[:half] - left, 64.0))
                bottom = jnp.exp2(cum[half:] - left)
                corner = jnp.exp2(jnp.minimum(cum[half:] - right, 64.0))
                tops.append((top * affinity[:half, :half]).astype(BF16))
                bottoms.append((bottom * affinity[half:, :half]).astype(BF16))
                bottoms.append((corner * affinity[half:, half:]).astype(BF16))
                mine = (lane >= i * width) & (lane < (i + 1) * width)
                masked.append(x * jnp.where(mine, 1.0, 0.0).astype(BF16))
            turned[...] = pltpu.roll(columns, LANES - per_tile, 1)
            upper = dot(
                jnp.concatenate(tops, axis=1),
                jnp.concatenate([m[:half] for m in masked], axis=0),
            )
            lower = dot(jnp.concatenate(bottoms, axis=1), jnp.concatenate(masked, axis=0))
            hot = hot_ref[:, cols]
            enter = dot(entry[...], jnp.concatenate([hot, hot], axis=0))
            high, low = two_parts(enter_ref[0, :, cols])
            outer = dot(twice, jnp.concatenate([high, low], axis=0))
            skip = row_ref[2 * count + 1 : 2 * count + 2, cols]
            y = jnp.concatenate([upper, lower], axis=0) + enter * outer + skip * x.astype(F32)
            z = z_ref[:, cols].astype(F32)
            gate = z / (1.0 + jnp.exp2(-LOG2E * z))
            y_ref[:, cols] = y * gate
            f_ref[:, cols] = (enter * gate * passed[0:1, cols]).astype(BF16)
            return rest

        lax.fori_loop(0, x_ref.shape[1] // LANES, tile, 0)


def join_kernel(sub_ref, own_ref, other_ref, c_ref, y_ref, f_ref, gated_ref, square_ref, total):
    k = pl.program_id(0)
    length = c_ref.shape[0]
    wide = y_ref.shape[1]
    start = pl.multiple_of(k * wide, wide)
    second = sub_ref[0] == 1

    @pl.when(k == 0)
    def _():
        total[...] = jnp.zeros_like(total)

    highs, lows = [], []
    for j in range(wide // LANES):
        own, other = own_ref[j], other_ref[j]
        carry = jnp.concatenate(
            [jnp.where(second, other, own), jnp.where(second, own, other)], axis=0
        )
        high, low = two_parts(carry)
        highs.append(high)
        lows.append(low)
    carry = jnp.concatenate(
        [jnp.concatenate(highs, axis=1), jnp.concatenate(lows, axis=1)], axis=0
    )
    for r in range(0, length, BLOCK):
        rows = slice(r, r + BLOCK)
        readout = c_ref[rows, :]
        outer = dot(jnp.concatenate([readout, readout], axis=1), carry)
        gated = y_ref[rows, :] + f_ref[rows, :].astype(F32) * outer
        gated_ref[rows, pl.ds(start, wide)] = gated
        square = total[rows, :]
        for j in range(wide // LANES):
            piece = gated[:, j * LANES : (j + 1) * LANES]
            square = square + piece * piece
        total[rows, :] = square

    @pl.when(k == pl.num_programs(0) - 1)
    def _():
        square_ref[...] = jnp.sum(total[...].T, axis=0, keepdims=True)


def norm_kernel(channels_all, square_ref, gain_ref, gated_ref, out_ref):
    rows = out_ref.shape[0]
    start = pl.multiple_of(pl.program_id(0) * rows, rows)
    scale = lax.rsqrt(square_ref[...] / channels_all + 1e-05)
    scale = jnp.broadcast_to(scale, (LANES, rows)).T
    for j in range(gated_ref.shape[1] // LANES):
        cols = slice(j * LANES, (j + 1) * LANES)
        gated = gated_ref[pl.ds(start, rows), cols]
        out_ref[:, cols] = (gated * gain_ref[:, cols] * scale).astype(BF16)


def chunk_of(total, most):
    wide = most
    while total % wide:
        wide -= LANES
    return wide


def whole(shape):
    return pl.BlockSpec(shape, lambda k, *_: (0,) * len(shape))


SMEM = pl.BlockSpec(memory_space=pltpu.SMEM)
VMEM = pl.BlockSpec(memory_space=pltpu.VMEM)


def plan(chips, tiles):
    chunks = 2 if tiles % 2 == 0 else 1
    hops = chunks + chips - 2
    pieces = 4 if tiles % 4 == 0 else 1
    return chunks, hops, pieces


def on_device(
    token_values,
    gate_values,
    state_input,
    state_readout,
    step_raw,
    step_bias,
    decay_log,
    skip_gain,
    norm_gain,
    document_ids,
    live_blocks,
):
    length, channels = token_values.shape
    heads = step_raw.shape[0]
    width = channels // heads
    states = state_input.shape[1]
    half = states // 2
    count = length // BLOCK
    tiles = channels // LANES
    rows = -(-heads // 8) * 8
    scalars = -(-(2 * count + 2) // 16) * 16
    extra = -(-(tiles + 2) // 8) * 8
    assert lax.axis_size("sub") == 2 and heads < LANES and 2 * half == states

    params = jnp.stack([step_bias, decay_log], axis=1)
    raw = step_raw
    if rows != heads:
        params = jnp.pad(params, ((0, rows - heads), (0, 0)))
        raw = jnp.pad(raw, ((0, rows - heads), (0, 0)))
    skip_row = jnp.pad(skip_gain, (0, LANES - heads)).reshape(1, LANES)
    doc_row = document_ids.reshape(1, length)
    sub = lax.axis_index("sub").astype(jnp.int32).reshape(1)
    hot = jnp.asarray(
        np.arange(LANES)[:, None] == np.arange(channels)[None, :] // width, dtype=BF16
    )

    g, col, enter, own, aux, sent, row = pl.pallas_call(
        functools.partial(state_kernel, heads),
        grid=(count,),
        in_specs=[
            SMEM,
            SMEM,
            SMEM,
            whole((rows, length)),
            whole((rows, 2)),
            whole((1, length)),
            whole((1, LANES)),
            whole((LANES, channels)),
            pl.BlockSpec((BLOCK, channels), lambda k: (k, 0)),
            pl.BlockSpec((BLOCK, states), lambda k: (k, 0)),
        ],
        out_specs=[
            whole((rows, 1, length)),
            whole((length, LANES)),
            pl.BlockSpec((1, states, channels), lambda k: (k, 0, 0)),
            whole((tiles, half, LANES)),
            whole((extra, LANES)),
            whole((tiles * half + extra, LANES)),
            whole((scalars, channels)),
        ],
        out_shape=[
            jax.ShapeDtypeStruct((rows, 1, length), F32),
            jax.ShapeDtypeStruct((length, LANES), F32),
            jax.ShapeDtypeStruct((count, states, channels), F32),
            jax.ShapeDtypeStruct((tiles, half, LANES), F32),
            jax.ShapeDtypeStruct((extra, LANES), F32),
            jax.ShapeDtypeStruct((tiles * half + extra, LANES), F32),
            jax.ShapeDtypeStruct((scalars, channels), F32),
        ],
        scratch_shapes=[
            pltpu.VMEM((LANES, length), F32),
            pltpu.VMEM((length, 2 * LANES), BF16),
            pltpu.VMEM((states, channels), F32),
            pltpu.VMEM((scalars, LANES), F32),
        ],
        name="shard_state",
    )(
        live_blocks,
        document_ids,
        sub,
        raw,
        params,
        doc_row,
        skip_row,
        hot,
        token_values,
        state_input,
    )

    pieces = plan(lax.axis_size("seq"), tiles)[2]
    wide = channels // pieces
    filled = ()
    for q in range(pieces):
        filled = pl.pallas_call(
            functools.partial(inner_kernel, heads, width, q * wide // LANES, count),
            grid=(count,),
            in_specs=[
                SMEM,
                SMEM,
                pl.BlockSpec((BLOCK, wide), lambda k, q=q: (k, q)),
                pl.BlockSpec((BLOCK, wide), lambda k, q=q: (k, q)),
                pl.BlockSpec((BLOCK, states), lambda k: (k, 0)),
                pl.BlockSpec((BLOCK, states), lambda k: (k, 0)),
                pl.BlockSpec((rows, 1, BLOCK), lambda k: (0, 0, k)),
                pl.BlockSpec((BLOCK, LANES), lambda k: (k, 0)),
                pl.BlockSpec((1, BLOCK), lambda k: (0, k)),
                pl.BlockSpec((1, states, wide), lambda k, q=q: (k, 0, q)),
                pl.BlockSpec((scalars, wide), lambda k, q=q: (0, q)),
                pl.BlockSpec((LANES, wide), lambda k, q=q: (0, q)),
            ]
            + [pl.BlockSpec(memory_space=pl.ANY)] * len(filled),
            out_specs=[pl.BlockSpec((BLOCK, wide), lambda k, q=q: (k, q))] * 2,
            out_shape=[
                jax.ShapeDtypeStruct((length, channels), F32),
                jax.ShapeDtypeStruct((length, channels), BF16),
            ],
            scratch_shapes=[
                pltpu.VMEM((BLOCK, BLOCK), F32),
                pltpu.VMEM((BLOCK, LANES), F32),
                pltpu.VMEM((BLOCK, 2 * LANES), BF16),
                pltpu.VMEM((8, wide), F32),
            ],
            input_output_aliases={12: 0, 13: 1} if filled else {},
            cost_estimate=pl.CostEstimate(
                flops=length * wide * 1200,
                bytes_accessed=length * wide * 10,
                transcendentals=0,
            ),
        )(
            live_blocks,
            document_ids,
            token_values,
            gate_values,
            state_input,
            state_readout,
            g,
            col,
            doc_row,
            enter,
            row,
            hot,
            *filled,
        )

    own, other = carry_in(own, aux, sent)

    joined = chunk_of(channels, 512)
    gated, squares = pl.pallas_call(
        join_kernel,
        grid=(channels // joined,),
        in_specs=[
            SMEM,
            pl.BlockSpec((joined // LANES, half, LANES), lambda k: (k, 0, 0)),
            pl.BlockSpec((joined // LANES, half, LANES), lambda k: (k, 0, 0)),
            whole((length, states)),
            pl.BlockSpec((length, joined), lambda k: (0, k)),
            pl.BlockSpec((length, joined), lambda k: (0, k)),
        ],
        out_specs=[VMEM, whole((1, length))],
        out_shape=[
            jax.ShapeDtypeStruct((length, channels), F32),
            jax.ShapeDtypeStruct((1, length), F32),
        ],
        scratch_shapes=[pltpu.VMEM((length, LANES), F32)],
        compiler_params=pltpu.CompilerParams(vmem_limit_bytes=40 << 20),
        name="join",
    )(sub, own, other, state_readout, *filled)

    squares = lax.psum(squares, "head")
    return pl.pallas_call(
        functools.partial(norm_kernel, channels * lax.axis_size("head")),
        grid=(count,),
        in_specs=[pl.BlockSpec((1, BLOCK), lambda k: (0, k)), whole((1, channels)), VMEM],
        out_specs=pl.BlockSpec((BLOCK, channels), lambda k: (k, 0)),
        out_shape=jax.ShapeDtypeStruct((length, channels), BF16),
        compiler_params=pltpu.CompilerParams(vmem_limit_bytes=40 << 20),
        name="norm",
    )(squares, norm_gain.reshape(1, channels), gated)


def carry_in(own, aux, sent):
    tiles, half, _ = own.shape
    body = tiles * half
    second = lax.axis_index("sub") == 1
    place, chips = lax.axis_index("seq"), lax.axis_size("seq")
    got = lax.ppermute(sent, "sub", [(0, 1), (1, 0)])
    got_state, got_aux = got[:body].reshape(tiles, half, LANES), got[body:]
    early = jnp.where(second, got_state, own)
    late = jnp.where(second, own, got_state)
    early_aux = jnp.where(second, got_aux, aux)
    late_aux = jnp.where(second, aux, got_aux)
    first, last = early_aux[tiles : tiles + 1], late_aux[tiles + 1 : tiles + 2]
    link = jnp.where(
        early_aux[tiles + 1 : tiles + 2] == late_aux[tiles : tiles + 1], 1.0, 0.0
    )
    early_decay = early_aux[:tiles].reshape(tiles, 1, LANES)
    late_decay = (late_aux[:tiles] * link).reshape(tiles, 1, LANES)
    chip_state = late_decay * early + late
    chip_decay = late_decay * early_decay

    chunks, hops, _ = plan(chips, tiles)
    size = tiles // chunks
    rows = size * half
    tail = jnp.broadcast_to(last, (8, LANES))

    def at(array, index):
        return lax.dynamic_slice_in_dim(array, index * size, size, 0)

    carry = jnp.zeros((size, half, LANES), F32)
    received = []
    for t in range(hops):
        index = jnp.clip(t - place, 0, chunks - 1)
        send = at(chip_decay, index) * carry + at(chip_state, index)
        send = jnp.concatenate([send.reshape(rows, LANES), tail], axis=0)
        pairs = [(z, z + 1) for z in range(chips - 1) if 0 <= t - z < chunks]
        got = lax.ppermute(send, "seq", pairs)
        joined = jnp.where(got[rows : rows + 1] == first, 1.0, 0.0)
        carry = joined[None] * got[:rows].reshape(size, half, LANES)
        received.append(carry)
    parts = []
    for c in range(chunks):
        part = jnp.zeros((size, half, LANES), F32)
        for z in range(1, chips):
            part = jnp.where(place == z, received[c + z - 1], part)
        parts.append(part)
    entering = jnp.concatenate(parts, axis=0)
    onward = link[None] * (early_decay * entering + early)
    mine = jnp.where(second, onward, entering)
    other = lax.ppermute(jnp.where(second, entering, onward), "sub", [(0, 1), (1, 0)])
    return mine, other


def solution(mesh):
    placed = (
        P(("groups", "seq", "sub"), "head"),
        P(("groups", "seq", "sub"), "head"),
        P(("groups", "seq", "sub"), None),
        P(("groups", "seq", "sub"), None),
        P("head", ("seq", "sub")),
        P("head"),
        P("head"),
        P("head"),
        P("head"),
        P(("groups", "seq", "sub")),
        P(("groups", "seq", "sub")),
    )

    return jax.shard_map(
        on_device,
        mesh=mesh,
        in_specs=placed,
        out_specs=P(("groups", "seq", "sub"), "head"),
        check_vma=False,
    )
```

profile of v0, /device:TPU:19, one launch (start us, length us, event | category | flops | bytes accessed | tf_op | source)
XLA Modules:
  0.0 127.8 jit_solution(4272034616081099110)
XLA Ops:
  0.7 0.7 pad_maximum_fusion.5
  1.3 0.7 copy.21.par_ref
  2.0 1.1 pad_bitcast_fusion.skip_ref
  3.2 11.0 %shard_state.1 = (f32[40,1,1024]{2,1,0:T(1,128)}, f32[1024,128]{1,0:T(8,128)}, f32[4,128,2560]{2,1,0:T(8,128)}, f32[20,64,128]{2,1,0:T(8,128)}, f32[24,128]{1,0:...) custom-call(s32[1]{0:T(128)S(6)} %copy.28.live_ref, s32[1024]{0:T(1024)} %docs_ref.9, s32[1]{0:T(128)} %bitcast.sub_ref, ...), custom_call_target="tpu_custom_call" | custom-call | tf_op jit(solution)/shard_map/shard_state/pallas_call | solution.py:356
  14.1 0.7 collective-permute-start
  14.9 2.0 %collective-permute-done = f32[1304,128]{1,0:T(8,128)S(1)} collective-permute-done((f32[1304,128]{1,0:T(8,128)}, f32[1304,128]{1,0:T(8,128)S(1)}, u32[]{:S(2)}, u32[]{:S(2)}) %collective-permute-start) | collective-permute-done | bytes 667680 | tf_op jit(solution)/shard_map/ppermute | solution.py:505
  16.8 0.7 slice_select_fusion.1
  17.6 1.2 select_add_fusion
  18.9 0.0 copy-start.3
  18.9 0.8 collective-permute-start.1
  19.8 0.0 collective-permute-done.1
  19.9 0.0 copy-start.4
  19.9 1.3 %collective-permute-start.2 = (f32[648,128]{1,0:T(8,128)S(1)}, f32[648,128]{1,0:T(8,128)S(1)}, u32[]{:S(2)}, u32[]{:S(2)}) collective-permute-start(f32[648,128]{1,0:T(8,128)S(1)} %pad_maximum_fusion.2), channel_id=1, source_target_pairs={{0,4},{4,8},{1,5},{5,9},{2,6},{6,10},{3,7},{7,11},{16,20},{20,24},... | collective-permute-start | bytes 995336 | tf_op jit(solution)/shard_map/ppermute | solution.py:535
  21.2 17.9 %collective-permute-done.2 = f32[648,128]{1,0:T(8,128)S(1)} collective-permute-done((f32[648,128]{1,0:T(8,128)S(1)}, f32[648,128]{1,0:T(8,128)S(1)}, u32[]{:S(2)}, u32[]{:S(2)}) %collective-permute-start.2) | collective-permute-done | bytes 331808 | tf_op jit(solution)/shard_map/ppermute | solution.py:535
  39.2 1.9 %collective-permute-start.3 = (f32[648,128]{1,0:T(8,128)S(1)}, f32[648,128]{1,0:T(8,128)S(1)}, u32[]{:S(2)}, u32[]{:S(2)}) collective-permute-start(f32[648,128]{1,0:T(8,128)S(1)} %pad_maximum_fusion.1), channel_id=1, source_target_pairs={{4,8},{8,12},{5,9},{9,13},{6,10},{10,14},{7,11},{11,15},{20,24},{2... | collective-permute-start | bytes 995336 | tf_op jit(solution)/shard_map/ppermute | solution.py:535
  41.2 7.5 %collective-permute-done.3 = f32[648,128]{1,0:T(8,128)S(1)} collective-permute-done((f32[648,128]{1,0:T(8,128)S(1)}, f32[648,128]{1,0:T(8,128)S(1)}, u32[]{:S(2)}, u32[]{:S(2)}) %collective-permute-start.3) | collective-permute-done | bytes 331808 | tf_op jit(solution)/shard_map/ppermute | solution.py:535
  48.8 2.2 %collective-permute-start.4 = (f32[648,128]{1,0:T(8,128)S(1)}, f32[648,128]{1,0:T(8,128)S(1)}, u32[]{:S(2)}, u32[]{:S(2)}) collective-permute-start(f32[648,128]{1,0:T(8,128)S(1)} %pad_maximum_fusion), channel_id=1, source_target_pairs={{8,12},{9,13},{10,14},{11,15},{24,28},{25,29},{26,30},{27,31}} | collective-permute-start | bytes 995336 | tf_op jit(solution)/shard_map/ppermute | solution.py:535
  51.0 4.7 %collective-permute-done.4 = f32[648,128]{1,0:T(8,128)S(1)} collective-permute-done((f32[648,128]{1,0:T(8,128)S(1)}, f32[648,128]{1,0:T(8,128)S(1)}, u32[]{:S(2)}, u32[]{:S(2)}) %collective-permute-start.4) | collective-permute-done | bytes 331808 | tf_op jit(solution)/shard_map/ppermute | solution.py:535
  55.8 0.1 select_select_fusion.1
  55.9 0.0 copy-done.3
  55.9 0.3 fusion
  56.2 3.3 %collective-permute-start.5 = (f32[20,64,128]{2,1,0:T(8,128)S(1)}, f32[20,64,128]{2,1,0:T(8,128)S(1)}, u32[]{:S(2)}, u32[]{:S(2)}) collective-permute-start(f32[20,64,128]{2,1,0:T(8,128)S(1)} %get-tuple-element.41), channel_id=1, source_target_pairs={{0,1},{1,0},{2,3},{3,2},{4,5},{5,4},{6,7},{7,6},{8,9},{9,8},{10,11... | collective-permute-start | bytes 1966088 | tf_op jit(solution)/shard_map/ppermute | solution.py:548
  59.5 0.0 copy-done.4
  59.5 11.0 %shard_map.118 = (f32[1024,2560]{1,0:T(8,128)}, bf16[1024,2560]{1,0:T(8,128)(2,1)}) custom-call(s32[1]{0:T(128)S(6)} %copy.28.live_ref, s32[1024]{0:T(1024)} %docs_ref.9, bf16[1024,2560]{1,0:T(8,128)(2,1)} %x_ref.9, bf16[1024,2560]{1,0:T(8,128)(2,1)} %z_ref.7, bf16[1024,128]{1,0:T(8,128)(2,1)} %b_ref.9, bf16[1024,128]{1,0:T(8,128)(2,1)} %c_ref.9, ...), custom_call_target="tpu_custom_call" | custom-call | flops 786432000 | bytes 6553600 | tf_op jit(solution)/shard_map/pallas_call | solution.py:413
  70.6 11.0 %shard_map.119 = (f32[1024,2560]{1,0:T(8,128)}, bf16[1024,2560]{1,0:T(8,128)(2,1)}) custom-call(s32[1]{0:T(128)S(6)} %copy.28.live_ref, s32[1024]{0:T(1024)} %docs_ref.9, bf16[1024,2560]{1,0:T(8,128)(2,1)} %x_ref.9, bf16[1024,2560]{1,0:T(8,128)(2,1)} %z_ref.7, bf16[1024,128]{1,0:T(8,128)(2,1)} %b_ref.9, ...), custom_call_target="tpu_custom_call", output_to_operand_aliasing={{0}: (12, {}), {1}: (13, {})} | custom-call | flops 786432000 | bytes 6553600 | tf_op jit(solution)/shard_map/pallas_call | solution.py:413
  81.6 11.1 %shard_map.120 = (f32[1024,2560]{1,0:T(8,128)}, bf16[1024,2560]{1,0:T(8,128)(2,1)}) custom-call(s32[1]{0:T(128)S(6)} %copy.28.live_ref, s32[1024]{0:T(1024)} %docs_ref.9, bf16[1024,2560]{1,0:T(8,128)(2,1)} %x_ref.9, bf16[1024,2560]{1,0:T(8,128)(2,1)} %z_ref.7, bf16[1024,128]{1,0:T(8,128)(2,1)} %b_ref.9, ...), custom_call_target="tpu_custom_call", output_to_operand_aliasing={{0}: (12, {}), {1}: (13, {})} | custom-call | flops 786432000 | bytes 6553600 | tf_op jit(solution)/shard_map/pallas_call | solution.py:413
  92.7 0.0 copy-start.2
  92.7 11.1 %shard_map.121 = (f32[1024,2560]{1,0:T(8,128)}, bf16[1024,2560]{1,0:T(8,128)(2,1)}) custom-call(s32[1]{0:T(128)S(6)} %copy.28.live_ref, s32[1024]{0:T(1024)} %docs_ref.9, bf16[1024,2560]{1,0:T(8,128)(2,1)} %x_ref.9, bf16[1024,2560]{1,0:T(8,128)(2,1)} %z_ref.7, bf16[1024,128]{1,0:T(8,128)(2,1)} %b_ref.9, ...), custom_call_target="tpu_custom_call", output_to_operand_aliasing={{0}: (12, {}), {1}: (13, {})} | custom-call | flops 786432000 | bytes 6553600 | tf_op jit(solution)/shard_map/pallas_call | solution.py:413
  103.8 0.0 collective-permute-done.5.other_ref
  103.8 0.0 copy-done.2
  103.8 0.0 copy-start
  103.8 2.5 %copy-done = bf16[1024,2560]{1,0:T(8,128)(2,1)S(1)} copy-done((bf16[1024,2560]{1,0:T(8,128)(2,1)S(1)}, bf16[1024,2560]{1,0:T(8,128)(2,1)}, u32[]{:S(2)}) %copy-start) | copy-done | bytes 5242904
  106.3 10.5 %join.1 = (f32[1024,2560]{1,0:T(8,128)}, f32[1,1024]{1,0:T(1,128)S(1)}) custom-call(s32[1]{0:T(128)} %bitcast.sub_ref, f32[20,64,128]{2,1,0:T(8,128)S(1)} %get-tuple-element.42.own_ref, f32[20,64,128]{2,1,0:T(8,128)S(1)} %collective-permute-done.5.other_ref, bf16[1024,128]{1,0:T(8,128)(2,1)S(1)} %copy-done.2, f32[1024,2560]{1,0:T(8,128)} %get-tuple-element.35.y_ref, ...), custom_call_target="tpu_custom_call" | custom-call | tf_op jit(solution)/shard_map/join/pallas_call | solution.py:467
  116.8 3.8 %psum.7.square_ref = f32[1,1024]{1,0:T(1,128)S(1)} all-reduce(f32[1,1024]{1,0:T(1,128)S(1)} %get-tuple-element.37), channel_id=1, replica_groups=mesh['groups'=2,'seq'=4,'head'=2,'sub'=2] {'head'}, use_global_device_ids=true, to_apply=%region_0.1 | all-reduce | flops 1024 | bytes 8192 | tf_op jit(solution)/shard_map/psum | solution.py:488
  120.5 0.0 copy-start.1
  120.5 4.0 %copy-done.1 = f32[1024,2560]{1,0:T(8,128)S(1)} copy-done((f32[1024,2560]{1,0:T(8,128)S(1)}, f32[1024,2560]{1,0:T(8,128)}, u32[]{:S(2)}) %copy-start.1) | copy-done | bytes 10485784
  124.5 3.3 %norm.1 = bf16[1024,2560]{1,0:T(8,128)(2,1)} custom-call(f32[1,1024]{1,0:T(1,128)S(1)} %psum.7.square_ref, f32[1,2560]{1,0:T(1,128)S(1)} %reshape.69.gain_ref, f32[1024,2560]{1,0:T(8,128)S(1)} %copy-done.1), custom_call_target="tpu_custom_call" | custom-call | tf_op jit(solution)/shard_map/norm/pallas_call | solution.py:489
  (22 shorter events, 0.5 us)
Async XLA Ops:
  14.1 2.7 %collective-permute-start = (f32[1304,128]{1,0:T(8,128)}, f32[1304,128]{1,0:T(8,128)S(1)}, u32[]{:S(2)}, u32[]{:S(2)}) collective-permute-start(f32[1304,128]{1,0:T(8,128)} %get-tuple-element.22), channel_id=1, source_target_pairs={{0,1},{1,0},{2,3},{3,2},{4,5},{5,4},{6,7},{7,6},{8,9},{9,8},{10,11... | collective-permute-start | bytes 2002952 | tf_op jit(solution)/shard_map/ppermute | solution.py:505
  18.9 37.1 %copy-start.3 = (f32[20,64,128]{2,1,0:T(8,128)S(1)}, f32[20,64,128]{2,1,0:T(8,128)}, u32[]{:S(2)}) copy-start(f32[20,64,128]{2,1,0:T(8,128)} %get-tuple-element.24) | copy-start | bytes 1966084
  18.9 0.8 collective-permute-start.1
  19.9 39.6 %copy-start.4 = (f32[2560]{0:T(1024)S(1)}, f32[2560]{0:T(1024)}, u32[]{:S(2)}) copy-start(f32[2560]{0:T(1024)} %param.20) | copy-start | bytes 30724
  19.9 19.2 %collective-permute-start.2 = (f32[648,128]{1,0:T(8,128)S(1)}, f32[648,128]{1,0:T(8,128)S(1)}, u32[]{:S(2)}, u32[]{:S(2)}) collective-permute-start(f32[648,128]{1,0:T(8,128)S(1)} %pad_maximum_fusion.2), channel_id=1, source_target_pairs={{0,4},{4,8},{1,5},{5,9},{2,6},{6,10},{3,7},{7,11},{16,20},{20,24},... | collective-permute-start | bytes 995336 | tf_op jit(solution)/shard_map/ppermute | solution.py:535
  39.2 9.4 %collective-permute-start.3 = (f32[648,128]{1,0:T(8,128)S(1)}, f32[648,128]{1,0:T(8,128)S(1)}, u32[]{:S(2)}, u32[]{:S(2)}) collective-permute-start(f32[648,128]{1,0:T(8,128)S(1)} %pad_maximum_fusion.1), channel_id=1, source_target_pairs={{4,8},{8,12},{5,9},{9,13},{6,10},{10,14},{7,11},{11,15},{20,24},{2... | collective-permute-start | bytes 995336 | tf_op jit(solution)/shard_map/ppermute | solution.py:535
  48.8 7.0 %collective-permute-start.4 = (f32[648,128]{1,0:T(8,128)S(1)}, f32[648,128]{1,0:T(8,128)S(1)}, u32[]{:S(2)}, u32[]{:S(2)}) collective-permute-start(f32[648,128]{1,0:T(8,128)S(1)} %pad_maximum_fusion), channel_id=1, source_target_pairs={{8,12},{9,13},{10,14},{11,15},{24,28},{25,29},{26,30},{27,31}} | collective-permute-start | bytes 995336 | tf_op jit(solution)/shard_map/ppermute | solution.py:535
  56.2 47.6 %collective-permute-start.5 = (f32[20,64,128]{2,1,0:T(8,128)S(1)}, f32[20,64,128]{2,1,0:T(8,128)S(1)}, u32[]{:S(2)}, u32[]{:S(2)}) collective-permute-start(f32[20,64,128]{2,1,0:T(8,128)S(1)} %get-tuple-element.41), channel_id=1, source_target_pairs={{0,1},{1,0},{2,3},{3,2},{4,5},{5,4},{6,7},{7,6},{8,9},{9,8},{10,11... | collective-permute-start | bytes 1966088 | tf_op jit(solution)/shard_map/ppermute | solution.py:548
  92.7 11.1 %copy-start.2 = (bf16[1024,128]{1,0:T(8,128)(2,1)S(1)}, bf16[1024,128]{1,0:T(8,128)(2,1)}, u32[]{:S(2)}) copy-start(bf16[1024,128]{1,0:T(8,128)(2,1)} %c_ref.9) | copy-start | bytes 786436
  103.8 2.5 %copy-start = (bf16[1024,2560]{1,0:T(8,128)(2,1)S(1)}, bf16[1024,2560]{1,0:T(8,128)(2,1)}, u32[]{:S(2)}) copy-start(bf16[1024,2560]{1,0:T(8,128)(2,1)} %get-tuple-element.36.f_ref) | copy-start | bytes 15728644
  120.5 4.0 %copy-start.1 = (f32[1024,2560]{1,0:T(8,128)S(1)}, f32[1024,2560]{1,0:T(8,128)}, u32[]{:S(2)}) copy-start(f32[1024,2560]{1,0:T(8,128)} %get-tuple-element.38.gated_ref) | copy-start | bytes 31457284
where the time goes:
time: 129 us; the launch traced here: 128 us
  Pallas kernels  68.9 us (53%)
  waiting for transfers between devices  32.1 us (25%)
  starting transfers between devices  10.3 us (8%)
  local copies, waits for them, and re-layouts  8.45 us (7%)
  blocking collectives  3.76 us (3%)
  other arithmetic  3.33 us (3%)
    pallas_call x4, Pallas kernels, on_device(): pl.pallas_call(functools.partial(inner_kernel, heads, width, q * wide //...  44.2 us
    ppermute x4, waiting for transfers between devices, carry_in(): got = lax.ppermute(send, 'seq', pairs)  30.1 us
    pallas_call x1, Pallas kernels, on_device(): pl.pallas_call(functools.partial(state_kernel, heads), grid=(count,), in_...  11 us
    pallas_call x1, Pallas kernels, on_device(): pl.pallas_call(join_kernel, grid=(channels // joined,), in_specs=[SMEM, p...  10.5 us
    unnamed x10, local copies, waits for them, and re-layouts  6.47 us
    ppermute x4, starting transfers between devices, carry_in(): got = lax.ppermute(send, 'seq', pairs)  6.24 us
    psum x1, blocking collectives, on_device(): squares = lax.psum(squares, 'head')  3.76 us
    ppermute x1, starting transfers between devices, carry_in(): lax.ppermute(jnp.where(second, entering, onward), 'sub', [(0, 1), (1, 0)])  3.3 us
  transfers between devices with their start and end apart: 6, of which 4 were waited for; matrix products, arithmetic and copies ran while one was open for 0% of the time, Pallas kernels for 35%

commit v1 on v0

v1 whole, which is shorter than its diff:
```python
import functools
import math

import jax
import jax.numpy as jnp
import numpy as np
from jax import lax
from jax.experimental import pallas as pl
from jax.experimental.pallas import tpu as pltpu
from jax.sharding import PartitionSpec as P

BLOCK = 256
LANES = 128
LOG2E = math.log2(math.e)
F32 = jnp.float32
BF16 = jnp.bfloat16


def dot(a, b, contract=((1,), (0,))):
    return lax.dot_general(a, b, (contract, ((), ())), preferred_element_type=F32)


def two_parts(value):
    high = value.astype(BF16)
    low = (value - high.astype(F32)).astype(BF16)
    return high, low


def pick_row(ref, base, count, k, cols):
    row = ref[base : base + 1, cols]
    for j in range(1, count):
        row = jnp.where(k == j, ref[base + j : base + j + 1, cols], row)
    return row


def softplus(v):
    u = jnp.exp(-jnp.abs(v))
    s = u / (2.0 + u)
    q = s * s
    series = jnp.full_like(q, 1.0 / 15.0)
    for odd in (13, 11, 9, 7, 5, 3, 1):
        series = series * q + 1.0 / odd
    return jnp.maximum(v, 0.0) + 2.0 * s * series


def state_kernel(
    heads,
    live_ref,
    docs_ref,
    sub_ref,
    raw_ref,
    bias_ref,
    decay_ref,
    skip_ref,
    doc_row_ref,
    tri_ref,
    hot_ref,
    hot_low_ref,
    x_ref,
    b_ref,
    g_ref,
    col_ref,
    enter_ref,
    own_ref,
    sent_ref,
    row_ref,
    pack,
    col_parts,
    inputs_t,
    state,
    scal,
):
    length = raw_ref.shape[0 + 1]
    rows = raw_ref.shape[0]
    count = length // BLOCK
    wide = x_ref.shape[1]
    ends = [docs_ref[j * BLOCK + BLOCK - 1] for j in range(count)]

    @pl.when(pl.program_id(0) == 0)
    def _():
        inputs_t[...] = b_ref[...].T
        pack[...] = jnp.zeros_like(pack)
        pack[0:1, 0:heads] = bias_ref[...]
        pack[1:2, 0:heads] = decay_ref[...]
        params = pack[0:LANES, 0:LANES].T
        lane = lax.broadcasted_iota(jnp.int32, (1, length), 1)
        step = softplus(raw_ref[...] + params[0:rows, 0:1])
        step = jnp.where(lane < live_ref[0] * BLOCK, step, 0.0)
        rate = (-LOG2E * jnp.exp(params[0:rows, 1:2])) * step
        high, _ = two_parts(rate)
        middle, low = two_parts(rate - high.astype(F32))
        tri = tri_ref[...]
        logs = jnp.where(step > 0.0, LOG2E * jnp.log(step), -1e30)
        for j in range(count):
            piece = slice(j * BLOCK, (j + 1) * BLOCK)
            cum = dot(high[:, piece], tri) + (dot(middle[:, piece], tri) + dot(low[:, piece], tri))
            g_ref[:, piece] = cum - logs[:, piece]
            same = doc_row_ref[:, piece] == ends[j]
            pack[0:rows, piece] = cum
            pack[rows : 2 * rows, piece] = jnp.where(
                same, step[:, piece] * jnp.exp2(cum[:, BLOCK - 1 :] - cum), 0.0
            )
        pack[LANES - 1 : LANES, :] = doc_row_ref[...].astype(F32)
        for j in range(count):
            piece = slice(j * BLOCK, (j + 1) * BLOCK)
            turned = pack[:, piece].T
            col_ref[piece, :] = turned
            high, low = two_parts(turned)
            col_parts[piece, 0:LANES] = high
            col_parts[piece, LANES:] = low
        head_lane = lax.broadcasted_iota(jnp.int32, (1, LANES), 1) < heads
        before = jnp.zeros((1, LANES), F32)
        scal[...] = jnp.zeros_like(scal)
        for j in range(count):
            end = jnp.where(head_lane, col_ref[(j + 1) * BLOCK - 1 : (j + 1) * BLOCK, :], 0.0)
            scal[j : j + 1, :] = jnp.where(head_lane, jnp.exp2(end), 0.0)
            scal[count + j : count + j + 1, :] = jnp.where(head_lane, jnp.exp2(before), 0.0)
            before = before + end
        scal[2 * count : 2 * count + 1, :] = jnp.where(head_lane, jnp.exp2(before), 0.0)
        scal[2 * count + 1 : 2 * count + 2, 0:heads] = skip_ref[...]

    hot = hot_ref[...]
    high, low = two_parts(scal[...])
    row = dot(high, hot) + dot(low, hot)
    row_ref[...] = row
    hot_low = jnp.concatenate([hot_low_ref[...]] * 2, axis=0)
    state[...] = jnp.zeros_like(state)
    for j in range(count):
        piece = slice(j * BLOCK, (j + 1) * BLOCK)
        prior = docs_ref[max(j * BLOCK - 1, 0)]
        passage = row[j : j + 1, :] * jnp.where(ends[j] == prior, 1.0, 0.0)
        grown = dot(col_parts[piece, :], hot_low)
        scaled = (x_ref[piece, :].astype(F32) * grown).astype(BF16)
        old = state[...]
        enter_ref[j] = old
        state[...] = passage * old + dot(inputs_t[:, piece], scaled)

    half = state.shape[0] // 2
    total = row[2 * count : 2 * count + 1, :] * jnp.where(ends[count - 1] == docs_ref[0], 1.0, 0.0)
    mine = pl.multiple_of(sub_ref[0] * half, half)
    theirs = pl.multiple_of((1 - sub_ref[0]) * half, half)
    line = lax.broadcasted_iota(jnp.int32, (8, LANES), 0)
    first, last = docs_ref[0].astype(F32), docs_ref[length - 1].astype(F32)
    for j in range(wide // LANES):
        cols = slice(j * LANES, (j + 1) * LANES)
        foot = jnp.where(line == 0, total[:, cols], jnp.where(line == 1, first, last))
        own_ref[j, 0:half, :] = state[pl.ds(mine, half), cols]
        sent_ref[j, 0:half, :] = state[pl.ds(theirs, half), cols]
        own_ref[j, half:, :] = foot
        sent_ref[j, half:, :] = foot


def prepare_kernel(heads, docs_ref, b_ref, c_ref, col_ref, doc_row_ref, affinity_ref, entry_ref):
    k = pl.program_id(0)
    doc_col = col_ref[:, LANES - 1 : LANES]
    doc_row = doc_row_ref[...].astype(F32)
    t = lax.broadcasted_iota(jnp.int32, (BLOCK, BLOCK), 0)
    s = lax.broadcasted_iota(jnp.int32, (BLOCK, BLOCK), 1)
    affinity_ref[0] = jnp.where(
        (t >= s) & (doc_col == doc_row), dot(c_ref[...], b_ref[...], ((1,), (1,))), 0.0
    )
    prior_doc = docs_ref[jnp.maximum(k * BLOCK - 1, 0)].astype(F32)
    lane = lax.broadcasted_iota(jnp.int32, (1, LANES), 1)
    linked = (doc_col == prior_doc) & (lane < heads)
    high, low = two_parts(jnp.where(linked, jnp.exp2(col_ref[...]), 0.0))
    entry_ref[:, 0:LANES] = high
    entry_ref[:, LANES:] = low


def inner_kernel(
    width,
    first_tile,
    group,
    count,
    live_ref,
    docs_ref,
    x_ref,
    z_ref,
    c_ref,
    g_ref,
    col_ref,
    affinity_ref,
    entry_ref,
    enter_ref,
    row_ref,
    hot_ref,
    *refs,
):
    y_ref, f_ref = refs[-2:]
    k = pl.program_id(0)
    half = BLOCK // 2
    per_tile = LANES // width

    @pl.when(k >= live_ref[0])
    def _():
        y_ref[...] = jnp.zeros_like(y_ref)
        f_ref[...] = jnp.zeros_like(f_ref)

    @pl.when(k < live_ref[0])
    def _():
        readout = c_ref[...]
        twice = jnp.concatenate([readout, readout], axis=1)
        lane = lax.broadcasted_iota(jnp.int32, (1, LANES), 1)
        nothing = jnp.zeros((BLOCK, LANES), BF16)
        reaches = jnp.where(docs_ref[jnp.maximum(k * BLOCK - 1, 0)] == docs_ref[0], 1.0, 0.0)
        passed = pick_row(row_ref, count, count, k, slice(None)) * reaches
        for q in range(x_ref.shape[1] // (group * LANES)):
            cols = slice(q * group * LANES, (q + 1) * group * LANES)
            x = x_ref[:, cols]
            tops, bottoms, masked = [], [], []
            for u in range(group):
                part = x[:, u * LANES : (u + 1) * LANES]
                for i in range(per_tile):
                    h = (first_tile + q * group + u) * per_tile + i
                    cum = jnp.broadcast_to(col_ref[:, h : h + 1], (BLOCK, LANES))
                    left, right = g_ref[h : h + 1, :half], g_ref[h : h + 1, half:]
                    top = jnp.exp2(jnp.minimum(cum[:half] - left, 64.0))
                    bottom = jnp.exp2(cum[half:] - left)
                    corner = jnp.exp2(jnp.minimum(cum[half:] - right, 64.0))
                    tops.append((top * affinity_ref[0, :half, :half]).astype(BF16))
                    bottoms.append((bottom * affinity_ref[0, half:, :half]).astype(BF16))
                    bottoms.append((corner * affinity_ref[0, half:, half:]).astype(BF16))
                    mine = (lane >= i * width) & (lane < (i + 1) * width)
                    kept = part * jnp.where(mine, 1.0, 0.0).astype(BF16)
                    masked.append(
                        jnp.concatenate(
                            [kept if v == u else nothing for v in range(group)], axis=1
                        )
                    )
            upper = dot(
                jnp.concatenate(tops, axis=1),
                jnp.concatenate([m[:half] for m in masked], axis=0),
            )
            lower = dot(jnp.concatenate(bottoms, axis=1), jnp.concatenate(masked, axis=0))
            hot = hot_ref[:, cols]
            enter = dot(entry_ref[...], jnp.concatenate([hot, hot], axis=0))
            high, low = two_parts(enter_ref[0, :, cols])
            outer = dot(twice, jnp.concatenate([high, low], axis=0))
            skip = row_ref[2 * count + 1 : 2 * count + 2, cols]
            y = jnp.concatenate([upper, lower], axis=0) + enter * outer + skip * x.astype(F32)
            z = z_ref[:, cols].astype(F32)
            gate = z / (1.0 + jnp.exp2(-LOG2E * z))
            y_ref[:, cols] = y * gate
            f_ref[:, cols] = (enter * gate * passed[:, cols]).astype(BF16)


def join_kernel(sub_ref, own_ref, other_ref, c_ref, y_ref, f_ref, gated_ref, square_ref, total):
    k = pl.program_id(0)
    length = c_ref.shape[0]
    wide = own_ref.shape[0] * LANES
    here = pl.ds(pl.multiple_of(k * wide, wide), wide)
    second = sub_ref[0] == 1

    @pl.when(k == 0)
    def _():
        total[...] = jnp.zeros_like(total)

    highs, lows = [], []
    for j in range(wide // LANES):
        own, other = own_ref[j], other_ref[j]
        carry = jnp.concatenate(
            [jnp.where(second, other, own), jnp.where(second, own, other)], axis=0
        )
        high, low = two_parts(carry)
        highs.append(high)
        lows.append(low)
    carry = jnp.concatenate(
        [jnp.concatenate(highs, axis=1), jnp.concatenate(lows, axis=1)], axis=0
    )
    for r in range(0, length, BLOCK):
        rows = slice(r, r + BLOCK)
        readout = c_ref[rows, :]
        outer = dot(jnp.concatenate([readout, readout], axis=1), carry)
        gated = y_ref[rows, here] + f_ref[rows, here].astype(F32) * outer
        gated_ref[rows, here] = gated
        square = total[rows, :]
        for j in range(wide // LANES):
            piece = gated[:, j * LANES : (j + 1) * LANES]
            square = square + piece * piece
        total[rows, :] = square

    @pl.when(k == pl.num_programs(0) - 1)
    def _():
        square_ref[...] = jnp.sum(total[...].T, axis=0, keepdims=True)


def norm_kernel(channels_all, square_ref, more_ref, gain_ref, gated_ref, out_ref):
    rows = out_ref.shape[0]
    start = pl.multiple_of(pl.program_id(0) * rows, rows)
    scale = lax.rsqrt((square_ref[...] + more_ref[...]) / channels_all + 1e-05)
    scale = jnp.broadcast_to(scale, (LANES, rows)).T
    for j in range(gated_ref.shape[1] // LANES):
        cols = slice(j * LANES, (j + 1) * LANES)
        gated = gated_ref[pl.ds(start, rows), cols]
        out_ref[:, cols] = (gated * gain_ref[:, cols] * scale).astype(BF16)


def chunk_of(total, most):
    wide = most
    while total % wide:
        wide -= LANES
    return wide


def whole(shape):
    return pl.BlockSpec(shape, lambda k, *_: (0,) * len(shape))


SMEM = pl.BlockSpec(memory_space=pltpu.SMEM)
VMEM = pl.BlockSpec(memory_space=pltpu.VMEM)


def plan(chips, tiles):
    chunks = 2 if tiles % 2 == 0 else 1
    hops = chunks + chips - 2
    group = 2 if tiles % 2 == 0 else 1
    pieces = 5 if tiles % (5 * group) == 0 else 1
    return chunks, hops, group, pieces


def on_device(
    token_values,
    gate_values,
    state_input,
    state_readout,
    step_raw,
    step_bias,
    decay_log,
    skip_gain,
    norm_gain,
    document_ids,
    live_blocks,
):
    length, channels = token_values.shape
    heads = step_raw.shape[0]
    width = channels // heads
    states = state_input.shape[1]
    half = states // 2
    count = length // BLOCK
    tiles = channels // LANES
    rows = -(-heads // 8) * 8
    scalars = -(-(2 * count + 2) // 16) * 16
    assert lax.axis_size("sub") == 2 and 2 * rows < LANES and states == LANES

    raw = step_raw
    if rows != heads:
        raw = jnp.pad(raw, ((0, rows - heads), (0, 0)))
    doc_row = document_ids.reshape(1, length)
    sub = lax.axis_index("sub").astype(jnp.int32).reshape(1)
    head_of = np.arange(channels)[None, :] // width
    lanes = np.arange(LANES)[:, None]
    hot = jnp.asarray(lanes == head_of, dtype=BF16)
    hot_low = jnp.asarray(lanes == head_of + rows, dtype=BF16)
    tri = jnp.asarray(np.triu(np.ones((BLOCK, BLOCK))), dtype=BF16)

    chunk = chunk_of(channels, 512)
    per_chunk = chunk // LANES
    g, col, enter, own, sent, row = pl.pallas_call(
        functools.partial(state_kernel, heads),
        grid=(channels // chunk,),
        in_specs=[
            SMEM,
            SMEM,
            SMEM,
            whole((rows, length)),
            whole((1, heads)),
            whole((1, heads)),
            whole((1, heads)),
            whole((1, length)),
            whole((BLOCK, BLOCK)),
            pl.BlockSpec((LANES, chunk), lambda c: (0, c)),
            pl.BlockSpec((LANES, chunk), lambda c: (0, c)),
            pl.BlockSpec((length, chunk), lambda c: (0, c)),
            whole((length, states)),
        ],
        out_specs=[
            whole((rows, length)),
            whole((length, LANES)),
            pl.BlockSpec((count, states, chunk), lambda c: (0, 0, c)),
            pl.BlockSpec((per_chunk, half + 8, LANES), lambda c: (c, 0, 0)),
            pl.BlockSpec((per_chunk, half + 8, LANES), lambda c: (c, 0, 0)),
            pl.BlockSpec((scalars, chunk), lambda c: (0, c)),
        ],
        out_shape=[
            jax.ShapeDtypeStruct((rows, length), F32),
            jax.ShapeDtypeStruct((length, LANES), F32),
            jax.ShapeDtypeStruct((count, states, channels), F32),
            jax.ShapeDtypeStruct((tiles, half + 8, LANES), F32),
            jax.ShapeDtypeStruct((tiles, half + 8, LANES), F32),
            jax.ShapeDtypeStruct((scalars, channels), F32),
        ],
        scratch_shapes=[
            pltpu.VMEM((LANES, length), F32),
            pltpu.VMEM((length, 2 * LANES), BF16),
            pltpu.VMEM((states, length), BF16),
            pltpu.VMEM((states, chunk), F32),
            pltpu.VMEM((scalars, LANES), F32),
        ],
        compiler_params=pltpu.CompilerParams(vmem_limit_bytes=24 << 20),
        name="shard_state",
    )(
        live_blocks,
        document_ids,
        sub,
        raw,
        step_bias.reshape(1, heads),
        decay_log.reshape(1, heads),
        skip_gain.reshape(1, heads),
        doc_row,
        tri,
        hot,
        hot_low,
        token_values,
        state_input,
    )

    affinity, entry = pl.pallas_call(
        functools.partial(prepare_kernel, heads),
        grid=(count,),
        in_specs=[
            SMEM,
            pl.BlockSpec((BLOCK, states), lambda k: (k, 0)),
            pl.BlockSpec((BLOCK, states), lambda k: (k, 0)),
            pl.BlockSpec((BLOCK, LANES), lambda k: (k, 0)),
            pl.BlockSpec((1, BLOCK), lambda k: (0, k)),
        ],
        out_specs=[
            pl.BlockSpec((1, BLOCK, BLOCK), lambda k: (k, 0, 0)),
            pl.BlockSpec((BLOCK, 2 * LANES), lambda k: (k, 0)),
        ],
        out_shape=[
            jax.ShapeDtypeStruct((count, BLOCK, BLOCK), F32),
            jax.ShapeDtypeStruct((length, 2 * LANES), BF16),
        ],
        compiler_params=pltpu.CompilerParams(vmem_limit_bytes=16 << 20),
        name="prepare",
    )(document_ids, state_input, state_readout, col, doc_row)

    group, pieces = plan(lax.axis_size("seq"), tiles)[2:]
    wide = channels // pieces
    filled = ()
    for q in range(pieces):
        filled = pl.pallas_call(
            functools.partial(inner_kernel, width, q * wide // LANES, group, count),
            grid=(count,),
            in_specs=[
                SMEM,
                SMEM,
                pl.BlockSpec((BLOCK, wide), lambda k, q=q: (k, q)),
                pl.BlockSpec((BLOCK, wide), lambda k, q=q: (k, q)),
                pl.BlockSpec((BLOCK, states), lambda k: (k, 0)),
                pl.BlockSpec((rows, BLOCK), lambda k: (0, k)),
                pl.BlockSpec((BLOCK, LANES), lambda k: (k, 0)),
                pl.BlockSpec((1, BLOCK, BLOCK), lambda k: (k, 0, 0)),
                pl.BlockSpec((BLOCK, 2 * LANES), lambda k: (k, 0)),
                pl.BlockSpec((1, states, wide), lambda k, q=q: (k, 0, q)),
                pl.BlockSpec((scalars, wide), lambda k, q=q: (0, q)),
                pl.BlockSpec((LANES, wide), lambda k, q=q: (0, q)),
            ]
            + [pl.BlockSpec(memory_space=pl.ANY)] * len(filled),
            out_specs=[pl.BlockSpec((BLOCK, wide), lambda k, q=q: (k, q))] * 2,
            out_shape=[
                jax.ShapeDtypeStruct((length, channels), F32),
                jax.ShapeDtypeStruct((length, channels), BF16),
            ],
            input_output_aliases={12: 0, 13: 1} if filled else {},
            cost_estimate=pl.CostEstimate(
                flops=length * wide * 1200,
                bytes_accessed=length * wide * 10,
                transcendentals=0,
            ),
            compiler_params=pltpu.CompilerParams(vmem_limit_bytes=16 << 20),
        )(
            live_blocks,
            document_ids,
            token_values,
            gate_values,
            state_readout,
            g,
            col,
            affinity,
            entry,
            enter,
            row,
            hot,
            *filled,
        )

    own, other = carry_in(own, sent, half)

    gated, squares = pl.pallas_call(
        join_kernel,
        grid=(channels // chunk,),
        in_specs=[
            SMEM,
            pl.BlockSpec((per_chunk, half, LANES), lambda k: (k, 0, 0)),
            pl.BlockSpec((per_chunk, half, LANES), lambda k: (k, 0, 0)),
            whole((length, states)),
            VMEM,
            VMEM,
        ],
        out_specs=[VMEM, whole((1, length))],
        out_shape=[
            jax.ShapeDtypeStruct((length, channels), F32),
            jax.ShapeDtypeStruct((1, length), F32),
        ],
        scratch_shapes=[pltpu.VMEM((length, LANES), F32)],
        compiler_params=pltpu.CompilerParams(vmem_limit_bytes=16 << 20),
        input_output_aliases={4: 0},
        name="join",
    )(sub, own, other, state_readout, *filled)

    squares, more = summed(squares, "head")
    return pl.pallas_call(
        functools.partial(norm_kernel, channels * lax.axis_size("head")),
        grid=(count,),
        in_specs=[
            pl.BlockSpec((1, BLOCK), lambda k: (0, k)),
            pl.BlockSpec((1, BLOCK), lambda k: (0, k)),
            whole((1, channels)),
            VMEM,
        ],
        out_specs=pl.BlockSpec((BLOCK, channels), lambda k: (k, 0)),
        out_shape=jax.ShapeDtypeStruct((length, channels), BF16),
        compiler_params=pltpu.CompilerParams(vmem_limit_bytes=16 << 20),
        name="norm",
    )(squares, more, norm_gain.reshape(1, channels), gated)


def summed(value, axis):
    size = lax.axis_size(axis)
    if size & (size - 1):
        total = value
        for shift in range(1, size):
            total = total + lax.ppermute(value, axis, [(i, (i + shift) % size) for i in range(size)])
        return total, jnp.zeros_like(value)
    more, shift = jnp.zeros_like(value), 1
    while shift < size:
        value = value + more if shift > 1 else value
        more = lax.ppermute(value, axis, [(i, i ^ shift) for i in range(size)])
        shift *= 2
    return value, more


def carry_in(own, sent, half):
    tiles = own.shape[0]
    second = lax.axis_index("sub") == 1
    place, chips = lax.axis_index("seq"), lax.axis_size("seq")
    got = lax.ppermute(sent, "sub", [(0, 1), (1, 0)])
    early = jnp.where(second, got, own)
    late = jnp.where(second, own, got)
    first, last = early[0, half + 1], late[0, half + 2]
    link = jnp.where(early[0, half + 2] == late[0, half + 1], 1.0, 0.0)
    early_decay, late_decay = early[:, half : half + 1], late[:, half : half + 1] * link
    early, late = early[:, :half], late[:, :half]
    chip_state = late_decay * early + late
    chip_decay = late_decay * early_decay

    chunks, hops = plan(chips, tiles)[:2]
    size = tiles // chunks
    rows = size * half
    tail = jnp.broadcast_to(last, (8, LANES))

    def at(array, index):
        return lax.dynamic_slice_in_dim(array, index * size, size, 0)

    carry = jnp.zeros((size, half, LANES), F32)
    received = []
    for t in range(hops):
        index = jnp.clip(t - place, 0, chunks - 1)
        send = at(chip_decay, index) * carry + at(chip_state, index)
        send = jnp.concatenate([send.reshape(rows, LANES), tail], axis=0)
        pairs = [(z, z + 1) for z in range(chips - 1) if 0 <= t - z < chunks]
        got = lax.ppermute(send, "seq", pairs)
        joined = jnp.where(got[rows : rows + 1] == first, 1.0, 0.0)
        carry = joined[None] * got[:rows].reshape(size, half, LANES)
        received.append(carry)
    parts = []
    for c in range(chunks):
        part = jnp.zeros((size, half, LANES), F32)
        for z in range(1, chips):
            part = jnp.where(place == z, received[c + z - 1], part)
        parts.append(part)
    entering = jnp.concatenate(parts, axis=0)
    onward = link * (early_decay * entering + early)
    mine = jnp.where(second, onward, entering)
    other = lax.ppermute(jnp.where(second, entering, onward), "sub", [(0, 1), (1, 0)])
    return mine, other


def solution(mesh):
    placed = (
        P(("groups", "seq", "sub"), "head"),
        P(("groups", "seq", "sub"), "head"),
        P(("groups", "seq", "sub"), None),
        P(("groups", "seq", "sub"), None),
        P("head", ("seq", "sub")),
        P("head"),
        P("head"),
        P("head"),
        P("head"),
        P(("groups", "seq", "sub")),
        P(("groups", "seq", "sub")),
    )

    return jax.shard_map(
        on_device,
        mesh=mesh,
        in_specs=placed,
        out_specs=P(("groups", "seq", "sub"), "head"),
        check_vma=False,
    )
```

time: 129 us -> 110 us (0.85)
  the two profiles are of different devices: /device:TPU:19 before, /device:TPU:17 now
where the time goes in v1:
time: 110 us; the launch traced here: 109 us
  Pallas kernels  38.3 us (35%)
  waiting for transfers between devices  32.8 us (30%)
  local copies, waits for them, and re-layouts  21.7 us (20%)
  starting transfers between devices  12.3 us (11%)
  other arithmetic  3.23 us (3%)
    ppermute x4, waiting for transfers between devices, carry_in(): got = lax.ppermute(send, 'seq', pairs)  29.7 us
    pallas_call x5, Pallas kernels, on_device(): pl.pallas_call(functools.partial(inner_kernel, width, q * wide // LANES,...  21.9 us
    unnamed x45, local copies, waits for them, and re-layouts  20.6 us
    pallas_call x1, Pallas kernels, on_device(): pl.pallas_call(functools.partial(state_kernel, heads), grid=(channels //...  8.17 us
    ppermute x4, starting transfers between devices, carry_in(): got = lax.ppermute(send, 'seq', pairs)  7.09 us
    pallas_call x1, Pallas kernels, on_device(): pl.pallas_call(join_kernel, grid=(channels // chunk,), in_specs=[SMEM, pl...  3.53 us
    ppermute x1, starting transfers between devices, carry_in(): lax.ppermute(jnp.where(second, entering, onward), 'sub', [(0, 1), (1, 0)])  3.3 us
    pallas_call x1, Pallas kernels, on_device(): pl.pallas_call(functools.partial(norm_kernel, channels * lax.axis_size('h...  3.27 us
  transfers between devices with their start and end apart: 7, of which 5 were waited for; matrix products, arithmetic and copies ran while one was open for 0% of the time, Pallas kernels for 21%

profile of v1, /device:TPU:17, one launch (start us, length us, event | category | flops | bytes accessed | tf_op | source)
XLA Modules:
  0.0 109.4 jit_solution(6632284205234365892)
XLA Ops:
  0.7 0.0 copy-start
  0.7 2.5 %copy-done = bf16[1024,2560]{1,0:T(8,128)(2,1)S(1)} copy-done((bf16[1024,2560]{1,0:T(8,128)(2,1)S(1)}, bf16[1024,2560]{1,0:T(8,128)(2,1)}, u32[]{:S(2)}) %copy-start) | copy-done | bytes 5242904
  3.1 1.1 copy-done.5
  4.2 0.9 copy-done.8
  5.2 1.1 copy-done.10
  6.3 0.7 copy-done.11
  7.0 0.9 copy-done.13
  7.9 0.9 copy-done.14
  8.8 0.7 copy-done.15
  9.4 0.7 copy-done.16
  10.1 0.7 copy-done.17
  10.7 8.2 %shard_state.1 = (f32[40,1024]{1,0:T(8,128)S(1)}, f32[1024,128]{1,0:T(8,128)S(1)}, f32[4,128,2560]{2,1,0:T(8,128)S(1)}, f32[20,72,128]{2,1,0:T(8,128)S(1)}, f32[...) custom-call(s32[1]{0:T(128)S(6)} %copy.49.live_ref, s32[1024]{0:T(1024)S(1)} %copy-done.11, s32[1]{0:T(128)} %bitcast.sub_ref, ...), custom_call_target="tpu_custom_call" | custom-call | tf_op jit(solution)/shard_map/shard_state/pallas_call | solution.py:358
  18.9 2.3 %copy-done.3 = f32[4,128,2560]{2,1,0:T(8,128)} copy-done((f32[4,128,2560]{2,1,0:T(8,128)}, f32[4,128,2560]{2,1,0:T(8,128)S(1)}, u32[]{:S(2)}) %copy-start.3) | copy-done | bytes 5242904
  21.3 0.7 collective-permute-start
  22.0 1.8 %collective-permute-done = f32[20,72,128]{2,1,0:T(8,128)S(1)} collective-permute-done((f32[20,72,128]{2,1,0:T(8,128)S(1)}, f32[20,72,128]{2,1,0:T(8,128)S(1)}, u32[]{:S(2)}, u32[]{:S(2)}) %collective-permute-start) | collective-permute-done | bytes 737312 | tf_op jit(solution)/shard_map/ppermute | solution.py:549
  23.8 0.1 broadcast_select_fusion
  24.0 0.1 slice_add_fusion
  24.2 0.7 collective-permute-start.1
  24.9 0.1 dynamic-slice_add_fusion.2
  25.1 1.4 %collective-permute-start.2 = (f32[648,128]{1,0:T(8,128)S(1)}, f32[648,128]{1,0:T(8,128)S(1)}, u32[]{:S(2)}, u32[]{:S(2)}) collective-permute-start(f32[648,128]{1,0:T(8,128)S(1)} %pad_maximum_fusion.2), channel_id=1, source_target_pairs={{0,4},{4,8},{1,5},{5,9},{2,6},{6,10},{3,7},{7,11},{16,20},{20,24},... | collective-permute-start | bytes 995336 | tf_op jit(solution)/shard_map/ppermute | solution.py:574
  26.5 17.9 %collective-permute-done.2 = f32[648,128]{1,0:T(8,128)S(1)} collective-permute-done((f32[648,128]{1,0:T(8,128)S(1)}, f32[648,128]{1,0:T(8,128)S(1)}, u32[]{:S(2)}, u32[]{:S(2)}) %collective-permute-start.2) | collective-permute-done | bytes 331808 | tf_op jit(solution)/shard_map/ppermute | solution.py:574
  44.4 0.0 copy-start.6
  44.4 0.1 dynamic-slice_add_fusion.1
  44.5 2.1 %collective-permute-start.3 = (f32[648,128]{1,0:T(8,128)S(1)}, f32[648,128]{1,0:T(8,128)S(1)}, u32[]{:S(2)}, u32[]{:S(2)}) collective-permute-start(f32[648,128]{1,0:T(8,128)S(1)} %pad_maximum_fusion.1), channel_id=1, source_target_pairs={{4,8},{8,12},{5,9},{9,13},{6,10},{10,14},{7,11},{11,15},{20,24},{2... | collective-permute-start | bytes 995336 | tf_op jit(solution)/shard_map/ppermute | solution.py:574
  46.6 7.5 %collective-permute-done.3 = f32[648,128]{1,0:T(8,128)S(1)} collective-permute-done((f32[648,128]{1,0:T(8,128)S(1)}, f32[648,128]{1,0:T(8,128)S(1)}, u32[]{:S(2)}, u32[]{:S(2)}) %collective-permute-start.3) | collective-permute-done | bytes 331808 | tf_op jit(solution)/shard_map/ppermute | solution.py:574
  54.1 0.1 dynamic-slice_add_fusion
  54.2 0.7 copy-done.18
  54.8 0.7 pad_maximum_fusion
  55.6 2.9 %collective-permute-start.4 = (f32[648,128]{1,0:T(8,128)}, f32[648,128]{1,0:T(8,128)}, u32[]{:S(2)}, u32[]{:S(2)}) collective-permute-start(f32[648,128]{1,0:T(8,128)} %pad_maximum_fusion), channel_id=1, source_target_pairs={{8,12},{9,13},{10,14},{11,15},{24,28},{25,29},{26,30},{27,31}} | collective-permute-start | bytes 995336 | tf_op jit(solution)/shard_map/ppermute | solution.py:574
  58.5 4.3 %collective-permute-done.4 = f32[648,128]{1,0:T(8,128)} collective-permute-done((f32[648,128]{1,0:T(8,128)}, f32[648,128]{1,0:T(8,128)}, u32[]{:S(2)}, u32[]{:S(2)}) %collective-permute-start.4) | collective-permute-done | bytes 331808 | tf_op jit(solution)/shard_map/ppermute | solution.py:574
  62.9 1.0 slice.79
  63.9 0.7 fusion.6
  64.5 1.1 %select_select_fusion.1 = (f32[10,64,128]{2,1,0:T(8,128)S(1)}, f32[10,64,128]{2,1,0:T(8,128)S(1)}) fusion(f32[10,64,128]{2,1,0:T(8,128)S(1)} %bitcast.57, f32[10,64,128]{2,1,0:T(8,128)} %bitcast.61, f32[10,64,128]{2,1,0:T(8,128)S(1)} %bitcast.59, f32[128]{0:T(128)S(1)} %fusion.5, f32[128]{0:T(128)S(1)} %fusion.4, f32[128]{0:T(128)S(1)} %fusion.3, ...), kind=kLoop, calls=%fused_computation.13 | loop fusion | flops 819200 | bytes 1968131 | tf_op jit(solution)/shard_map/jit(_where)/select_n | solution.py:582
  65.7 0.2 fusion
  65.8 3.3 %collective-permute-start.5 = (f32[20,64,128]{2,1,0:T(8,128)S(1)}, f32[20,64,128]{2,1,0:T(8,128)S(1)}, u32[]{:S(2)}, u32[]{:S(2)}) collective-permute-start(f32[20,64,128]{2,1,0:T(8,128)S(1)} %get-tuple-element.49), channel_id=1, source_target_pairs={{0,1},{1,0},{2,3},{3,2},{4,5},{5,4},{6,7},{7,6},{8,9},{9,8},{10,11... | collective-permute-start | bytes 1966088 | tf_op jit(solution)/shard_map/ppermute | solution.py:587
  69.2 1.4 %prepare.1 = (f32[4,256,256]{2,1,0:T(8,128)S(1)}, bf16[1024,256]{1,0:T(8,128)(2,1)S(1)}) custom-call(s32[1024]{0:T(1024)S(1)} %copy-done.12, bf16[1024,128]{1,0:T(8,128)(2,1)S(1)} %copy-done.9, bf16[1024,128]{1,0:T(8,128)(2,1)S(1)} %copy-done.7, f32[1024,128]{1,0:T(8,128)S(1)} %get-tuple-element.28.col_ref, s32[1,1024]{1,0:T(1,128)S(1)} %bitcast.52), custom_call_target="tpu_custom_call" | custom-call | tf_op jit(solution)/shard_map/prepare/pallas_call | solution.py:417
  70.6 2.5 %copy-done.1 = bf16[1024,2560]{1,0:T(8,128)(2,1)S(1)} copy-done((bf16[1024,2560]{1,0:T(8,128)(2,1)S(1)}, bf16[1024,2560]{1,0:T(8,128)(2,1)}, u32[]{:S(2)}) %copy-start.1) | copy-done | bytes 5242904
  73.1 2.5 %copy-done.2 = bf16[1024,2560]{1,0:T(8,128)(2,1)S(1)} copy-done((bf16[1024,2560]{1,0:T(8,128)(2,1)S(1)}, bf16[1024,2560]{1,0:T(8,128)(2,1)}, u32[]{:S(2)}) %copy-start.2) | copy-done | bytes 5242904
  75.6 2.5 %copy-done.4 = f32[4,128,2560]{2,1,0:T(8,128)S(1)} copy-done((f32[4,128,2560]{2,1,0:T(8,128)S(1)}, f32[4,128,2560]{2,1,0:T(8,128)}, u32[]{:S(2)}) %copy-start.4) | copy-done | bytes 5242904
  78.1 4.4 %shard_map.136 = (f32[1024,2560]{1,0:T(8,128)S(1)}, bf16[1024,2560]{1,0:T(8,128)(2,1)S(1)}) custom-call(s32[1]{0:T(128)S(6)} %copy.49.live_ref, s32[1024]{0:T(1024)S(1)} %copy-done.12, bf16[1024,2560]{1,0:T(8,128)(2,1)S(1)} %copy-done.1, bf16[1024,2560]{1,0:T(8,128)(2,1)S(1)} %copy-done.2, bf16[1024,128]{1,0:T(8,128)(2,1)S(1)} %copy-done.7, ...), custom_call_target="tpu_custom_call" | custom-call | flops 629145600 | bytes 5242880 | tf_op jit(solution)/shard_map/pallas_call | solution.py:443
  82.4 4.4 %shard_map.137 = (f32[1024,2560]{1,0:T(8,128)S(1)}, bf16[1024,2560]{1,0:T(8,128)(2,1)S(1)}) custom-call(s32[1]{0:T(128)S(6)} %copy.49.live_ref, s32[1024]{0:T(1024)S(1)} %copy-done.12, bf16[1024,2560]{1,0:T(8,128)(2,1)S(1)} %copy-done.1, bf16[1024,2560]{1,0:T(8,128)(2,1)S(1)} %copy-done.2, ...), custom_call_target="tpu_custom_call", output_to_operand_aliasing={{0}: (12, {}), {1}: (13, {})} | custom-call | flops 629145600 | bytes 5242880 | tf_op jit(solution)/shard_map/pallas_call | solution.py:443
  86.8 4.4 %shard_map.138 = (f32[1024,2560]{1,0:T(8,128)S(1)}, bf16[1024,2560]{1,0:T(8,128)(2,1)S(1)}) custom-call(s32[1]{0:T(128)S(6)} %copy.49.live_ref, s32[1024]{0:T(1024)S(1)} %copy-done.12, bf16[1024,2560]{1,0:T(8,128)(2,1)S(1)} %copy-done.1, bf16[1024,2560]{1,0:T(8,128)(2,1)S(1)} %copy-done.2, ...), custom_call_target="tpu_custom_call", output_to_operand_aliasing={{0}: (12, {}), {1}: (13, {})} | custom-call | flops 629145600 | bytes 5242880 | tf_op jit(solution)/shard_map/pallas_call | solution.py:443
  91.3 4.4 %shard_map.139 = (f32[1024,2560]{1,0:T(8,128)S(1)}, bf16[1024,2560]{1,0:T(8,128)(2,1)S(1)}) custom-call(s32[1]{0:T(128)S(6)} %copy.49.live_ref, s32[1024]{0:T(1024)S(1)} %copy-done.12, bf16[1024,2560]{1,0:T(8,128)(2,1)S(1)} %copy-done.1, bf16[1024,2560]{1,0:T(8,128)(2,1)S(1)} %copy-done.2, ...), custom_call_target="tpu_custom_call", output_to_operand_aliasing={{0}: (12, {}), {1}: (13, {})} | custom-call | flops 629145600 | bytes 5242880 | tf_op jit(solution)/shard_map/pallas_call | solution.py:443
  95.7 4.4 %shard_map.140 = (f32[1024,2560]{1,0:T(8,128)S(1)}, bf16[1024,2560]{1,0:T(8,128)(2,1)S(1)}) custom-call(s32[1]{0:T(128)S(6)} %copy.49.live_ref, s32[1024]{0:T(1024)S(1)} %copy-done.12, bf16[1024,2560]{1,0:T(8,128)(2,1)S(1)} %copy-done.1, bf16[1024,2560]{1,0:T(8,128)(2,1)S(1)} %copy-done.2, ...), custom_call_target="tpu_custom_call", output_to_operand_aliasing={{0}: (12, {}), {1}: (13, {})} | custom-call | flops 629145600 | bytes 5242880 | tf_op jit(solution)/shard_map/pallas_call | solution.py:443
  100.1 3.5 %join.1 = (f32[1024,2560]{1,0:T(8,128)S(1)}, f32[1,1024]{1,0:T(1,128)S(1)}) custom-call(s32[1]{0:T(128)} %bitcast.sub_ref, f32[20,64,128]{2,1,0:T(8,128)S(1)} %get-tuple-element.50.own_ref, f32[20,64,128]{2,1,0:T(8,128)S(1)} %collective-permute-done.5.other_ref, bf16[1024,128]{1,0:T(8,128)(2,1)S(1)} %copy-done.7, ...), custom_call_target="tpu_custom_call", output_to_operand_aliasing={{0}: (4, {})} | custom-call | tf_op jit(solution)/shard_map/join/pallas_call | solution.py:491
  103.6 1.2 %collective-permute-start.6 = (f32[1,1024]{1,0:T(1,128)S(1)}, f32[1,1024]{1,0:T(1,128)S(1)}, u32[]{:S(2)}, u32[]{:S(2)}) collective-permute-start(f32[1,1024]{1,0:T(1,128)S(1)} %get-tuple-element.43.square_ref), channel_id=1, source_target_pairs={{0,2},{2,0},{1,3},{3,1},{4,6},{6,4},{5,7},{7,5},{8,10},{10,8},{9,1... | collective-permute-start | bytes 12296 | tf_op jit(solution)/shard_map/ppermute | solution.py:540
  104.9 1.3 %collective-permute-done.6.more_ref = f32[1,1024]{1,0:T(1,128)S(1)} collective-permute-done((f32[1,1024]{1,0:T(1,128)S(1)}, f32[1,1024]{1,0:T(1,128)S(1)}, u32[]{:S(2)}, u32[]{:S(2)}) %collective-permute-start.6) | collective-permute-done | bytes 4128 | tf_op jit(solution)/shard_map/ppermute | solution.py:540
  106.1 3.3 %norm.1 = bf16[1024,2560]{1,0:T(8,128)(2,1)} custom-call(f32[1,1024]{1,0:T(1,128)S(1)} %get-tuple-element.43.square_ref, f32[1,1024]{1,0:T(1,128)S(1)} %collective-permute-done.6.more_ref, f32[1,2560]{1,0:T(1,128)S(1)} %reshape.66.gain_ref, f32[1024,2560]{1,0:T(8,128)S(1)} %get-tuple-element.44.gated_ref), custom_call_target="tpu_custom_call" | custom-call | tf_op jit(solution)/shard_map/norm/pallas_call | solution.py:514
  (45 shorter events, 0.3 us)
Async XLA Ops:
  0.7 2.5 %copy-start = (bf16[1024,2560]{1,0:T(8,128)(2,1)S(1)}, bf16[1024,2560]{1,0:T(8,128)(2,1)}, u32[]{:S(2)}) copy-start(bf16[1024,2560]{1,0:T(8,128)(2,1)} %x_ref.11) | copy-start | bytes 15728644
  3.1 1.1 copy-start.5
  4.2 0.9 copy-start.8
  5.2 1.1 copy-start.10
  6.3 0.7 copy-start.11
  7.0 0.9 copy-start.13
  7.9 0.9 copy-start.14
  8.8 0.7 copy-start.15
  9.4 0.7 copy-start.16
  10.1 0.7 copy-start.17
  18.9 2.4 %copy-start.3 = (f32[4,128,2560]{2,1,0:T(8,128)}, f32[4,128,2560]{2,1,0:T(8,128)S(1)}, u32[]{:S(2)}) copy-start(f32[4,128,2560]{2,1,0:T(8,128)S(1)} %get-tuple-element.31.enter_ref) | copy-start | bytes 15728644
  21.3 2.5 %collective-permute-start = (f32[20,72,128]{2,1,0:T(8,128)S(1)}, f32[20,72,128]{2,1,0:T(8,128)S(1)}, u32[]{:S(2)}, u32[]{:S(2)}) collective-permute-start(f32[20,72,128]{2,1,0:T(8,128)S(1)} %get-tuple-element.25), channel_id=1, source_target_pairs={{0,1},{1,0},{2,3},{3,2},{4,5},{5,4},{6,7},{7,6},{8,9},{9,8},{10,11... | collective-permute-start | bytes 2211848 | tf_op jit(solution)/shard_map/ppermute | solution.py:549
  24.2 0.7 collective-permute-start.1
  25.0 44.1 %copy-start.7 = (bf16[1024,128]{1,0:T(8,128)(2,1)S(1)}, bf16[1024,128]{1,0:T(8,128)(2,1)}, u32[]{:S(2)}) copy-start(bf16[1024,128]{1,0:T(8,128)(2,1)} %c_ref.13) | copy-start | bytes 786436
  25.0 44.1 %copy-start.9 = (bf16[1024,128]{1,0:T(8,128)(2,1)S(1)}, bf16[1024,128]{1,0:T(8,128)(2,1)}, u32[]{:S(2)}) copy-start(bf16[1024,128]{1,0:T(8,128)(2,1)} %b_ref.3) | copy-start | bytes 786436
  25.0 44.1 %copy-start.12 = (s32[1024]{0:T(1024)S(1)}, s32[1024]{0:T(1024)}, u32[]{:S(2)}) copy-start(s32[1024]{0:T(1024)} %docs_ref.13) | copy-start | bytes 12292
  25.1 19.3 %collective-permute-start.2 = (f32[648,128]{1,0:T(8,128)S(1)}, f32[648,128]{1,0:T(8,128)S(1)}, u32[]{:S(2)}, u32[]{:S(2)}) collective-permute-start(f32[648,128]{1,0:T(8,128)S(1)} %pad_maximum_fusion.2), channel_id=1, source_target_pairs={{0,4},{4,8},{1,5},{5,9},{2,6},{6,10},{3,7},{7,11},{16,20},{20,24},... | collective-permute-start | bytes 995336 | tf_op jit(solution)/shard_map/ppermute | solution.py:574
  44.4 26.2 %copy-start.6 = (bf16[128,2560]{1,0:T(8,128)(2,1)S(1)}, bf16[128,2560]{1,0:T(8,128)(2,1)}, u32[]{:S(2)}) copy-start(bf16[128,2560]{1,0:T(8,128)(2,1)} %constant.32.clone.hot_ref) | copy-start | bytes 1966084
  44.5 9.6 %collective-permute-start.3 = (f32[648,128]{1,0:T(8,128)S(1)}, f32[648,128]{1,0:T(8,128)S(1)}, u32[]{:S(2)}, u32[]{:S(2)}) collective-permute-start(f32[648,128]{1,0:T(8,128)S(1)} %pad_maximum_fusion.1), channel_id=1, source_target_pairs={{4,8},{8,12},{5,9},{9,13},{6,10},{10,14},{7,11},{11,15},{20,24},{2... | collective-permute-start | bytes 995336 | tf_op jit(solution)/shard_map/ppermute | solution.py:574
  54.1 0.7 copy-start.18
  55.6 7.3 %collective-permute-start.4 = (f32[648,128]{1,0:T(8,128)}, f32[648,128]{1,0:T(8,128)}, u32[]{:S(2)}, u32[]{:S(2)}) collective-permute-start(f32[648,128]{1,0:T(8,128)} %pad_maximum_fusion), channel_id=1, source_target_pairs={{8,12},{9,13},{10,14},{11,15},{24,28},{25,29},{26,30},{27,31}} | collective-permute-start | bytes 995336 | tf_op jit(solution)/shard_map/ppermute | solution.py:574
  65.8 34.2 %collective-permute-start.5 = (f32[20,64,128]{2,1,0:T(8,128)S(1)}, f32[20,64,128]{2,1,0:T(8,128)S(1)}, u32[]{:S(2)}, u32[]{:S(2)}) collective-permute-start(f32[20,64,128]{2,1,0:T(8,128)S(1)} %get-tuple-element.49), channel_id=1, source_target_pairs={{0,1},{1,0},{2,3},{3,2},{4,5},{5,4},{6,7},{7,6},{8,9},{9,8},{10,11... | collective-permute-start | bytes 1966088 | tf_op jit(solution)/shard_map/ppermute | solution.py:587
  70.6 2.5 %copy-start.1 = (bf16[1024,2560]{1,0:T(8,128)(2,1)S(1)}, bf16[1024,2560]{1,0:T(8,128)(2,1)}, u32[]{:S(2)}) copy-start(bf16[1024,2560]{1,0:T(8,128)(2,1)} %x_ref.11) | copy-start | bytes 15728644
  73.1 2.5 %copy-start.2 = (bf16[1024,2560]{1,0:T(8,128)(2,1)S(1)}, bf16[1024,2560]{1,0:T(8,128)(2,1)}, u32[]{:S(2)}) copy-start(bf16[1024,2560]{1,0:T(8,128)(2,1)} %z_ref.9) | copy-start | bytes 15728644
  75.6 2.5 %copy-start.4 = (f32[4,128,2560]{2,1,0:T(8,128)S(1)}, f32[4,128,2560]{2,1,0:T(8,128)}, u32[]{:S(2)}) copy-start(f32[4,128,2560]{2,1,0:T(8,128)} %copy-done.3) | copy-start | bytes 15728644
  100.1 4.8 %copy-start.19 = (f32[2560]{0:T(1024)S(1)}, f32[2560]{0:T(1024)}, u32[]{:S(2)}) copy-start(f32[2560]{0:T(1024)} %param.22) | copy-start | bytes 30724
  103.6 2.5 %collective-permute-start.6 = (f32[1,1024]{1,0:T(1,128)S(1)}, f32[1,1024]{1,0:T(1,128)S(1)}, u32[]{:S(2)}, u32[]{:S(2)}) collective-permute-start(f32[1,1024]{1,0:T(1,128)S(1)} %get-tuple-element.43.square_ref), channel_id=1, source_target_pairs={{0,2},{2,0},{1,3},{3,1},{4,6},{6,4},{5,7},{7,5},{8,10},{10,8},{9,1... | collective-permute-start | bytes 12296 | tf_op jit(solution)/shard_map/ppermute | solution.py:540

commit v2 on v1

--- a/solution.py
+++ b/solution.py
@@ -271,7 +271,7 @@
         rows = slice(r, r + BLOCK)
         readout = c_ref[rows, :]
         outer = dot(jnp.concatenate([readout, readout], axis=1), carry)
-        gated = y_ref[rows, here] + f_ref[rows, here].astype(F32) * outer
+        gated = y_ref[rows, :] + f_ref[rows, :].astype(F32) * outer
         gated_ref[rows, here] = gated
         square = total[rows, :]
         for j in range(wide // LANES):
@@ -396,7 +396,6 @@
             pltpu.VMEM((states, chunk), F32),
             pltpu.VMEM((scalars, LANES), F32),
         ],
-        compiler_params=pltpu.CompilerParams(vmem_limit_bytes=24 << 20),
         name="shard_state",
     )(
         live_blocks,
@@ -432,7 +431,6 @@
             jax.ShapeDtypeStruct((count, BLOCK, BLOCK), F32),
             jax.ShapeDtypeStruct((length, 2 * LANES), BF16),
         ],
-        compiler_params=pltpu.CompilerParams(vmem_limit_bytes=16 << 20),
         name="prepare",
     )(document_ids, state_input, state_readout, col, doc_row)
 
@@ -469,7 +467,6 @@
                 bytes_accessed=length * wide * 10,
                 transcendentals=0,
             ),
-            compiler_params=pltpu.CompilerParams(vmem_limit_bytes=16 << 20),
         )(
             live_blocks,
             document_ids,
@@ -496,8 +493,8 @@
             pl.BlockSpec((per_chunk, half, LANES), lambda k: (k, 0, 0)),
             pl.BlockSpec((per_chunk, half, LANES), lambda k: (k, 0, 0)),
             whole((length, states)),
-            VMEM,
-            VMEM,
+            pl.BlockSpec((length, chunk), lambda k: (0, k)),
+            pl.BlockSpec((length, chunk), lambda k: (0, k)),
         ],
         out_specs=[VMEM, whole((1, length))],
         out_shape=[
@@ -505,8 +502,7 @@
             jax.ShapeDtypeStruct((1, length), F32),
         ],
         scratch_shapes=[pltpu.VMEM((length, LANES), F32)],
-        compiler_params=pltpu.CompilerParams(vmem_limit_bytes=16 << 20),
-        input_output_aliases={4: 0},
+        compiler_params=pltpu.CompilerParams(vmem_limit_bytes=24 << 20),
         name="join",
     )(sub, own, other, state_readout, *filled)
 

time: 110 us -> 110 us (level)
  Pallas kernels: 38.3 us -> 55 us
  local copies, waits for them, and re-layouts: 21.7 us -> 6.58 us
  other arithmetic: 3.23 us -> 1.95 us
    unnamed x45 -> x13, local copies, waits for them, and re-layouts: 20.6 us -> 6.48 us
    pallas_call x5, Pallas kernels: 21.9 us -> 33.5 us  [on_device(): pl.pallas_call(functools.partial(inner_kernel, width, q * wide // LANES,...]
    pallas_call x1, Pallas kernels: 1.45 us -> 3.79 us  [on_device(): pl.pallas_call(functools.partial(prepare_kernel, heads), grid=(count,), i...]
    pallas_call x1, Pallas kernels: 8.17 us -> 10.4 us  [on_device(): pl.pallas_call(functools.partial(state_kernel, heads), grid=(channels //...]
    select_n x1, other arithmetic: 0.1 us -> 1.21 us  [carry_in(): late = jnp.where(second, own, got)]
  transfers between devices with their start and end apart: 7 -> 7, of which waited for: 5 -> 5; matrix products, arithmetic and copies ran while one was open for 0% -> 0% of each run, Pallas kernels for 21% -> 34%
where the time goes in v2:
time: 110 us; the launch traced here: 109 us
  Pallas kernels  55 us (50%)
  waiting for transfers between devices  33.4 us (30%)
  starting transfers between devices  11.4 us (10%)
  local copies, waits for them, and re-layouts  6.58 us (6%)
  other arithmetic  1.95 us (2%)
    pallas_call x5, Pallas kernels, on_device(): pl.pallas_call(functools.partial(inner_kernel, width, q * wide // LANES,...  33.5 us
    ppermute x4, waiting for transfers between devices, carry_in(): got = lax.ppermute(send, 'seq', pairs)  30.1 us
    pallas_call x1, Pallas kernels, on_device(): pl.pallas_call(functools.partial(state_kernel, heads), grid=(channels //...  10.4 us
    unnamed x13, local copies, waits for them, and re-layouts  6.48 us
    ppermute x4, starting transfers between devices, carry_in(): got = lax.ppermute(send, 'seq', pairs)  6.11 us
    pallas_call x1, Pallas kernels, on_device(): pl.pallas_call(join_kernel, grid=(channels // chunk,), in_specs=[SMEM, pl...  3.96 us
    pallas_call x1, Pallas kernels, on_device(): pl.pallas_call(functools.partial(prepare_kernel, heads), grid=(count,), i...  3.79 us
    ppermute x1, starting transfers between devices, carry_in(): lax.ppermute(jnp.where(second, entering, onward), 'sub', [(0, 1), (1, 0)])  3.3 us
  transfers between devices with their start and end apart: 7, of which 5 were waited for; matrix products, arithmetic and copies ran while one was open for 0% of the time, Pallas kernels for 34%

profile of v2, /device:TPU:17, one launch (start us, length us, event | category | flops | bytes accessed | tf_op | source)
XLA Modules:
  0.0 109.3 jit_solution(3459152883495067110)
XLA Ops:
  0.7 10.4 %shard_state.1 = (f32[40,1024]{1,0:T(8,128)}, f32[1024,128]{1,0:T(8,128)}, f32[4,128,2560]{2,1,0:T(8,128)}, f32[20,72,128]{2,1,0:T(8,128)}, f32[20,72,128]{2,1,0:T(8,128)}, /*index=5*/f32[16,2560]{1,0:T(8,128)}) custom-call(s32[1]{0:T(128)S(6)} %copy.47.live_ref, s32[1024]{0:T(1024)} %docs_ref.13, s32[1]{0:T(128)} %bitcast.sub_ref, f32[40,1024]{1,0:T(8,128)} %raw_ref.1, ...), custom_call_target="tpu_custom_call" | custom-call | tf_op jit(solution)/shard_map/shard_state/pallas_call | solution.py:358
  11.1 0.7 collective-permute-start
  11.8 2.1 %collective-permute-done = f32[20,72,128]{2,1,0:T(8,128)S(1)} collective-permute-done((f32[20,72,128]{2,1,0:T(8,128)}, f32[20,72,128]{2,1,0:T(8,128)S(1)}, u32[]{:S(2)}, u32[]{:S(2)}) %collective-permute-start) | collective-permute-done | bytes 737312 | tf_op jit(solution)/shard_map/ppermute | solution.py:545
  13.9 1.2 %broadcast_select_fusion = (f32[20,72,128]{2,1,0:T(8,128)S(1)}, f32[20,72,128]{2,1,0:T(8,128)S(1)}) fusion(f32[20,72,128]{2,1,0:T(8,128)} %get-tuple-element.26, f32[20,72,128]{2,1,0:T(8,128)S(1)} %collective-permute-done, pred[]{:T(512)S(6)} %eq.32), kind=kLoop, calls=%fused_computation.9 | loop fusion | flops 368640 | bytes 2949121 | tf_op jit(solution)/shard_map/jit(_where)/select_n | solution.py:547
  15.1 0.1 slice_add_fusion
  15.4 0.7 collective-permute-start.1
  16.1 0.0 collective-permute-done.1
  16.2 1.3 %collective-permute-start.2 = (f32[648,128]{1,0:T(8,128)S(1)}, f32[648,128]{1,0:T(8,128)S(1)}, u32[]{:S(2)}, u32[]{:S(2)}) collective-permute-start(f32[648,128]{1,0:T(8,128)S(1)} %pad_maximum_fusion.2), channel_id=1, source_target_pairs={{0,4},{4,8},{1,5},{5,9},{2,6},{6,10},{3,7},{7,11},{16,20},{20,24},... | collective-permute-start | bytes 995336 | tf_op jit(solution)/shard_map/ppermute | solution.py:570
  17.5 17.9 %collective-permute-done.2 = f32[648,128]{1,0:T(8,128)S(1)} collective-permute-done((f32[648,128]{1,0:T(8,128)S(1)}, f32[648,128]{1,0:T(8,128)S(1)}, u32[]{:S(2)}, u32[]{:S(2)}) %collective-permute-start.2) | collective-permute-done | bytes 331808 | tf_op jit(solution)/shard_map/ppermute | solution.py:570
  35.5 1.9 %collective-permute-start.3 = (f32[648,128]{1,0:T(8,128)S(1)}, f32[648,128]{1,0:T(8,128)S(1)}, u32[]{:S(2)}, u32[]{:S(2)}) collective-permute-start(f32[648,128]{1,0:T(8,128)S(1)} %pad_maximum_fusion.1), channel_id=1, source_target_pairs={{4,8},{8,12},{5,9},{9,13},{6,10},{10,14},{7,11},{11,15},{20,24},{2... | collective-permute-start | bytes 995336 | tf_op jit(solution)/shard_map/ppermute | solution.py:570
  37.5 7.5 %collective-permute-done.3 = f32[648,128]{1,0:T(8,128)S(1)} collective-permute-done((f32[648,128]{1,0:T(8,128)S(1)}, f32[648,128]{1,0:T(8,128)S(1)}, u32[]{:S(2)}, u32[]{:S(2)}) %collective-permute-start.3) | collective-permute-done | bytes 331808 | tf_op jit(solution)/shard_map/ppermute | solution.py:570
  45.1 2.2 %collective-permute-start.4 = (f32[648,128]{1,0:T(8,128)S(1)}, f32[648,128]{1,0:T(8,128)S(1)}, u32[]{:S(2)}, u32[]{:S(2)}) collective-permute-start(f32[648,128]{1,0:T(8,128)S(1)} %pad_maximum_fusion), channel_id=1, source_target_pairs={{8,12},{9,13},{10,14},{11,15},{24,28},{25,29},{26,30},{27,31}} | collective-permute-start | bytes 995336 | tf_op jit(solution)/shard_map/ppermute | solution.py:570
  47.3 4.7 %collective-permute-done.4 = f32[648,128]{1,0:T(8,128)S(1)} collective-permute-done((f32[648,128]{1,0:T(8,128)S(1)}, f32[648,128]{1,0:T(8,128)S(1)}, u32[]{:S(2)}, u32[]{:S(2)}) %collective-permute-start.4) | collective-permute-done | bytes 331808 | tf_op jit(solution)/shard_map/ppermute | solution.py:570
  52.1 0.1 select_select_fusion.1
  52.2 0.2 fusion
  52.4 3.3 %collective-permute-start.5 = (f32[20,64,128]{2,1,0:T(8,128)S(1)}, f32[20,64,128]{2,1,0:T(8,128)S(1)}, u32[]{:S(2)}, u32[]{:S(2)}) collective-permute-start(f32[20,64,128]{2,1,0:T(8,128)S(1)} %get-tuple-element.49), channel_id=1, source_target_pairs={{0,1},{1,0},{2,3},{3,2},{4,5},{5,4},{6,7},{7,6},{8,9},{9,8},{10,11... | collective-permute-start | bytes 1966088 | tf_op jit(solution)/shard_map/ppermute | solution.py:583
  55.7 3.8 %prepare.1 = (f32[4,256,256]{2,1,0:T(8,128)}, bf16[1024,256]{1,0:T(8,128)(2,1)}) custom-call(s32[1024]{0:T(1024)} %docs_ref.13, bf16[1024,128]{1,0:T(8,128)(2,1)} %b_ref.3, bf16[1024,128]{1,0:T(8,128)(2,1)} %c_ref.13, f32[1024,128]{1,0:T(8,128)} %get-tuple-element.28.col_ref, s32[1,1024]{1,0:T(1,128)} %bitcast.63), custom_call_target="tpu_custom_call" | custom-call | tf_op jit(solution)/shard_map/prepare/pallas_call | solution.py:416
  59.5 6.7 %shard_map.136 = (f32[1024,2560]{1,0:T(8,128)}, bf16[1024,2560]{1,0:T(8,128)(2,1)}) custom-call(s32[1]{0:T(128)S(6)} %copy.47.live_ref, s32[1024]{0:T(1024)} %docs_ref.13, bf16[1024,2560]{1,0:T(8,128)(2,1)} %x_ref.11, bf16[1024,2560]{1,0:T(8,128)(2,1)} %z_ref.9, bf16[1024,128]{1,0:T(8,128)(2,1)} %c_ref.13, f32[40,1024]{1,0:T(8,128)} %get-tuple-element.27.g_ref, ...), custom_call_target="tpu_custom_call" | custom-call | flops 629145600 | bytes 5242880 | tf_op jit(solution)/shard_map/pallas_call | solution.py:441
  66.2 6.7 %shard_map.137 = (f32[1024,2560]{1,0:T(8,128)}, bf16[1024,2560]{1,0:T(8,128)(2,1)}) custom-call(s32[1]{0:T(128)S(6)} %copy.47.live_ref, s32[1024]{0:T(1024)} %docs_ref.13, bf16[1024,2560]{1,0:T(8,128)(2,1)} %x_ref.11, bf16[1024,2560]{1,0:T(8,128)(2,1)} %z_ref.9, bf16[1024,128]{1,0:T(8,128)(2,1)} %c_ref.13, ...), custom_call_target="tpu_custom_call", output_to_operand_aliasing={{0}: (12, {}), {1}: (13, {})} | custom-call | flops 629145600 | bytes 5242880 | tf_op jit(solution)/shard_map/pallas_call | solution.py:441
  72.9 6.7 %shard_map.138 = (f32[1024,2560]{1,0:T(8,128)}, bf16[1024,2560]{1,0:T(8,128)(2,1)}) custom-call(s32[1]{0:T(128)S(6)} %copy.47.live_ref, s32[1024]{0:T(1024)} %docs_ref.13, bf16[1024,2560]{1,0:T(8,128)(2,1)} %x_ref.11, bf16[1024,2560]{1,0:T(8,128)(2,1)} %z_ref.9, bf16[1024,128]{1,0:T(8,128)(2,1)} %c_ref.13, ...), custom_call_target="tpu_custom_call", output_to_operand_aliasing={{0}: (12, {}), {1}: (13, {})} | custom-call | flops 629145600 | bytes 5242880 | tf_op jit(solution)/shard_map/pallas_call | solution.py:441
  79.6 6.7 %shard_map.139 = (f32[1024,2560]{1,0:T(8,128)}, bf16[1024,2560]{1,0:T(8,128)(2,1)}) custom-call(s32[1]{0:T(128)S(6)} %copy.47.live_ref, s32[1024]{0:T(1024)} %docs_ref.13, bf16[1024,2560]{1,0:T(8,128)(2,1)} %x_ref.11, bf16[1024,2560]{1,0:T(8,128)(2,1)} %z_ref.9, bf16[1024,128]{1,0:T(8,128)(2,1)} %c_ref.13, ...), custom_call_target="tpu_custom_call", output_to_operand_aliasing={{0}: (12, {}), {1}: (13, {})} | custom-call | flops 629145600 | bytes 5242880 | tf_op jit(solution)/shard_map/pallas_call | solution.py:441
  86.4 0.0 copy-start.2
  86.4 6.7 %shard_map.140 = (f32[1024,2560]{1,0:T(8,128)}, bf16[1024,2560]{1,0:T(8,128)(2,1)}) custom-call(s32[1]{0:T(128)S(6)} %copy.47.live_ref, s32[1024]{0:T(1024)} %docs_ref.13, bf16[1024,2560]{1,0:T(8,128)(2,1)} %x_ref.11, bf16[1024,2560]{1,0:T(8,128)(2,1)} %z_ref.9, bf16[1024,128]{1,0:T(8,128)(2,1)} %c_ref.13, ...), custom_call_target="tpu_custom_call", output_to_operand_aliasing={{0}: (12, {}), {1}: (13, {})} | custom-call | flops 629145600 | bytes 5242880 | tf_op jit(solution)/shard_map/pallas_call | solution.py:441
  93.0 0.0 collective-permute-done.5.other_ref
  93.0 0.0 copy-done.2
  93.1 0.0 copy-start
  93.1 4.0 %copy-done = f32[1024,2560]{1,0:T(8,128)S(1)} copy-done((f32[1024,2560]{1,0:T(8,128)S(1)}, f32[1024,2560]{1,0:T(8,128)}, u32[]{:S(2)}) %copy-start) | copy-done | bytes 10485784
  97.0 0.0 copy-start.1
  97.0 2.5 %copy-done.1 = bf16[1024,2560]{1,0:T(8,128)(2,1)S(1)} copy-done((bf16[1024,2560]{1,0:T(8,128)(2,1)S(1)}, bf16[1024,2560]{1,0:T(8,128)(2,1)}, u32[]{:S(2)}) %copy-start.1) | copy-done | bytes 5242904
  99.5 0.0 copy-start.3
  99.5 4.0 %join.1 = (f32[1024,2560]{1,0:T(8,128)S(1)}, f32[1,1024]{1,0:T(1,128)S(1)}) custom-call(s32[1]{0:T(128)} %bitcast.sub_ref, f32[20,64,128]{2,1,0:T(8,128)S(1)} %get-tuple-element.50.own_ref, f32[20,64,128]{2,1,0:T(8,128)S(1)} %collective-permute-done.5.other_ref, bf16[1024,128]{1,0:T(8,128)(2,1)S(1)} %copy-done.2, f32[1024,2560]{1,0:T(8,128)S(1)} %copy-done, ...), custom_call_target="tpu_custom_call" | custom-call | tf_op jit(solution)/shard_map/join/pallas_call | solution.py:488
  103.5 1.3 %collective-permute-start.6 = (f32[1,1024]{1,0:T(1,128)S(1)}, f32[1,1024]{1,0:T(1,128)S(1)}, u32[]{:S(2)}, u32[]{:S(2)}) collective-permute-start(f32[1,1024]{1,0:T(1,128)S(1)} %get-tuple-element.43.square_ref), channel_id=1, source_target_pairs={{0,2},{2,0},{1,3},{3,1},{4,6},{6,4},{5,7},{7,5},{8,10},{10,8},{9,1... | collective-permute-start | bytes 12296 | tf_op jit(solution)/shard_map/ppermute | solution.py:536
  104.8 0.0 copy-done.3
  104.8 1.2 %collective-permute-done.6.more_ref = f32[1,1024]{1,0:T(1,128)S(1)} collective-permute-done((f32[1,1024]{1,0:T(1,128)S(1)}, f32[1,1024]{1,0:T(1,128)S(1)}, u32[]{:S(2)}, u32[]{:S(2)}) %collective-permute-start.6) | collective-permute-done | bytes 4128 | tf_op jit(solution)/shard_map/ppermute | solution.py:536
  106.0 3.3 %norm.1 = bf16[1024,2560]{1,0:T(8,128)(2,1)} custom-call(f32[1,1024]{1,0:T(1,128)S(1)} %get-tuple-element.43.square_ref, f32[1,1024]{1,0:T(1,128)S(1)} %collective-permute-done.6.more_ref, f32[1,2560]{1,0:T(1,128)S(1)} %reshape.66.gain_ref, f32[1024,2560]{1,0:T(8,128)S(1)} %get-tuple-element.44.gated_ref), custom_call_target="tpu_custom_call" | custom-call | tf_op jit(solution)/shard_map/norm/pallas_call | solution.py:510
  (26 shorter events, 0.5 us)
Async XLA Ops:
  11.1 2.8 %collective-permute-start = (f32[20,72,128]{2,1,0:T(8,128)}, f32[20,72,128]{2,1,0:T(8,128)S(1)}, u32[]{:S(2)}, u32[]{:S(2)}) collective-permute-start(f32[20,72,128]{2,1,0:T(8,128)} %get-tuple-element.25), channel_id=1, source_target_pairs={{0,1},{1,0},{2,3},{3,2},{4,5},{5,4},{6,7},{7,6},{8,9},{9,8},{10,11... | collective-permute-start | bytes 2211848 | tf_op jit(solution)/shard_map/ppermute | solution.py:545
  15.4 0.7 collective-permute-start.1
  16.2 19.2 %collective-permute-start.2 = (f32[648,128]{1,0:T(8,128)S(1)}, f32[648,128]{1,0:T(8,128)S(1)}, u32[]{:S(2)}, u32[]{:S(2)}) collective-permute-start(f32[648,128]{1,0:T(8,128)S(1)} %pad_maximum_fusion.2), channel_id=1, source_target_pairs={{0,4},{4,8},{1,5},{5,9},{2,6},{6,10},{3,7},{7,11},{16,20},{20,24},... | collective-permute-start | bytes 995336 | tf_op jit(solution)/shard_map/ppermute | solution.py:570
  35.5 9.4 %collective-permute-start.3 = (f32[648,128]{1,0:T(8,128)S(1)}, f32[648,128]{1,0:T(8,128)S(1)}, u32[]{:S(2)}, u32[]{:S(2)}) collective-permute-start(f32[648,128]{1,0:T(8,128)S(1)} %pad_maximum_fusion.1), channel_id=1, source_target_pairs={{4,8},{8,12},{5,9},{9,13},{6,10},{10,14},{7,11},{11,15},{20,24},{2... | collective-permute-start | bytes 995336 | tf_op jit(solution)/shard_map/ppermute | solution.py:570
  45.1 7.0 %collective-permute-start.4 = (f32[648,128]{1,0:T(8,128)S(1)}, f32[648,128]{1,0:T(8,128)S(1)}, u32[]{:S(2)}, u32[]{:S(2)}) collective-permute-start(f32[648,128]{1,0:T(8,128)S(1)} %pad_maximum_fusion), channel_id=1, source_target_pairs={{8,12},{9,13},{10,14},{11,15},{24,28},{25,29},{26,30},{27,31}} | collective-permute-start | bytes 995336 | tf_op jit(solution)/shard_map/ppermute | solution.py:570
  52.4 40.6 %collective-permute-start.5 = (f32[20,64,128]{2,1,0:T(8,128)S(1)}, f32[20,64,128]{2,1,0:T(8,128)S(1)}, u32[]{:S(2)}, u32[]{:S(2)}) collective-permute-start(f32[20,64,128]{2,1,0:T(8,128)S(1)} %get-tuple-element.49), channel_id=1, source_target_pairs={{0,1},{1,0},{2,3},{3,2},{4,5},{5,4},{6,7},{7,6},{8,9},{9,8},{10,11... | collective-permute-start | bytes 1966088 | tf_op jit(solution)/shard_map/ppermute | solution.py:583
  86.4 6.7 %copy-start.2 = (bf16[1024,128]{1,0:T(8,128)(2,1)S(1)}, bf16[1024,128]{1,0:T(8,128)(2,1)}, u32[]{:S(2)}) copy-start(bf16[1024,128]{1,0:T(8,128)(2,1)} %c_ref.13) | copy-start | bytes 786436
  93.1 4.0 %copy-start = (f32[1024,2560]{1,0:T(8,128)S(1)}, f32[1024,2560]{1,0:T(8,128)}, u32[]{:S(2)}) copy-start(f32[1024,2560]{1,0:T(8,128)} %get-tuple-element.41.y_ref) | copy-start | bytes 31457284
  97.0 2.5 %copy-start.1 = (bf16[1024,2560]{1,0:T(8,128)(2,1)S(1)}, bf16[1024,2560]{1,0:T(8,128)(2,1)}, u32[]{:S(2)}) copy-start(bf16[1024,2560]{1,0:T(8,128)(2,1)} %get-tuple-element.42.f_ref) | copy-start | bytes 15728644
  99.5 5.2 %copy-start.3 = (f32[2560]{0:T(1024)S(1)}, f32[2560]{0:T(1024)}, u32[]{:S(2)}) copy-start(f32[2560]{0:T(1024)} %param.22) | copy-start | bytes 30724
  103.5 2.5 %collective-permute-start.6 = (f32[1,1024]{1,0:T(1,128)S(1)}, f32[1,1024]{1,0:T(1,128)S(1)}, u32[]{:S(2)}, u32[]{:S(2)}) collective-permute-start(f32[1,1024]{1,0:T(1,128)S(1)} %get-tuple-element.43.square_ref), channel_id=1, source_target_pairs={{0,2},{2,0},{1,3},{3,1},{4,6},{6,4},{5,7},{7,5},{8,10},{10,8},{9,1... | collective-permute-start | bytes 12296 | tf_op jit(solution)/shard_map/ppermute | solution.py:536

commit v3 on v2

--- a/solution.py
+++ b/solution.py
@@ -125,15 +125,14 @@
     row_ref[...] = row
     hot_low = jnp.concatenate([hot_low_ref[...]] * 2, axis=0)
     state[...] = jnp.zeros_like(state)
+    scaled = (x_ref[...].astype(F32) * dot(col_parts[...], hot_low)).astype(BF16)
     for j in range(count):
         piece = slice(j * BLOCK, (j + 1) * BLOCK)
         prior = docs_ref[max(j * BLOCK - 1, 0)]
         passage = row[j : j + 1, :] * jnp.where(ends[j] == prior, 1.0, 0.0)
-        grown = dot(col_parts[piece, :], hot_low)
-        scaled = (x_ref[piece, :].astype(F32) * grown).astype(BF16)
         old = state[...]
-        enter_ref[j] = old
-        state[...] = passage * old + dot(inputs_t[:, piece], scaled)
+        enter_ref[j] = old.astype(BF16)
+        state[...] = passage * old + dot(inputs_t[:, piece], scaled[piece])
 
     half = state.shape[0] // 2
     total = row[2 * count : 2 * count + 1, :] * jnp.where(ends[count - 1] == docs_ref[0], 1.0, 0.0)
@@ -151,20 +150,25 @@
 
 
 def prepare_kernel(heads, docs_ref, b_ref, c_ref, col_ref, doc_row_ref, affinity_ref, entry_ref):
-    k = pl.program_id(0)
-    doc_col = col_ref[:, LANES - 1 : LANES]
-    doc_row = doc_row_ref[...].astype(F32)
     t = lax.broadcasted_iota(jnp.int32, (BLOCK, BLOCK), 0)
     s = lax.broadcasted_iota(jnp.int32, (BLOCK, BLOCK), 1)
-    affinity_ref[0] = jnp.where(
-        (t >= s) & (doc_col == doc_row), dot(c_ref[...], b_ref[...], ((1,), (1,))), 0.0
-    )
-    prior_doc = docs_ref[jnp.maximum(k * BLOCK - 1, 0)].astype(F32)
     lane = lax.broadcasted_iota(jnp.int32, (1, LANES), 1)
-    linked = (doc_col == prior_doc) & (lane < heads)
-    high, low = two_parts(jnp.where(linked, jnp.exp2(col_ref[...]), 0.0))
-    entry_ref[:, 0:LANES] = high
-    entry_ref[:, LANES:] = low
+    for j in range(affinity_ref.shape[0]):
+        piece = slice(j * BLOCK, (j + 1) * BLOCK)
+        block = pl.program_id(0) * affinity_ref.shape[0] + j
+        columns = col_ref[piece, :]
+        doc_col = columns[:, LANES - 1 :]
+        doc_row = doc_row_ref[:, piece].astype(F32)
+        affinity_ref[j] = jnp.where(
+            (t >= s) & (doc_col == doc_row),
+            dot(c_ref[piece, :], b_ref[piece, :], ((1,), (1,))),
+            0.0,
+        )
+        prior_doc = docs_ref[jnp.maximum(block * BLOCK - 1, 0)].astype(F32)
+        linked = (doc_col == prior_doc) & (lane < heads)
+        high, low = two_parts(jnp.where(linked, jnp.exp2(columns), 0.0))
+        entry_ref[piece, 0:LANES] = high
+        entry_ref[piece, LANES:] = low
 
 
 def inner_kernel(
@@ -199,7 +203,6 @@
     @pl.when(k < live_ref[0])
     def _():
         readout = c_ref[...]
-        twice = jnp.concatenate([readout, readout], axis=1)
         lane = lax.broadcasted_iota(jnp.int32, (1, LANES), 1)
         nothing = jnp.zeros((BLOCK, LANES), BF16)
         reaches = jnp.where(docs_ref[jnp.maximum(k * BLOCK - 1, 0)] == docs_ref[0], 1.0, 0.0)
@@ -232,10 +235,9 @@
                 jnp.concatenate([m[:half] for m in masked], axis=0),
             )
             lower = dot(jnp.concatenate(bottoms, axis=1), jnp.concatenate(masked, axis=0))
-            hot = hot_ref[:, cols]
-            enter = dot(entry_ref[...], jnp.concatenate([hot, hot], axis=0))
-            high, low = two_parts(enter_ref[0, :, cols])
-            outer = dot(twice, jnp.concatenate([high, low], axis=0))
+            hot = jnp.concatenate([hot_ref[:, cols]] * 2, axis=0)
+            enter = dot(entry_ref[...], hot)
+            outer = dot(readout, enter_ref[0, :, cols])
             skip = row_ref[2 * count + 1 : 2 * count + 2, cols]
             y = jnp.concatenate([upper, lower], axis=0) + enter * outer + skip * x.astype(F32)
             z = z_ref[:, cols].astype(F32)
@@ -255,22 +257,18 @@
     def _():
         total[...] = jnp.zeros_like(total)
 
-    highs, lows = [], []
+    parts = []
     for j in range(wide // LANES):
-        own, other = own_ref[j], other_ref[j]
-        carry = jnp.concatenate(
-            [jnp.where(second, other, own), jnp.where(second, own, other)], axis=0
+        own, other = own_ref[j].astype(BF16), other_ref[j].astype(BF16)
+        parts.append(
+            jnp.concatenate(
+                [jnp.where(second, other, own), jnp.where(second, own, other)], axis=0
+            )
         )
-        high, low = two_parts(carry)
-        highs.append(high)
-        lows.append(low)
-    carry = jnp.concatenate(
-        [jnp.concatenate(highs, axis=1), jnp.concatenate(lows, axis=1)], axis=0
-    )
+    carry = jnp.concatenate(parts, axis=1)
     for r in range(0, length, BLOCK):
         rows = slice(r, r + BLOCK)
-        readout = c_ref[rows, :]
-        outer = dot(jnp.concatenate([readout, readout], axis=1), carry)
+        outer = dot(c_ref[rows, :], carry)
         gated = y_ref[rows, :] + f_ref[rows, :].astype(F32) * outer
         gated_ref[rows, here] = gated
         square = total[rows, :]
@@ -312,10 +310,10 @@
 
 def plan(chips, tiles):
     chunks = 2 if tiles % 2 == 0 else 1
-    hops = chunks + chips - 2
-    group = 2 if tiles % 2 == 0 else 1
-    pieces = 5 if tiles % (5 * group) == 0 else 1
-    return chunks, hops, group, pieces
+    pieces = (tiles,)
+    if tiles % 10 == 0:
+        pieces = (3 * tiles // 10,) * 2 + (tiles // 5,) * 2
+    return chunks, chunks + chips - 2, pieces
 
 
 def on_device(
@@ -384,7 +382,7 @@
         out_shape=[
             jax.ShapeDtypeStruct((rows, length), F32),
             jax.ShapeDtypeStruct((length, LANES), F32),
-            jax.ShapeDtypeStruct((count, states, channels), F32),
+            jax.ShapeDtypeStruct((count, states, channels), BF16),
             jax.ShapeDtypeStruct((tiles, half + 8, LANES), F32),
             jax.ShapeDtypeStruct((tiles, half + 8, LANES), F32),
             jax.ShapeDtypeStruct((scalars, channels), F32),
@@ -413,19 +411,20 @@
         state_input,
     )
 
+    span = 2 if count % 2 == 0 else 1
     affinity, entry = pl.pallas_call(
         functools.partial(prepare_kernel, heads),
-        grid=(count,),
+        grid=(count // span,),
         in_specs=[
             SMEM,
-            pl.BlockSpec((BLOCK, states), lambda k: (k, 0)),
-            pl.BlockSpec((BLOCK, states), lambda k: (k, 0)),
-            pl.BlockSpec((BLOCK, LANES), lambda k: (k, 0)),
-            pl.BlockSpec((1, BLOCK), lambda k: (0, k)),
+            pl.BlockSpec((span * BLOCK, states), lambda k: (k, 0)),
+            pl.BlockSpec((span * BLOCK, states), lambda k: (k, 0)),
+            pl.BlockSpec((span * BLOCK, LANES), lambda k: (k, 0)),
+            pl.BlockSpec((1, span * BLOCK), lambda k: (0, k)),
         ],
         out_specs=[
-            pl.BlockSpec((1, BLOCK, BLOCK), lambda k: (k, 0, 0)),
-            pl.BlockSpec((BLOCK, 2 * LANES), lambda k: (k, 0)),
+            pl.BlockSpec((span, BLOCK, BLOCK), lambda k: (k, 0, 0)),
+            pl.BlockSpec((span * BLOCK, 2 * LANES), lambda k: (k, 0)),
         ],
         out_shape=[
             jax.ShapeDtypeStruct((count, BLOCK, BLOCK), F32),
@@ -434,29 +433,30 @@
         name="prepare",
     )(document_ids, state_input, state_readout, col, doc_row)
 
-    group, pieces = plan(lax.axis_size("seq"), tiles)[2:]
-    wide = channels // pieces
-    filled = ()
-    for q in range(pieces):
+    pieces = plan(lax.axis_size("seq"), tiles)[2]
+    group = 2 if tiles % 2 == 0 else 1
+    filled, at = (), 0
+    for size in pieces:
+        wide, first = size * LANES, at // size
         filled = pl.pallas_call(
-            functools.partial(inner_kernel, width, q * wide // LANES, group, count),
+            functools.partial(inner_kernel, width, at, group, count),
             grid=(count,),
             in_specs=[
                 SMEM,
                 SMEM,
-                pl.BlockSpec((BLOCK, wide), lambda k, q=q: (k, q)),
-                pl.BlockSpec((BLOCK, wide), lambda k, q=q: (k, q)),
+                pl.BlockSpec((BLOCK, wide), lambda k, q=first: (k, q)),
+                pl.BlockSpec((BLOCK, wide), lambda k, q=first: (k, q)),
                 pl.BlockSpec((BLOCK, states), lambda k: (k, 0)),
                 pl.BlockSpec((rows, BLOCK), lambda k: (0, k)),
                 pl.BlockSpec((BLOCK, LANES), lambda k: (k, 0)),
                 pl.BlockSpec((1, BLOCK, BLOCK), lambda k: (k, 0, 0)),
                 pl.BlockSpec((BLOCK, 2 * LANES), lambda k: (k, 0)),
-                pl.BlockSpec((1, states, wide), lambda k, q=q: (k, 0, q)),
-                pl.BlockSpec((scalars, wide), lambda k, q=q: (0, q)),
-                pl.BlockSpec((LANES, wide), lambda k, q=q: (0, q)),
+                pl.BlockSpec((1, states, wide), lambda k, q=first: (k, 0, q)),
+                pl.BlockSpec((scalars, wide), lambda k, q=first: (0, q)),
+                pl.BlockSpec((LANES, wide), lambda k, q=first: (0, q)),
             ]
             + [pl.BlockSpec(memory_space=pl.ANY)] * len(filled),
-            out_specs=[pl.BlockSpec((BLOCK, wide), lambda k, q=q: (k, q))] * 2,
+            out_specs=[pl.BlockSpec((BLOCK, wide), lambda k, q=first: (k, q))] * 2,
             out_shape=[
                 jax.ShapeDtypeStruct((length, channels), F32),
                 jax.ShapeDtypeStruct((length, channels), BF16),
@@ -482,6 +482,7 @@
             hot,
             *filled,
         )
+        at += size
 
     own, other = carry_in(own, sent, half)
 
@@ -504,7 +505,13 @@
         scratch_shapes=[pltpu.VMEM((length, LANES), F32)],
         compiler_params=pltpu.CompilerParams(vmem_limit_bytes=24 << 20),
         name="join",
-    )(sub, own, other, state_readout, *filled)
+    )(
+        sub,
+        own,
+        other,
+        state_readout,
+        *[pltpu.with_memory_space_constraint(part, pltpu.HBM) for part in filled],
+    )
 
     squares, more = summed(squares, "head")
     return pl.pallas_call(

time: 110 us -> 99.8 us (0.907)
  local copies, waits for them, and re-layouts: 6.58 us -> 0.13 us
  Pallas kernels: 55 us -> 51.2 us
    unnamed x13 -> x9, local copies, waits for them, and re-layouts: 6.48 us -> 0.03 us
    pallas_call x6 -> x5, Pallas kernels: 37.3 us -> 31.6 us  [the longest x4 29 us: on_device(): pl.pallas_call(functools.partial(inner_kernel, width, at, group, count),...]
    pallas_call x1, Pallas kernels: 3.96 us -> 7.61 us  [on_device(): pl.pallas_call(join_kernel, grid=(channels // chunk,), in_specs=[SMEM, pl...]
    pallas_call x1, Pallas kernels: 10.4 us -> 8.71 us  [on_device(): pl.pallas_call(functools.partial(state_kernel, heads), grid=(channels //...]
  transfers between devices with their start and end apart: 7 -> 7, of which waited for: 5 -> 5; matrix products, arithmetic and copies ran while one was open for 0% -> 0% of each run, Pallas kernels for 34% -> 32%
where the time goes in v3:
time: 99.8 us; the launch traced here: 99.1 us
  Pallas kernels  51.2 us (51%)
  waiting for transfers between devices  33.4 us (33%)
  starting transfers between devices  11.4 us (11%)
  other arithmetic  1.95 us (2%)
    ppermute x4, waiting for transfers between devices, carry_in(): got = lax.ppermute(send, 'seq', pairs)  30.1 us
    pallas_call x4, Pallas kernels, on_device(): pl.pallas_call(functools.partial(inner_kernel, width, at, group, count),...  29 us
    pallas_call x1, Pallas kernels, on_device(): pl.pallas_call(functools.partial(state_kernel, heads), grid=(channels //...  8.71 us
    pallas_call x1, Pallas kernels, on_device(): pl.pallas_call(join_kernel, grid=(channels // chunk,), in_specs=[SMEM, pl...  7.61 us
    ppermute x4, starting transfers between devices, carry_in(): got = lax.ppermute(send, 'seq', pairs)  6.11 us
    ppermute x1, starting transfers between devices, carry_in(): lax.ppermute(jnp.where(second, entering, onward), 'sub', [(0, 1), (1, 0)])  3.3 us
    pallas_call x1, Pallas kernels, on_device(): pl.pallas_call(functools.partial(norm_kernel, channels * lax.axis_size('h...  3.26 us
    pallas_call x1, Pallas kernels, on_device(): pl.pallas_call(functools.partial(prepare_kernel, heads), grid=(count // s...  2.56 us
  transfers between devices with their start and end apart: 7, of which 5 were waited for; matrix products, arithmetic and copies ran while one was open for 0% of the time, Pallas kernels for 32%

profile of v3, /device:TPU:17, one launch (start us, length us, event | category | flops | bytes accessed | tf_op | source)
XLA Modules:
  0.0 99.1 jit_solution(12241273656710614619)
XLA Ops:
  0.7 8.7 %shard_state.1 = (f32[40,1024]{1,0:T(8,128)}, f32[1024,128]{1,0:T(8,128)}, bf16[4,128,2560]{2,1,0:T(8,128)(2,1)}, f32[20,72,128]{2,1,0:T(8,128)}, f32[20,72,128]{2,1,0:T(8,128)}, /*index=5*/f32[16,2560]{1,0:T(8,128)}) custom-call(s32[1]{0:T(128)S(6)} %copy.43.live_ref, s32[1024]{0:T(1024)} %docs_ref.11, s32[1]{0:T(128)} %bitcast.sub_ref, ...), custom_call_target="tpu_custom_call" | custom-call | tf_op jit(solution)/shard_map/shard_state/pallas_call | solution.py:356
  9.4 0.7 collective-permute-start
  10.1 2.1 %collective-permute-done = f32[20,72,128]{2,1,0:T(8,128)S(1)} collective-permute-done((f32[20,72,128]{2,1,0:T(8,128)}, f32[20,72,128]{2,1,0:T(8,128)S(1)}, u32[]{:S(2)}, u32[]{:S(2)}) %collective-permute-start) | collective-permute-done | bytes 737312 | tf_op jit(solution)/shard_map/ppermute | solution.py:552
  12.1 1.2 %broadcast_select_fusion = (f32[20,72,128]{2,1,0:T(8,128)S(1)}, f32[20,72,128]{2,1,0:T(8,128)S(1)}) fusion(f32[20,72,128]{2,1,0:T(8,128)} %get-tuple-element.24, f32[20,72,128]{2,1,0:T(8,128)S(1)} %collective-permute-done, pred[]{:T(512)S(6)} %eq.32), kind=kLoop, calls=%fused_computation.9 | loop fusion | flops 368640 | bytes 2949121 | tf_op jit(solution)/shard_map/jit(_where)/select_n | solution.py:554
  13.4 0.1 slice_add_fusion
  13.6 0.7 collective-permute-start.1
  14.3 0.0 collective-permute-done.1
  14.5 1.3 %collective-permute-start.2 = (f32[648,128]{1,0:T(8,128)S(1)}, f32[648,128]{1,0:T(8,128)S(1)}, u32[]{:S(2)}, u32[]{:S(2)}) collective-permute-start(f32[648,128]{1,0:T(8,128)S(1)} %pad_maximum_fusion.2), channel_id=1, source_target_pairs={{0,4},{4,8},{1,5},{5,9},{2,6},{6,10},{3,7},{7,11},{16,20},{20,24},... | collective-permute-start | bytes 995336 | tf_op jit(solution)/shard_map/ppermute | solution.py:577
  15.8 17.9 %collective-permute-done.2 = f32[648,128]{1,0:T(8,128)S(1)} collective-permute-done((f32[648,128]{1,0:T(8,128)S(1)}, f32[648,128]{1,0:T(8,128)S(1)}, u32[]{:S(2)}, u32[]{:S(2)}) %collective-permute-start.2) | collective-permute-done | bytes 331808 | tf_op jit(solution)/shard_map/ppermute | solution.py:577
  33.8 1.9 %collective-permute-start.3 = (f32[648,128]{1,0:T(8,128)S(1)}, f32[648,128]{1,0:T(8,128)S(1)}, u32[]{:S(2)}, u32[]{:S(2)}) collective-permute-start(f32[648,128]{1,0:T(8,128)S(1)} %pad_maximum_fusion.1), channel_id=1, source_target_pairs={{4,8},{8,12},{5,9},{9,13},{6,10},{10,14},{7,11},{11,15},{20,24},{2... | collective-permute-start | bytes 995336 | tf_op jit(solution)/shard_map/ppermute | solution.py:577
  35.7 7.5 %collective-permute-done.3 = f32[648,128]{1,0:T(8,128)S(1)} collective-permute-done((f32[648,128]{1,0:T(8,128)S(1)}, f32[648,128]{1,0:T(8,128)S(1)}, u32[]{:S(2)}, u32[]{:S(2)}) %collective-permute-start.3) | collective-permute-done | bytes 331808 | tf_op jit(solution)/shard_map/ppermute | solution.py:577
  43.4 2.2 %collective-permute-start.4 = (f32[648,128]{1,0:T(8,128)S(1)}, f32[648,128]{1,0:T(8,128)S(1)}, u32[]{:S(2)}, u32[]{:S(2)}) collective-permute-start(f32[648,128]{1,0:T(8,128)S(1)} %pad_maximum_fusion), channel_id=1, source_target_pairs={{8,12},{9,13},{10,14},{11,15},{24,28},{25,29},{26,30},{27,31}} | collective-permute-start | bytes 995336 | tf_op jit(solution)/shard_map/ppermute | solution.py:577
  45.6 4.7 %collective-permute-done.4 = f32[648,128]{1,0:T(8,128)S(1)} collective-permute-done((f32[648,128]{1,0:T(8,128)S(1)}, f32[648,128]{1,0:T(8,128)S(1)}, u32[]{:S(2)}, u32[]{:S(2)}) %collective-permute-start.4) | collective-permute-done | bytes 331808 | tf_op jit(solution)/shard_map/ppermute | solution.py:577
  50.4 0.1 select_select_fusion.1
  50.5 0.2 fusion
  50.7 3.3 %collective-permute-start.5 = (f32[20,64,128]{2,1,0:T(8,128)S(1)}, f32[20,64,128]{2,1,0:T(8,128)S(1)}, u32[]{:S(2)}, u32[]{:S(2)}) collective-permute-start(f32[20,64,128]{2,1,0:T(8,128)S(1)} %get-tuple-element.45), channel_id=1, source_target_pairs={{0,1},{1,0},{2,3},{3,2},{4,5},{5,4},{6,7},{7,6},{8,9},{9,8},{10,11... | collective-permute-start | bytes 1966088 | tf_op jit(solution)/shard_map/ppermute | solution.py:590
  54.0 2.6 %prepare.1 = (f32[4,256,256]{2,1,0:T(8,128)}, bf16[1024,256]{1,0:T(8,128)(2,1)}) custom-call(s32[1024]{0:T(1024)} %docs_ref.11, bf16[1024,128]{1,0:T(8,128)(2,1)} %b_ref.3, bf16[1024,128]{1,0:T(8,128)(2,1)} %c_ref.11, f32[1024,128]{1,0:T(8,128)} %get-tuple-element.26.col_ref, s32[1,1024]{1,0:T(1,128)} %bitcast.63), custom_call_target="tpu_custom_call" | custom-call | tf_op jit(solution)/shard_map/prepare/pallas_call | solution.py:415
  56.6 8.0 %shard_map.136 = (f32[1024,2560]{1,0:T(8,128)}, bf16[1024,2560]{1,0:T(8,128)(2,1)}) custom-call(s32[1]{0:T(128)S(6)} %copy.43.live_ref, s32[1024]{0:T(1024)} %docs_ref.11, bf16[1024,2560]{1,0:T(8,128)(2,1)} %x_ref.9, bf16[1024,2560]{1,0:T(8,128)(2,1)} %z_ref.7, bf16[1024,128]{1,0:T(8,128)(2,1)} %c_ref.11, f32[40,1024]{1,0:T(8,128)} %get-tuple-element.25.g_ref, ...), custom_call_target="tpu_custom_call" | custom-call | flops 943718400 | bytes 7864320 | tf_op jit(solution)/shard_map/pallas_call | solution.py:441
  64.5 8.0 %shard_map.137 = (f32[1024,2560]{1,0:T(8,128)}, bf16[1024,2560]{1,0:T(8,128)(2,1)}) custom-call(s32[1]{0:T(128)S(6)} %copy.43.live_ref, s32[1024]{0:T(1024)} %docs_ref.11, bf16[1024,2560]{1,0:T(8,128)(2,1)} %x_ref.9, bf16[1024,2560]{1,0:T(8,128)(2,1)} %z_ref.7, bf16[1024,128]{1,0:T(8,128)(2,1)} %c_ref.11, ...), custom_call_target="tpu_custom_call", output_to_operand_aliasing={{0}: (12, {}), {1}: (13, {})} | custom-call | flops 943718400 | bytes 7864320 | tf_op jit(solution)/shard_map/pallas_call | solution.py:441
  72.6 6.5 %shard_map.138 = (f32[1024,2560]{1,0:T(8,128)}, bf16[1024,2560]{1,0:T(8,128)(2,1)}) custom-call(s32[1]{0:T(128)S(6)} %copy.43.live_ref, s32[1024]{0:T(1024)} %docs_ref.11, bf16[1024,2560]{1,0:T(8,128)(2,1)} %x_ref.9, bf16[1024,2560]{1,0:T(8,128)(2,1)} %z_ref.7, bf16[1024,128]{1,0:T(8,128)(2,1)} %c_ref.11, ...), custom_call_target="tpu_custom_call", output_to_operand_aliasing={{0}: (12, {}), {1}: (13, {})} | custom-call | flops 629145600 | bytes 5242880 | tf_op jit(solution)/shard_map/pallas_call | solution.py:441
  79.1 0.0 copy-start
  79.1 6.5 %shard_map.139 = (f32[1024,2560]{1,0:T(8,128)}, bf16[1024,2560]{1,0:T(8,128)(2,1)}) custom-call(s32[1]{0:T(128)S(6)} %copy.43.live_ref, s32[1024]{0:T(1024)} %docs_ref.11, bf16[1024,2560]{1,0:T(8,128)(2,1)} %x_ref.9, bf16[1024,2560]{1,0:T(8,128)(2,1)} %z_ref.7, bf16[1024,128]{1,0:T(8,128)(2,1)} %c_ref.11, ...), custom_call_target="tpu_custom_call", output_to_operand_aliasing={{0}: (12, {}), {1}: (13, {})} | custom-call | flops 629145600 | bytes 5242880 | tf_op jit(solution)/shard_map/pallas_call | solution.py:441
  85.6 0.0 collective-permute-done.5.other_ref
  85.6 0.0 copy-done
  85.6 0.0 copy-start.1
  85.7 7.6 %join.1 = (f32[1024,2560]{1,0:T(8,128)S(1)}, f32[1,1024]{1,0:T(1,128)S(1)}) custom-call(s32[1]{0:T(128)} %bitcast.sub_ref, f32[20,64,128]{2,1,0:T(8,128)S(1)} %get-tuple-element.46.own_ref, f32[20,64,128]{2,1,0:T(8,128)S(1)} %collective-permute-done.5.other_ref, bf16[1024,128]{1,0:T(8,128)(2,1)S(1)} %copy-done, f32[1024,2560]{1,0:T(8,128)} %get-tuple-element.37.y_ref, ...), custom_call_target="tpu_custom_call" | custom-call | tf_op jit(solution)/shard_map/join/pallas_call | solution.py:489
  93.3 1.3 %collective-permute-start.6 = (f32[1,1024]{1,0:T(1,128)S(1)}, f32[1,1024]{1,0:T(1,128)S(1)}, u32[]{:S(2)}, u32[]{:S(2)}) collective-permute-start(f32[1,1024]{1,0:T(1,128)S(1)} %get-tuple-element.39.square_ref), channel_id=1, source_target_pairs={{0,2},{2,0},{1,3},{3,1},{4,6},{6,4},{5,7},{7,5},{8,10},{10,8},{9,1... | collective-permute-start | bytes 12296 | tf_op jit(solution)/shard_map/ppermute | solution.py:543
  94.5 0.0 copy-done.1
  94.5 1.3 %collective-permute-done.6.more_ref = f32[1,1024]{1,0:T(1,128)S(1)} collective-permute-done((f32[1,1024]{1,0:T(1,128)S(1)}, f32[1,1024]{1,0:T(1,128)S(1)}, u32[]{:S(2)}, u32[]{:S(2)}) %collective-permute-start.6) | collective-permute-done | bytes 4128 | tf_op jit(solution)/shard_map/ppermute | solution.py:543
  95.8 3.3 %norm.1 = bf16[1024,2560]{1,0:T(8,128)(2,1)} custom-call(f32[1,1024]{1,0:T(1,128)S(1)} %get-tuple-element.39.square_ref, f32[1,1024]{1,0:T(1,128)S(1)} %collective-permute-done.6.more_ref, f32[1,2560]{1,0:T(1,128)S(1)} %reshape.66.gain_ref, f32[1024,2560]{1,0:T(8,128)S(1)} %get-tuple-element.40.gated_ref), custom_call_target="tpu_custom_call" | custom-call | tf_op jit(solution)/shard_map/norm/pallas_call | solution.py:517
  (26 shorter events, 0.5 us)
Async XLA Ops:
  9.4 2.8 %collective-permute-start = (f32[20,72,128]{2,1,0:T(8,128)}, f32[20,72,128]{2,1,0:T(8,128)S(1)}, u32[]{:S(2)}, u32[]{:S(2)}) collective-permute-start(f32[20,72,128]{2,1,0:T(8,128)} %get-tuple-element.23), channel_id=1, source_target_pairs={{0,1},{1,0},{2,3},{3,2},{4,5},{5,4},{6,7},{7,6},{8,9},{9,8},{10,11... | collective-permute-start | bytes 2211848 | tf_op jit(solution)/shard_map/ppermute | solution.py:552
  13.6 0.7 collective-permute-start.1
  14.5 19.2 %collective-permute-start.2 = (f32[648,128]{1,0:T(8,128)S(1)}, f32[648,128]{1,0:T(8,128)S(1)}, u32[]{:S(2)}, u32[]{:S(2)}) collective-permute-start(f32[648,128]{1,0:T(8,128)S(1)} %pad_maximum_fusion.2), channel_id=1, source_target_pairs={{0,4},{4,8},{1,5},{5,9},{2,6},{6,10},{3,7},{7,11},{16,20},{20,24},... | collective-permute-start | bytes 995336 | tf_op jit(solution)/shard_map/ppermute | solution.py:577
  33.8 9.4 %collective-permute-start.3 = (f32[648,128]{1,0:T(8,128)S(1)}, f32[648,128]{1,0:T(8,128)S(1)}, u32[]{:S(2)}, u32[]{:S(2)}) collective-permute-start(f32[648,128]{1,0:T(8,128)S(1)} %pad_maximum_fusion.1), channel_id=1, source_target_pairs={{4,8},{8,12},{5,9},{9,13},{6,10},{10,14},{7,11},{11,15},{20,24},{2... | collective-permute-start | bytes 995336 | tf_op jit(solution)/shard_map/ppermute | solution.py:577
  43.4 7.0 %collective-permute-start.4 = (f32[648,128]{1,0:T(8,128)S(1)}, f32[648,128]{1,0:T(8,128)S(1)}, u32[]{:S(2)}, u32[]{:S(2)}) collective-permute-start(f32[648,128]{1,0:T(8,128)S(1)} %pad_maximum_fusion), channel_id=1, source_target_pairs={{8,12},{9,13},{10,14},{11,15},{24,28},{25,29},{26,30},{27,31}} | collective-permute-start | bytes 995336 | tf_op jit(solution)/shard_map/ppermute | solution.py:577
  50.7 34.9 %collective-permute-start.5 = (f32[20,64,128]{2,1,0:T(8,128)S(1)}, f32[20,64,128]{2,1,0:T(8,128)S(1)}, u32[]{:S(2)}, u32[]{:S(2)}) collective-permute-start(f32[20,64,128]{2,1,0:T(8,128)S(1)} %get-tuple-element.45), channel_id=1, source_target_pairs={{0,1},{1,0},{2,3},{3,2},{4,5},{5,4},{6,7},{7,6},{8,9},{9,8},{10,11... | collective-permute-start | bytes 1966088 | tf_op jit(solution)/shard_map/ppermute | solution.py:590
  79.1 6.6 %copy-start = (bf16[1024,128]{1,0:T(8,128)(2,1)S(1)}, bf16[1024,128]{1,0:T(8,128)(2,1)}, u32[]{:S(2)}) copy-start(bf16[1024,128]{1,0:T(8,128)(2,1)} %c_ref.11) | copy-start | bytes 786436
  85.6 8.9 %copy-start.1 = (f32[2560]{0:T(1024)S(1)}, f32[2560]{0:T(1024)}, u32[]{:S(2)}) copy-start(f32[2560]{0:T(1024)} %param.22) | copy-start | bytes 30724
  93.3 2.5 %collective-permute-start.6 = (f32[1,1024]{1,0:T(1,128)S(1)}, f32[1,1024]{1,0:T(1,128)S(1)}, u32[]{:S(2)}, u32[]{:S(2)}) collective-permute-start(f32[1,1024]{1,0:T(1,128)S(1)} %get-tuple-element.39.square_ref), channel_id=1, source_target_pairs={{0,2},{2,0},{1,3},{3,1},{4,6},{6,4},{5,7},{7,5},{8,10},{10,8},{9,1... | collective-permute-start | bytes 12296 | tf_op jit(solution)/shard_map/ppermute | solution.py:543

commit v4 on v3

--- a/solution.py
+++ b/solution.py
@@ -12,6 +12,7 @@
 BLOCK = 256
 LANES = 128
 LOG2E = math.log2(math.e)
+INNER_VMEM = 40 << 20
 F32 = jnp.float32
 BF16 = jnp.bfloat16
 
@@ -246,40 +247,36 @@
             f_ref[:, cols] = (enter * gate * passed[:, cols]).astype(BF16)
 
 
-def join_kernel(sub_ref, own_ref, other_ref, c_ref, y_ref, f_ref, gated_ref, square_ref, total):
-    k = pl.program_id(0)
+def join_kernel(sub_ref, own_ref, other_ref, c_ref, *refs):
+    pieces = (len(refs) - 3) // 2
+    gated_ref, square_ref, total = refs[2 * pieces :]
     length = c_ref.shape[0]
-    wide = own_ref.shape[0] * LANES
-    here = pl.ds(pl.multiple_of(k * wide, wide), wide)
     second = sub_ref[0] == 1
-
-    @pl.when(k == 0)
-    def _():
-        total[...] = jnp.zeros_like(total)
-
-    parts = []
-    for j in range(wide // LANES):
-        own, other = own_ref[j].astype(BF16), other_ref[j].astype(BF16)
-        parts.append(
-            jnp.concatenate(
-                [jnp.where(second, other, own), jnp.where(second, own, other)], axis=0
-            )
-        )
-    carry = jnp.concatenate(parts, axis=1)
-    for r in range(0, length, BLOCK):
-        rows = slice(r, r + BLOCK)
-        outer = dot(c_ref[rows, :], carry)
-        gated = y_ref[rows, :] + f_ref[rows, :].astype(F32) * outer
-        gated_ref[rows, here] = gated
-        square = total[rows, :]
-        for j in range(wide // LANES):
-            piece = gated[:, j * LANES : (j + 1) * LANES]
-            square = square + piece * piece
-        total[rows, :] = square
-
-    @pl.when(k == pl.num_programs(0) - 1)
-    def _():
-        square_ref[...] = jnp.sum(total[...].T, axis=0, keepdims=True)
+    total[...] = jnp.zeros_like(total)
+    tile = 0
+    for y_ref, f_ref in zip(refs[:pieces], refs[pieces : 2 * pieces]):
+        wide = chunk_of(y_ref.shape[1], 4 * LANES)
+        for c in range(0, y_ref.shape[1], wide):
+            parts = []
+            for j in range(tile, tile + wide // LANES):
+                own, other = own_ref[j].astype(BF16), other_ref[j].astype(BF16)
+                parts.append(
+                    jnp.concatenate(
+                        [jnp.where(second, other, own), jnp.where(second, own, other)], axis=0
+                    )
+                )
+            carry = jnp.concatenate(parts, axis=1)
+            for r in range(0, length, BLOCK):
+                rows = slice(r, r + BLOCK)
+                outer = dot(c_ref[rows, :], carry)
+                gated = y_ref[rows, c : c + wide] + f_ref[rows, c : c + wide].astype(F32) * outer
+                gated_ref[rows, tile * LANES : tile * LANES + wide] = gated
+                square = total[rows, :]
+                for j in range(0, wide, LANES):
+                    square = square + gated[:, j : j + LANES] * gated[:, j : j + LANES]
+                total[rows, :] = square
+            tile += wide // LANES
+    square_ref[...] = jnp.sum(total[...].T, axis=0, keepdims=True)
 
 
 def norm_kernel(channels_all, square_ref, more_ref, gain_ref, gated_ref, out_ref):
@@ -435,10 +432,25 @@
 
     pieces = plan(lax.axis_size("seq"), tiles)[2]
     group = 2 if tiles % 2 == 0 else 1
-    filled, at = (), 0
+    ys, fs, at = [], [], 0
+    inputs = [
+        pltpu.with_memory_space_constraint(value, pltpu.HBM)
+        for value in (
+            token_values,
+            gate_values,
+            state_readout,
+            g,
+            col,
+            affinity,
+            entry,
+            enter,
+            row,
+            hot,
+        )
+    ]
     for size in pieces:
         wide, first = size * LANES, at // size
-        filled = pl.pallas_call(
+        y, f = pl.pallas_call(
             functools.partial(inner_kernel, width, at, group, count),
             grid=(count,),
             in_specs=[
@@ -454,64 +466,37 @@
                 pl.BlockSpec((1, states, wide), lambda k, q=first: (k, 0, q)),
                 pl.BlockSpec((scalars, wide), lambda k, q=first: (0, q)),
                 pl.BlockSpec((LANES, wide), lambda k, q=first: (0, q)),
-            ]
-            + [pl.BlockSpec(memory_space=pl.ANY)] * len(filled),
-            out_specs=[pl.BlockSpec((BLOCK, wide), lambda k, q=first: (k, q))] * 2,
+            ],
+            out_specs=[pl.BlockSpec((BLOCK, wide), lambda k: (k, 0))] * 2,
             out_shape=[
-                jax.ShapeDtypeStruct((length, channels), F32),
-                jax.ShapeDtypeStruct((length, channels), BF16),
+                jax.ShapeDtypeStruct((length, wide), F32),
+                jax.ShapeDtypeStruct((length, wide), BF16),
             ],
-            input_output_aliases={12: 0, 13: 1} if filled else {},
             cost_estimate=pl.CostEstimate(
                 flops=length * wide * 1200,
                 bytes_accessed=length * wide * 10,
                 transcendentals=0,
             ),
-        )(
-            live_blocks,
-            document_ids,
-            token_values,
-            gate_values,
-            state_readout,
-            g,
-            col,
-            affinity,
-            entry,
-            enter,
-            row,
-            hot,
-            *filled,
-        )
+            compiler_params=pltpu.CompilerParams(vmem_limit_bytes=INNER_VMEM),
+        )(live_blocks, document_ids, *inputs)
+        ys.append(y)
+        fs.append(f)
         at += size
 
     own, other = carry_in(own, sent, half)
 
     gated, squares = pl.pallas_call(
         join_kernel,
-        grid=(channels // chunk,),
-        in_specs=[
-            SMEM,
-            pl.BlockSpec((per_chunk, half, LANES), lambda k: (k, 0, 0)),
-            pl.BlockSpec((per_chunk, half, LANES), lambda k: (k, 0, 0)),
-            whole((length, states)),
-            pl.BlockSpec((length, chunk), lambda k: (0, k)),
-            pl.BlockSpec((length, chunk), lambda k: (0, k)),
-        ],
-        out_specs=[VMEM, whole((1, length))],
+        in_specs=[SMEM] + [VMEM] * (3 + 2 * len(pieces)),
+        out_specs=[VMEM, VMEM],
         out_shape=[
             jax.ShapeDtypeStruct((length, channels), F32),
             jax.ShapeDtypeStruct((1, length), F32),
         ],
         scratch_shapes=[pltpu.VMEM((length, LANES), F32)],
-        compiler_params=pltpu.CompilerParams(vmem_limit_bytes=24 << 20),
+        compiler_params=pltpu.CompilerParams(vmem_limit_bytes=16 << 20),
         name="join",
-    )(
-        sub,
-        own,
-        other,
-        state_readout,
-        *[pltpu.with_memory_space_constraint(part, pltpu.HBM) for part in filled],
-    )
+    )(sub, own, other, state_readout, *ys, *fs)
 
     squares, more = summed(squares, "head")
     return pl.pallas_call(

time: 99.8 us -> 89.5 us (0.90)
  Pallas kernels: 51.2 us -> 41 us
    pallas_call x4, Pallas kernels: 29 us -> 23.8 us  [on_device(): pl.pallas_call(functools.partial(inner_kernel, width, at, group, count),...]
    pallas_call x1, Pallas kernels: 7.61 us -> 2.65 us  [on_device(): pl.pallas_call(join_kernel, in_specs=[SMEM] + [VMEM] * (3 + 2 * len(piece...]
  transfers between devices with their start and end apart: 7 -> 7, of which waited for: 5 -> 5; matrix products, arithmetic and copies ran while one was open for 0% -> 0% of each run, Pallas kernels for 32% -> 30%
where the time goes in v4:
time: 89.5 us; the launch traced here: 88.9 us
  Pallas kernels  41 us (46%)
  waiting for transfers between devices  33.4 us (37%)
  starting transfers between devices  11.5 us (13%)
  other arithmetic  1.92 us (2%)
  between operations  0.96 us (1%)
    ppermute x4, waiting for transfers between devices, carry_in(): got = lax.ppermute(send, 'seq', pairs)  30.1 us
    pallas_call x4, Pallas kernels, on_device(): pl.pallas_call(functools.partial(inner_kernel, width, at, group, count),...  23.8 us
    pallas_call x1, Pallas kernels, on_device(): pl.pallas_call(functools.partial(state_kernel, heads), grid=(channels //...  8.69 us
    ppermute x4, starting transfers between devices, carry_in(): got = lax.ppermute(send, 'seq', pairs)  6.11 us
    ppermute x1, starting transfers between devices, carry_in(): lax.ppermute(jnp.where(second, entering, onward), 'sub', [(0, 1), (1, 0)])  3.3 us
    pallas_call x1, Pallas kernels, on_device(): pl.pallas_call(functools.partial(norm_kernel, channels * lax.axis_size('h...  3.27 us
    pallas_call x1, Pallas kernels, on_device(): pl.pallas_call(join_kernel, in_specs=[SMEM] + [VMEM] * (3 + 2 * len(piece...  2.65 us
    pallas_call x1, Pallas kernels, on_device(): pl.pallas_call(functools.partial(prepare_kernel, heads), grid=(count // s...  2.56 us
  transfers between devices with their start and end apart: 7, of which 5 were waited for; matrix products, arithmetic and copies ran while one was open for 0% of the time, Pallas kernels for 30%

profile of v4, /device:TPU:17, one launch (start us, length us, event | category | flops | bytes accessed | tf_op | source)
XLA Modules:
  0.0 88.9 jit_solution(9521631047286715244)
XLA Ops:
  0.7 8.7 %shard_state.1 = (f32[40,1024]{1,0:T(8,128)}, f32[1024,128]{1,0:T(8,128)}, bf16[4,128,2560]{2,1,0:T(8,128)(2,1)}, f32[20,72,128]{2,1,0:T(8,128)}, f32[20,72,128]{2,1,0:T(8,128)}, /*index=5*/f32[16,2560]{1,0:T(8,128)}) custom-call(s32[1]{0:T(128)S(6)} %copy.31.live_ref, s32[1024]{0:T(1024)} %docs_ref.11, s32[1]{0:T(128)} %bitcast.sub_ref, ...), custom_call_target="tpu_custom_call" | custom-call | tf_op jit(solution)/shard_map/shard_state/pallas_call | solution.py:353
  9.4 0.8 collective-permute-start
  10.2 2.1 %collective-permute-done = f32[20,72,128]{2,1,0:T(8,128)S(1)} collective-permute-done((f32[20,72,128]{2,1,0:T(8,128)}, f32[20,72,128]{2,1,0:T(8,128)S(1)}, u32[]{:S(2)}, u32[]{:S(2)}) %collective-permute-start) | collective-permute-done | bytes 737312 | tf_op jit(solution)/shard_map/ppermute | solution.py:537
  12.2 1.2 %broadcast_select_fusion = (f32[20,72,128]{2,1,0:T(8,128)S(1)}, f32[20,72,128]{2,1,0:T(8,128)S(1)}) fusion(f32[20,72,128]{2,1,0:T(8,128)} %get-tuple-element.24, f32[20,72,128]{2,1,0:T(8,128)S(1)} %collective-permute-done, pred[]{:T(512)S(6)} %eq.32), kind=kLoop, calls=%fused_computation.9 | loop fusion | flops 368640 | bytes 2949121 | tf_op jit(solution)/shard_map/jit(_where)/select_n | solution.py:539
  13.5 0.1 slice_add_fusion
  13.7 0.7 collective-permute-start.1
  14.4 0.0 collective-permute-done.1
  14.6 1.3 %collective-permute-start.2 = (f32[648,128]{1,0:T(8,128)S(1)}, f32[648,128]{1,0:T(8,128)S(1)}, u32[]{:S(2)}, u32[]{:S(2)}) collective-permute-start(f32[648,128]{1,0:T(8,128)S(1)} %pad_maximum_fusion.2), channel_id=1, source_target_pairs={{0,4},{4,8},{1,5},{5,9},{2,6},{6,10},{3,7},{7,11},{16,20},{20,24},... | collective-permute-start | bytes 995336 | tf_op jit(solution)/shard_map/ppermute | solution.py:562
  15.9 17.9 %collective-permute-done.2 = f32[648,128]{1,0:T(8,128)S(1)} collective-permute-done((f32[648,128]{1,0:T(8,128)S(1)}, f32[648,128]{1,0:T(8,128)S(1)}, u32[]{:S(2)}, u32[]{:S(2)}) %collective-permute-start.2) | collective-permute-done | bytes 331808 | tf_op jit(solution)/shard_map/ppermute | solution.py:562
  33.9 1.9 %collective-permute-start.3 = (f32[648,128]{1,0:T(8,128)S(1)}, f32[648,128]{1,0:T(8,128)S(1)}, u32[]{:S(2)}, u32[]{:S(2)}) collective-permute-start(f32[648,128]{1,0:T(8,128)S(1)} %pad_maximum_fusion.1), channel_id=1, source_target_pairs={{4,8},{8,12},{5,9},{9,13},{6,10},{10,14},{7,11},{11,15},{20,24},{2... | collective-permute-start | bytes 995336 | tf_op jit(solution)/shard_map/ppermute | solution.py:562
  35.8 7.5 %collective-permute-done.3 = f32[648,128]{1,0:T(8,128)S(1)} collective-permute-done((f32[648,128]{1,0:T(8,128)S(1)}, f32[648,128]{1,0:T(8,128)S(1)}, u32[]{:S(2)}, u32[]{:S(2)}) %collective-permute-start.3) | collective-permute-done | bytes 331808 | tf_op jit(solution)/shard_map/ppermute | solution.py:562
  43.4 2.2 %collective-permute-start.4 = (f32[648,128]{1,0:T(8,128)S(1)}, f32[648,128]{1,0:T(8,128)S(1)}, u32[]{:S(2)}, u32[]{:S(2)}) collective-permute-start(f32[648,128]{1,0:T(8,128)S(1)} %pad_maximum_fusion), channel_id=1, source_target_pairs={{8,12},{9,13},{10,14},{11,15},{24,28},{25,29},{26,30},{27,31}} | collective-permute-start | bytes 995336 | tf_op jit(solution)/shard_map/ppermute | solution.py:562
  45.6 4.7 %collective-permute-done.4 = f32[648,128]{1,0:T(8,128)S(1)} collective-permute-done((f32[648,128]{1,0:T(8,128)S(1)}, f32[648,128]{1,0:T(8,128)S(1)}, u32[]{:S(2)}, u32[]{:S(2)}) %collective-permute-start.4) | collective-permute-done | bytes 331808 | tf_op jit(solution)/shard_map/ppermute | solution.py:562
  50.4 0.0 copy-start.1
  50.4 0.1 select_select_fusion.1
  50.5 0.2 fusion
  50.7 3.3 %collective-permute-start.5 = (f32[20,64,128]{2,1,0:T(8,128)S(1)}, f32[20,64,128]{2,1,0:T(8,128)S(1)}, u32[]{:S(2)}, u32[]{:S(2)}) collective-permute-start(f32[20,64,128]{2,1,0:T(8,128)S(1)} %get-tuple-element.45), channel_id=1, source_target_pairs={{0,1},{1,0},{2,3},{3,2},{4,5},{5,4},{6,7},{7,6},{8,9},{9,8},{10,11... | collective-permute-start | bytes 1966088 | tf_op jit(solution)/shard_map/ppermute | solution.py:575
  54.0 2.6 %prepare.1 = (f32[4,256,256]{2,1,0:T(8,128)}, bf16[1024,256]{1,0:T(8,128)(2,1)}) custom-call(s32[1024]{0:T(1024)} %docs_ref.11, bf16[1024,128]{1,0:T(8,128)(2,1)} %b_ref.3, bf16[1024,128]{1,0:T(8,128)(2,1)} %c_ref.11, f32[1024,128]{1,0:T(8,128)} %get-tuple-element.26.col_ref, s32[1,1024]{1,0:T(1,128)} %bitcast.52), custom_call_target="tpu_custom_call" | custom-call | tf_op jit(solution)/shard_map/prepare/pallas_call | solution.py:412
  56.6 0.0 copy-done.1
  56.6 5.4 %shard_map.139 = (f32[1024,512]{1,0:T(8,128)S(1)}, bf16[1024,512]{1,0:T(8,128)(2,1)S(1)}) custom-call(s32[1]{0:T(128)S(6)} %copy.31.live_ref, s32[1024]{0:T(1024)S(1)} %copy-done.1, bf16[1024,2560]{1,0:T(8,128)(2,1)} %x_ref.9, bf16[1024,2560]{1,0:T(8,128)(2,1)} %z_ref.7, bf16[1024,128]{1,0:T(8,128)(2,1)} %c_ref.11, f32[40,1024]{1,0:T(8,128)} %get-tuple-element.25.g_ref, ...), custom_call_target="tpu_custom_call" | custom-call | flops 629145600 | bytes 5242880 | tf_op jit(solution)/shard_map/pallas_call | solution.py:453
  62.0 5.4 %shard_map.138 = (f32[1024,512]{1,0:T(8,128)S(1)}, bf16[1024,512]{1,0:T(8,128)(2,1)S(1)}) custom-call(s32[1]{0:T(128)S(6)} %copy.31.live_ref, s32[1024]{0:T(1024)S(1)} %copy-done.1, bf16[1024,2560]{1,0:T(8,128)(2,1)} %x_ref.9, bf16[1024,2560]{1,0:T(8,128)(2,1)} %z_ref.7, bf16[1024,128]{1,0:T(8,128)(2,1)} %c_ref.11, f32[40,1024]{1,0:T(8,128)} %get-tuple-element.25.g_ref, ...), custom_call_target="tpu_custom_call" | custom-call | flops 629145600 | bytes 5242880 | tf_op jit(solution)/shard_map/pallas_call | solution.py:453
  67.3 6.5 %shard_map.137 = (f32[1024,768]{1,0:T(8,128)S(1)}, bf16[1024,768]{1,0:T(8,128)(2,1)S(1)}) custom-call(s32[1]{0:T(128)S(6)} %copy.31.live_ref, s32[1024]{0:T(1024)S(1)} %copy-done.1, bf16[1024,2560]{1,0:T(8,128)(2,1)} %x_ref.9, bf16[1024,2560]{1,0:T(8,128)(2,1)} %z_ref.7, bf16[1024,128]{1,0:T(8,128)(2,1)} %c_ref.11, f32[40,1024]{1,0:T(8,128)} %get-tuple-element.25.g_ref, ...), custom_call_target="tpu_custom_call" | custom-call | flops 943718400 | bytes 7864320 | tf_op jit(solution)/shard_map/pallas_call | solution.py:453
  73.8 0.0 copy-start
  73.9 6.5 %shard_map.136 = (f32[1024,768]{1,0:T(8,128)S(1)}, bf16[1024,768]{1,0:T(8,128)(2,1)S(1)}) custom-call(s32[1]{0:T(128)S(6)} %copy.31.live_ref, s32[1024]{0:T(1024)S(1)} %copy-done.1, bf16[1024,2560]{1,0:T(8,128)(2,1)} %x_ref.9, bf16[1024,2560]{1,0:T(8,128)(2,1)} %z_ref.7, bf16[1024,128]{1,0:T(8,128)(2,1)} %c_ref.11, f32[40,1024]{1,0:T(8,128)} %get-tuple-element.25.g_ref, ...), custom_call_target="tpu_custom_call" | custom-call | flops 943718400 | bytes 7864320 | tf_op jit(solution)/shard_map/pallas_call | solution.py:453
  80.4 0.0 collective-permute-done.5.other_ref
  80.4 0.0 copy-done
  80.4 0.0 copy-start.2
  80.4 2.7 %join.1 = (f32[1024,2560]{1,0:T(8,128)S(1)}, f32[1,1024]{1,0:T(1,128)S(1)}) custom-call(s32[1]{0:T(128)} %bitcast.sub_ref, f32[20,64,128]{2,1,0:T(8,128)S(1)} %get-tuple-element.46.own_ref, f32[20,64,128]{2,1,0:T(8,128)S(1)} %collective-permute-done.5.other_ref, bf16[1024,128]{1,0:T(8,128)(2,1)S(1)} %copy-done, f32[1024,768]{1,0:T(8,128)S(1)} %get-tuple-element.31.refs_0_, ...), custom_call_target="tpu_custom_call" | custom-call | tf_op jit(solution)/shard_map/join/pallas_call | solution.py:488
  83.1 1.3 %collective-permute-start.6 = (f32[1,1024]{1,0:T(1,128)S(1)}, f32[1,1024]{1,0:T(1,128)S(1)}, u32[]{:S(2)}, u32[]{:S(2)}) collective-permute-start(f32[1,1024]{1,0:T(1,128)S(1)} %get-tuple-element.39.square_ref), channel_id=1, source_target_pairs={{0,2},{2,0},{1,3},{3,1},{4,6},{6,4},{5,7},{7,5},{8,10},{10,8},{9,1... | collective-permute-start | bytes 12296 | tf_op jit(solution)/shard_map/ppermute | solution.py:528
  84.4 0.0 copy-done.2
  84.4 1.2 %collective-permute-done.6.more_ref = f32[1,1024]{1,0:T(1,128)S(1)} collective-permute-done((f32[1,1024]{1,0:T(1,128)S(1)}, f32[1,1024]{1,0:T(1,128)S(1)}, u32[]{:S(2)}, u32[]{:S(2)}) %collective-permute-start.6) | collective-permute-done | bytes 4128 | tf_op jit(solution)/shard_map/ppermute | solution.py:528
  85.6 3.3 %norm.1 = bf16[1024,2560]{1,0:T(8,128)(2,1)} custom-call(f32[1,1024]{1,0:T(1,128)S(1)} %get-tuple-element.39.square_ref, f32[1,1024]{1,0:T(1,128)S(1)} %collective-permute-done.6.more_ref, f32[1,2560]{1,0:T(1,128)S(1)} %reshape.66.gain_ref, f32[1024,2560]{1,0:T(8,128)S(1)} %get-tuple-element.40.gated_ref), custom_call_target="tpu_custom_call" | custom-call | tf_op jit(solution)/shard_map/norm/pallas_call | solution.py:502
  (26 shorter events, 0.5 us)
Async XLA Ops:
  9.4 2.9 %collective-permute-start = (f32[20,72,128]{2,1,0:T(8,128)}, f32[20,72,128]{2,1,0:T(8,128)S(1)}, u32[]{:S(2)}, u32[]{:S(2)}) collective-permute-start(f32[20,72,128]{2,1,0:T(8,128)} %get-tuple-element.23), channel_id=1, source_target_pairs={{0,1},{1,0},{2,3},{3,2},{4,5},{5,4},{6,7},{7,6},{8,9},{9,8},{10,11... | collective-permute-start | bytes 2211848 | tf_op jit(solution)/shard_map/ppermute | solution.py:537
  13.7 0.7 collective-permute-start.1
  14.6 19.2 %collective-permute-start.2 = (f32[648,128]{1,0:T(8,128)S(1)}, f32[648,128]{1,0:T(8,128)S(1)}, u32[]{:S(2)}, u32[]{:S(2)}) collective-permute-start(f32[648,128]{1,0:T(8,128)S(1)} %pad_maximum_fusion.2), channel_id=1, source_target_pairs={{0,4},{4,8},{1,5},{5,9},{2,6},{6,10},{3,7},{7,11},{16,20},{20,24},... | collective-permute-start | bytes 995336 | tf_op jit(solution)/shard_map/ppermute | solution.py:562
  33.9 9.4 %collective-permute-start.3 = (f32[648,128]{1,0:T(8,128)S(1)}, f32[648,128]{1,0:T(8,128)S(1)}, u32[]{:S(2)}, u32[]{:S(2)}) collective-permute-start(f32[648,128]{1,0:T(8,128)S(1)} %pad_maximum_fusion.1), channel_id=1, source_target_pairs={{4,8},{8,12},{5,9},{9,13},{6,10},{10,14},{7,11},{11,15},{20,24},{2... | collective-permute-start | bytes 995336 | tf_op jit(solution)/shard_map/ppermute | solution.py:562
  43.4 7.0 %collective-permute-start.4 = (f32[648,128]{1,0:T(8,128)S(1)}, f32[648,128]{1,0:T(8,128)S(1)}, u32[]{:S(2)}, u32[]{:S(2)}) collective-permute-start(f32[648,128]{1,0:T(8,128)S(1)} %pad_maximum_fusion), channel_id=1, source_target_pairs={{8,12},{9,13},{10,14},{11,15},{24,28},{25,29},{26,30},{27,31}} | collective-permute-start | bytes 995336 | tf_op jit(solution)/shard_map/ppermute | solution.py:562
  50.4 6.2 %copy-start.1 = (s32[1024]{0:T(1024)S(1)}, s32[1024]{0:T(1024)}, u32[]{:S(2)}) copy-start(s32[1024]{0:T(1024)} %docs_ref.11) | copy-start | bytes 12292
  50.7 29.7 %collective-permute-start.5 = (f32[20,64,128]{2,1,0:T(8,128)S(1)}, f32[20,64,128]{2,1,0:T(8,128)S(1)}, u32[]{:S(2)}, u32[]{:S(2)}) collective-permute-start(f32[20,64,128]{2,1,0:T(8,128)S(1)} %get-tuple-element.45), channel_id=1, source_target_pairs={{0,1},{1,0},{2,3},{3,2},{4,5},{5,4},{6,7},{7,6},{8,9},{9,8},{10,11... | collective-permute-start | bytes 1966088 | tf_op jit(solution)/shard_map/ppermute | solution.py:575
  73.8 6.6 %copy-start = (bf16[1024,128]{1,0:T(8,128)(2,1)S(1)}, bf16[1024,128]{1,0:T(8,128)(2,1)}, u32[]{:S(2)}) copy-start(bf16[1024,128]{1,0:T(8,128)(2,1)} %c_ref.11) | copy-start | bytes 786436
  80.4 3.9 %copy-start.2 = (f32[2560]{0:T(1024)S(1)}, f32[2560]{0:T(1024)}, u32[]{:S(2)}) copy-start(f32[2560]{0:T(1024)} %param.22) | copy-start | bytes 30724
  83.1 2.5 %collective-permute-start.6 = (f32[1,1024]{1,0:T(1,128)S(1)}, f32[1,1024]{1,0:T(1,128)S(1)}, u32[]{:S(2)}, u32[]{:S(2)}) collective-permute-start(f32[1,1024]{1,0:T(1,128)S(1)} %get-tuple-element.39.square_ref), channel_id=1, source_target_pairs={{0,2},{2,0},{1,3},{3,1},{4,6},{6,4},{5,7},{7,5},{8,10},{10,8},{9,1... | collective-permute-start | bytes 12296 | tf_op jit(solution)/shard_map/ppermute | solution.py:528

commit v5 on v4

--- a/solution.py
+++ b/solution.py
@@ -12,7 +12,8 @@
 BLOCK = 256
 LANES = 128
 LOG2E = math.log2(math.e)
-INNER_VMEM = 40 << 20
+INNER_VMEM = 24 << 20
+EARLY_VMEM = 32 << 20
 F32 = jnp.float32
 BF16 = jnp.bfloat16
 
@@ -48,7 +49,7 @@
     heads,
     live_ref,
     docs_ref,
-    sub_ref,
+    spot_ref,
     raw_ref,
     bias_ref,
     decay_ref,
@@ -137,13 +138,15 @@
 
     half = state.shape[0] // 2
     total = row[2 * count : 2 * count + 1, :] * jnp.where(ends[count - 1] == docs_ref[0], 1.0, 0.0)
-    mine = pl.multiple_of(sub_ref[0] * half, half)
-    theirs = pl.multiple_of((1 - sub_ref[0]) * half, half)
+    mine = pl.multiple_of(spot_ref[0] * half, half)
+    theirs = pl.multiple_of((1 - spot_ref[0]) * half, half)
     line = lax.broadcasted_iota(jnp.int32, (8, LANES), 0)
-    first, last = docs_ref[0].astype(F32), docs_ref[length - 1].astype(F32)
+    marks = jnp.zeros((8, LANES), F32)
+    for at, mark in enumerate((docs_ref[0], docs_ref[length - 1], spot_ref[0], spot_ref[1])):
+        marks = jnp.where(line == at + 1, mark.astype(F32), marks)
     for j in range(wide // LANES):
         cols = slice(j * LANES, (j + 1) * LANES)
-        foot = jnp.where(line == 0, total[:, cols], jnp.where(line == 1, first, last))
+        foot = jnp.where(line == 0, total[:, cols], marks)
         own_ref[j, 0:half, :] = state[pl.ds(mine, half), cols]
         sent_ref[j, 0:half, :] = state[pl.ds(theirs, half), cols]
         own_ref[j, half:, :] = foot
@@ -247,11 +250,11 @@
             f_ref[:, cols] = (enter * gate * passed[:, cols]).astype(BF16)
 
 
-def join_kernel(sub_ref, own_ref, other_ref, c_ref, *refs):
+def join_kernel(spot_ref, own_ref, other_ref, c_ref, *refs):
     pieces = (len(refs) - 3) // 2
     gated_ref, square_ref, total = refs[2 * pieces :]
     length = c_ref.shape[0]
-    second = sub_ref[0] == 1
+    second = spot_ref[0] == 1
     total[...] = jnp.zeros_like(total)
     tile = 0
     for y_ref, f_ref in zip(refs[:pieces], refs[pieces : 2 * pieces]):
@@ -279,15 +282,22 @@
     square_ref[...] = jnp.sum(total[...].T, axis=0, keepdims=True)
 
 
-def norm_kernel(channels_all, square_ref, more_ref, gain_ref, gated_ref, out_ref):
+def norm_kernel(channels_all, square_ref, more_ref, gain_ref, gated_ref, out_ref, scale):
     rows = out_ref.shape[0]
     start = pl.multiple_of(pl.program_id(0) * rows, rows)
-    scale = lax.rsqrt((square_ref[...] + more_ref[...]) / channels_all + 1e-05)
-    scale = jnp.broadcast_to(scale, (LANES, rows)).T
-    for j in range(gated_ref.shape[1] // LANES):
-        cols = slice(j * LANES, (j + 1) * LANES)
-        gated = gated_ref[pl.ds(start, rows), cols]
-        out_ref[:, cols] = (gated * gain_ref[:, cols] * scale).astype(BF16)
+    row = lax.rsqrt((square_ref[...] + more_ref[...]) / channels_all + 1e-05)
+    scale[...] = jnp.broadcast_to(row, (LANES, rows)).T
+
+    def strip(i, rest):
+        at = pl.multiple_of(i * 32, 32)
+        part = scale[pl.ds(at, 32), :]
+        for j in range(gated_ref.shape[1] // LANES):
+            cols = slice(j * LANES, (j + 1) * LANES)
+            gated = gated_ref[pl.ds(start + at, 32), cols]
+            out_ref[pl.ds(at, 32), cols] = (gated * gain_ref[:, cols] * part).astype(BF16)
+        return rest
+
+    lax.fori_loop(0, rows // 32, strip, 0)
 
 
 def chunk_of(total, most):
@@ -299,6 +309,10 @@
 
 def whole(shape):
     return pl.BlockSpec(shape, lambda k, *_: (0,) * len(shape))
+
+
+def in_hbm(*values):
+    return [pltpu.with_memory_space_constraint(value, pltpu.HBM) for value in values]
 
 
 SMEM = pl.BlockSpec(memory_space=pltpu.SMEM)
@@ -341,7 +355,7 @@
     if rows != heads:
         raw = jnp.pad(raw, ((0, rows - heads), (0, 0)))
     doc_row = document_ids.reshape(1, length)
-    sub = lax.axis_index("sub").astype(jnp.int32).reshape(1)
+    spot = jnp.stack([lax.axis_index("sub"), lax.axis_index("seq")]).astype(jnp.int32)
     head_of = np.arange(channels)[None, :] // width
     lanes = np.arange(LANES)[:, None]
     hot = jnp.asarray(lanes == head_of, dtype=BF16)
@@ -391,21 +405,24 @@
             pltpu.VMEM((states, chunk), F32),
             pltpu.VMEM((scalars, LANES), F32),
         ],
+        compiler_params=pltpu.CompilerParams(vmem_limit_bytes=EARLY_VMEM),
         name="shard_state",
     )(
         live_blocks,
         document_ids,
-        sub,
-        raw,
-        step_bias.reshape(1, heads),
-        decay_log.reshape(1, heads),
-        skip_gain.reshape(1, heads),
-        doc_row,
-        tri,
-        hot,
-        hot_low,
-        token_values,
-        state_input,
+        spot,
+        *in_hbm(
+            raw,
+            step_bias.reshape(1, heads),
+            decay_log.reshape(1, heads),
+            skip_gain.reshape(1, heads),
+            doc_row,
+            tri,
+            hot,
+            hot_low,
+            token_values,
+            state_input,
+        ),
     )
 
     span = 2 if count % 2 == 0 else 1
@@ -427,27 +444,15 @@
             jax.ShapeDtypeStruct((count, BLOCK, BLOCK), F32),
             jax.ShapeDtypeStruct((length, 2 * LANES), BF16),
         ],
+        compiler_params=pltpu.CompilerParams(vmem_limit_bytes=EARLY_VMEM),
         name="prepare",
-    )(document_ids, state_input, state_readout, col, doc_row)
+    )(document_ids, *in_hbm(state_input, state_readout), col, doc_row)
 
     pieces = plan(lax.axis_size("seq"), tiles)[2]
     group = 2 if tiles % 2 == 0 else 1
     ys, fs, at = [], [], 0
-    inputs = [
-        pltpu.with_memory_space_constraint(value, pltpu.HBM)
-        for value in (
-            token_values,
-            gate_values,
-            state_readout,
-            g,
-            col,
-            affinity,
-            entry,
-            enter,
-            row,
-            hot,
-        )
-    ]
+    x, z, readout, heads_hot = in_hbm(token_values, gate_values, state_readout, hot)
+    inputs = (x, z, readout, g, col, affinity, entry, enter, row, heads_hot)
     for size in pieces:
         wide, first = size * LANES, at // size
         y, f = pl.pallas_call(
@@ -496,7 +501,7 @@
         scratch_shapes=[pltpu.VMEM((length, LANES), F32)],
         compiler_params=pltpu.CompilerParams(vmem_limit_bytes=16 << 20),
         name="join",
-    )(sub, own, other, state_readout, *ys, *fs)
+    )(spot, own, other, state_readout, *ys, *fs)
 
     squares, more = summed(squares, "head")
     return pl.pallas_call(
@@ -510,6 +515,7 @@
         ],
         out_specs=pl.BlockSpec((BLOCK, channels), lambda k: (k, 0)),
         out_shape=jax.ShapeDtypeStruct((length, channels), BF16),
+        scratch_shapes=[pltpu.VMEM((BLOCK, LANES), F32)],
         compiler_params=pltpu.CompilerParams(vmem_limit_bytes=16 << 20),
         name="norm",
     )(squares, more, norm_gain.reshape(1, channels), gated)
@@ -532,8 +538,8 @@
 
 def carry_in(own, sent, half):
     tiles = own.shape[0]
-    second = lax.axis_index("sub") == 1
-    place, chips = lax.axis_index("seq"), lax.axis_size("seq")
+    chips = lax.axis_size("seq")
+    second, place = own[0, half + 3] == 1.0, own[0, half + 4]
     got = lax.ppermute(sent, "sub", [(0, 1), (1, 0)])
     early = jnp.where(second, got, own)
     late = jnp.where(second, own, got)
@@ -549,19 +555,21 @@
     rows = size * half
     tail = jnp.broadcast_to(last, (8, LANES))
 
-    def at(array, index):
-        return lax.dynamic_slice_in_dim(array, index * size, size, 0)
+    def at(array, t):
+        part = array[:size]
+        for c in range(1, chunks):
+            part = jnp.where(place <= t - c, array[c * size : (c + 1) * size], part)
+        return part
 
     carry = jnp.zeros((size, half, LANES), F32)
     received = []
     for t in range(hops):
-        index = jnp.clip(t - place, 0, chunks - 1)
-        send = at(chip_decay, index) * carry + at(chip_state, index)
+        send = at(chip_decay, t) * carry + at(chip_state, t)
         send = jnp.concatenate([send.reshape(rows, LANES), tail], axis=0)
         pairs = [(z, z + 1) for z in range(chips - 1) if 0 <= t - z < chunks]
         got = lax.ppermute(send, "seq", pairs)
-        joined = jnp.where(got[rows : rows + 1] == first, 1.0, 0.0)
-        carry = joined[None] * got[:rows].reshape(size, half, LANES)
+        joined = jnp.where(got[rows] == first, 1.0, 0.0)
+        carry = joined * got[:rows].reshape(size, half, LANES)
         received.append(carry)
     parts = []
     for c in range(chunks):

time: 89.5 us -> 84.6 us (0.945)
  Pallas kernels: 41 us -> 37.4 us
    pallas_call x4, Pallas kernels: 23.8 us -> 21.8 us  [on_device(): pl.pallas_call(functools.partial(inner_kernel, width, at, group, count),...]
    pallas_call x1, Pallas kernels: 8.69 us -> 7.35 us  [on_device(): pl.pallas_call(functools.partial(state_kernel, heads), grid=(channels //...]
    select_n x1, other arithmetic: 1.21 us -> 0.1 us  [carry_in(): late = jnp.where(second, own, got)]
    pallas_call x1, Pallas kernels: 2.56 us -> 1.55 us  [on_device(): pl.pallas_call(functools.partial(prepare_kernel, heads), grid=(count // s...]
  transfers between devices with their start and end apart: 7 -> 7, of which waited for: 5 -> 5; matrix products, arithmetic and copies ran while one was open for 0% -> 0% of each run, Pallas kernels for 30% -> 28%
where the time goes in v5:
time: 84.6 us; the launch traced here: 84.2 us
  Pallas kernels  37.4 us (44%)
  waiting for transfers between devices  33.2 us (39%)
  starting transfers between devices  11.4 us (13%)
  other arithmetic  1.04 us (1%)
  between operations  0.96 us (1%)
    ppermute x4, waiting for transfers between devices, carry_in(): got = lax.ppermute(send, 'seq', pairs)  30.1 us
    pallas_call x4, Pallas kernels, on_device(): pl.pallas_call(functools.partial(inner_kernel, width, at, group, count),...  21.8 us
    pallas_call x1, Pallas kernels, on_device(): pl.pallas_call(functools.partial(state_kernel, heads), grid=(channels //...  7.35 us
    ppermute x4, starting transfers between devices, carry_in(): got = lax.ppermute(send, 'seq', pairs)  6.11 us
    pallas_call x1, Pallas kernels, on_device(): pl.pallas_call(functools.partial(norm_kernel, channels * lax.axis_size('h...  3.48 us
    ppermute x1, starting transfers between devices, carry_in(): lax.ppermute(jnp.where(second, entering, onward), 'sub', [(0, 1), (1, 0)])  3.3 us
    pallas_call x1, Pallas kernels, on_device(): pl.pallas_call(join_kernel, in_specs=[SMEM] + [VMEM] * (3 + 2 * len(piece...  3.24 us
    ppermute x1, waiting for transfers between devices, carry_in(): got = lax.ppermute(sent, 'sub', [(0, 1), (1, 0)])  1.83 us
  transfers between devices with their start and end apart: 7, of which 5 were waited for; matrix products, arithmetic and copies ran while one was open for 0% of the time, Pallas kernels for 28%

profile of v5, /device:TPU:17, one launch (start us, length us, event | category | flops | bytes accessed | tf_op | source)
XLA Modules:
  0.0 84.2 jit_solution(8548037058203176010)
XLA Ops:
  0.7 0.1 pad_add_fusion.spot_ref
  0.7 7.3 %shard_state.1 = (f32[40,1024]{1,0:T(8,128)S(1)}, f32[1024,128]{1,0:T(8,128)S(1)}, bf16[4,128,2560]{2,1,0:T(8,128)(2,1)S(1)}, f32[20,72,128]{2,1,0:T(8,128)S(1)}...) custom-call(s32[1]{0:T(128)S(6)} %copy.31.live_ref, s32[1024]{0:T(1024)} %docs_ref.11, s32[2]{0:T(128)S(1)} %pad_add_fusion.spot_ref, ...), custom_call_target="tpu_custom_call" | custom-call | tf_op jit(solution)/shard_map/shard_state/pallas_call | solution.py:367
  8.1 0.7 collective-permute-start
  8.8 1.8 %collective-permute-done = f32[20,72,128]{2,1,0:T(8,128)S(1)} collective-permute-done((f32[20,72,128]{2,1,0:T(8,128)S(1)}, f32[20,72,128]{2,1,0:T(8,128)S(1)}, u32[]{:S(2)}, u32[]{:S(2)}) %collective-permute-start) | collective-permute-done | bytes 737312 | tf_op jit(solution)/shard_map/ppermute | solution.py:543
  10.7 0.1 broadcast_select_fusion
  10.9 0.1 slice_add_fusion
  11.0 0.7 collective-permute-start.1
  11.7 0.0 collective-permute-done.1
  11.8 0.1 select_add_fusion.2
  11.9 1.3 %collective-permute-start.2 = (f32[648,128]{1,0:T(8,128)S(1)}, f32[648,128]{1,0:T(8,128)S(1)}, u32[]{:S(2)}, u32[]{:S(2)}) collective-permute-start(f32[648,128]{1,0:T(8,128)S(1)} %pad_maximum_fusion.2), channel_id=1, source_target_pairs={{0,4},{4,8},{1,5},{5,9},{2,6},{6,10},{3,7},{7,11},{16,20},{20,24},... | collective-permute-start | bytes 995336 | tf_op jit(solution)/shard_map/ppermute | solution.py:570
  13.2 17.9 %collective-permute-done.2 = f32[648,128]{1,0:T(8,128)S(1)} collective-permute-done((f32[648,128]{1,0:T(8,128)S(1)}, f32[648,128]{1,0:T(8,128)S(1)}, u32[]{:S(2)}, u32[]{:S(2)}) %collective-permute-start.2) | collective-permute-done | bytes 331808 | tf_op jit(solution)/shard_map/ppermute | solution.py:570
  31.1 0.1 select_add_fusion.1
  31.3 1.9 %collective-permute-start.3 = (f32[648,128]{1,0:T(8,128)S(1)}, f32[648,128]{1,0:T(8,128)S(1)}, u32[]{:S(2)}, u32[]{:S(2)}) collective-permute-start(f32[648,128]{1,0:T(8,128)S(1)} %pad_maximum_fusion.1), channel_id=1, source_target_pairs={{4,8},{8,12},{5,9},{9,13},{6,10},{10,14},{7,11},{11,15},{20,24},{2... | collective-permute-start | bytes 995336 | tf_op jit(solution)/shard_map/ppermute | solution.py:570
  33.2 7.5 %collective-permute-done.3 = f32[648,128]{1,0:T(8,128)S(1)} collective-permute-done((f32[648,128]{1,0:T(8,128)S(1)}, f32[648,128]{1,0:T(8,128)S(1)}, u32[]{:S(2)}, u32[]{:S(2)}) %collective-permute-start.3) | collective-permute-done | bytes 331808 | tf_op jit(solution)/shard_map/ppermute | solution.py:570
  40.7 0.1 select_add_fusion
  40.8 0.0 copy-start.1
  40.9 2.2 %collective-permute-start.4 = (f32[648,128]{1,0:T(8,128)S(1)}, f32[648,128]{1,0:T(8,128)S(1)}, u32[]{:S(2)}, u32[]{:S(2)}) collective-permute-start(f32[648,128]{1,0:T(8,128)S(1)} %pad_maximum_fusion), channel_id=1, source_target_pairs={{8,12},{9,13},{10,14},{11,15},{24,28},{25,29},{26,30},{27,31}} | collective-permute-start | bytes 995336 | tf_op jit(solution)/shard_map/ppermute | solution.py:570
  43.1 4.7 %collective-permute-done.4 = f32[648,128]{1,0:T(8,128)S(1)} collective-permute-done((f32[648,128]{1,0:T(8,128)S(1)}, f32[648,128]{1,0:T(8,128)S(1)}, u32[]{:S(2)}, u32[]{:S(2)}) %collective-permute-start.4) | collective-permute-done | bytes 331808 | tf_op jit(solution)/shard_map/ppermute | solution.py:570
  47.9 0.1 select_select_fusion.1
  48.0 0.2 fusion
  48.2 3.3 %collective-permute-start.5 = (f32[20,64,128]{2,1,0:T(8,128)S(1)}, f32[20,64,128]{2,1,0:T(8,128)S(1)}, u32[]{:S(2)}, u32[]{:S(2)}) collective-permute-start(f32[20,64,128]{2,1,0:T(8,128)S(1)} %get-tuple-element.45), channel_id=1, source_target_pairs={{0,1},{1,0},{2,3},{3,2},{4,5},{5,4},{6,7},{7,6},{8,9},{9,8},{10,11... | collective-permute-start | bytes 1966088 | tf_op jit(solution)/shard_map/ppermute | solution.py:583
  51.5 0.0 copy-done.1
  51.5 1.6 %prepare.1 = (f32[4,256,256]{2,1,0:T(8,128)S(1)}, bf16[1024,256]{1,0:T(8,128)(2,1)S(1)}) custom-call(s32[1024]{0:T(1024)S(1)} %copy-done.1, bf16[1024,128]{1,0:T(8,128)(2,1)} %b_ref.3, bf16[1024,128]{1,0:T(8,128)(2,1)} %c_ref.11, f32[1024,128]{1,0:T(8,128)S(1)} %get-tuple-element.26.col_ref, s32[1,1024]{1,0:T(1,128)S(1)} %bitcast.75), custom_call_target="tpu_custom_call" | custom-call | tf_op jit(solution)/shard_map/prepare/pallas_call | solution.py:429
  53.0 4.8 %shard_map.139 = (f32[1024,512]{1,0:T(8,128)S(1)}, bf16[1024,512]{1,0:T(8,128)(2,1)S(1)}) custom-call(s32[1]{0:T(128)S(6)} %copy.31.live_ref, s32[1024]{0:T(1024)S(1)} %copy-done.1, bf16[1024,2560]{1,0:T(8,128)(2,1)} %x_ref.9, bf16[1024,2560]{1,0:T(8,128)(2,1)} %z_ref.7, bf16[1024,128]{1,0:T(8,128)(2,1)} %c_ref.11, f32[40,1024]{1,0:T(8,128)S(1)} %get-tuple-element.25.g_ref, ...), custom_call_target="tpu_custom_call" | custom-call | flops 629145600 | bytes 5242880 | tf_op jit(solution)/shard_map/pallas_call | solution.py:458
  57.8 4.8 %shard_map.138 = (f32[1024,512]{1,0:T(8,128)S(1)}, bf16[1024,512]{1,0:T(8,128)(2,1)S(1)}) custom-call(s32[1]{0:T(128)S(6)} %copy.31.live_ref, s32[1024]{0:T(1024)S(1)} %copy-done.1, bf16[1024,2560]{1,0:T(8,128)(2,1)} %x_ref.9, bf16[1024,2560]{1,0:T(8,128)(2,1)} %z_ref.7, bf16[1024,128]{1,0:T(8,128)(2,1)} %c_ref.11, f32[40,1024]{1,0:T(8,128)S(1)} %get-tuple-element.25.g_ref, ...), custom_call_target="tpu_custom_call" | custom-call | flops 629145600 | bytes 5242880 | tf_op jit(solution)/shard_map/pallas_call | solution.py:458
  62.6 6.1 %shard_map.137 = (f32[1024,768]{1,0:T(8,128)S(1)}, bf16[1024,768]{1,0:T(8,128)(2,1)S(1)}) custom-call(s32[1]{0:T(128)S(6)} %copy.31.live_ref, s32[1024]{0:T(1024)S(1)} %copy-done.1, bf16[1024,2560]{1,0:T(8,128)(2,1)} %x_ref.9, bf16[1024,2560]{1,0:T(8,128)(2,1)} %z_ref.7, bf16[1024,128]{1,0:T(8,128)(2,1)} %c_ref.11, f32[40,1024]{1,0:T(8,128)S(1)} %get-tuple-element.25.g_ref, ...), custom_call_target="tpu_custom_call" | custom-call | flops 943718400 | bytes 7864320 | tf_op jit(solution)/shard_map/pallas_call | solution.py:458
  68.7 0.0 copy-start
  68.7 6.1 %shard_map.136 = (f32[1024,768]{1,0:T(8,128)S(1)}, bf16[1024,768]{1,0:T(8,128)(2,1)S(1)}) custom-call(s32[1]{0:T(128)S(6)} %copy.31.live_ref, s32[1024]{0:T(1024)S(1)} %copy-done.1, bf16[1024,2560]{1,0:T(8,128)(2,1)} %x_ref.9, bf16[1024,2560]{1,0:T(8,128)(2,1)} %z_ref.7, bf16[1024,128]{1,0:T(8,128)(2,1)} %c_ref.11, f32[40,1024]{1,0:T(8,128)S(1)} %get-tuple-element.25.g_ref, ...), custom_call_target="tpu_custom_call" | custom-call | flops 943718400 | bytes 7864320 | tf_op jit(solution)/shard_map/pallas_call | solution.py:458
  74.9 0.0 collective-permute-done.5.other_ref
  74.9 0.0 copy-done
  74.9 0.0 copy-start.2
  74.9 3.2 %join.1 = (f32[1024,2560]{1,0:T(8,128)S(1)}, f32[1,1024]{1,0:T(1,128)S(1)}) custom-call(s32[2]{0:T(128)S(1)} %pad_add_fusion.spot_ref, f32[20,64,128]{2,1,0:T(8,128)S(1)} %get-tuple-element.46.own_ref, f32[20,64,128]{2,1,0:T(8,128)S(1)} %collective-permute-done.5.other_ref, bf16[1024,128]{1,0:T(8,128)(2,1)S(1)} %copy-done, ...), custom_call_target="tpu_custom_call" | custom-call | tf_op jit(solution)/shard_map/join/pallas_call | solution.py:493
  78.1 1.3 %collective-permute-start.6 = (f32[1,1024]{1,0:T(1,128)S(1)}, f32[1,1024]{1,0:T(1,128)S(1)}, u32[]{:S(2)}, u32[]{:S(2)}) collective-permute-start(f32[1,1024]{1,0:T(1,128)S(1)} %get-tuple-element.39.square_ref), channel_id=1, source_target_pairs={{0,2},{2,0},{1,3},{3,1},{4,6},{6,4},{5,7},{7,5},{8,10},{10,8},{9,1... | collective-permute-start | bytes 12296 | tf_op jit(solution)/shard_map/ppermute | solution.py:534
  79.4 0.0 copy-done.2
  79.4 1.3 %collective-permute-done.6.more_ref = f32[1,1024]{1,0:T(1,128)S(1)} collective-permute-done((f32[1,1024]{1,0:T(1,128)S(1)}, f32[1,1024]{1,0:T(1,128)S(1)}, u32[]{:S(2)}, u32[]{:S(2)}) %collective-permute-start.6) | collective-permute-done | bytes 4128 | tf_op jit(solution)/shard_map/ppermute | solution.py:534
  80.7 3.5 %norm.1 = bf16[1024,2560]{1,0:T(8,128)(2,1)} custom-call(f32[1,1024]{1,0:T(1,128)S(1)} %get-tuple-element.39.square_ref, f32[1,1024]{1,0:T(1,128)S(1)} %collective-permute-done.6.more_ref, f32[1,2560]{1,0:T(1,128)S(1)} %reshape.78.gain_ref, f32[1024,2560]{1,0:T(8,128)S(1)} %get-tuple-element.40.gated_ref), custom_call_target="tpu_custom_call" | custom-call | tf_op jit(solution)/shard_map/norm/pallas_call | solution.py:507
  (24 shorter events, 0.3 us)
Async XLA Ops:
  8.1 2.6 %collective-permute-start = (f32[20,72,128]{2,1,0:T(8,128)S(1)}, f32[20,72,128]{2,1,0:T(8,128)S(1)}, u32[]{:S(2)}, u32[]{:S(2)}) collective-permute-start(f32[20,72,128]{2,1,0:T(8,128)S(1)} %get-tuple-element.24), channel_id=1, source_target_pairs={{0,1},{1,0},{2,3},{3,2},{4,5},{5,4},{6,7},{7,6},{8,9},{9,8},{10,11... | collective-permute-start | bytes 2211848 | tf_op jit(solution)/shard_map/ppermute | solution.py:543
  11.0 0.7 collective-permute-start.1
  11.9 19.2 %collective-permute-start.2 = (f32[648,128]{1,0:T(8,128)S(1)}, f32[648,128]{1,0:T(8,128)S(1)}, u32[]{:S(2)}, u32[]{:S(2)}) collective-permute-start(f32[648,128]{1,0:T(8,128)S(1)} %pad_maximum_fusion.2), channel_id=1, source_target_pairs={{0,4},{4,8},{1,5},{5,9},{2,6},{6,10},{3,7},{7,11},{16,20},{20,24},... | collective-permute-start | bytes 995336 | tf_op jit(solution)/shard_map/ppermute | solution.py:570
  31.3 9.4 %collective-permute-start.3 = (f32[648,128]{1,0:T(8,128)S(1)}, f32[648,128]{1,0:T(8,128)S(1)}, u32[]{:S(2)}, u32[]{:S(2)}) collective-permute-start(f32[648,128]{1,0:T(8,128)S(1)} %pad_maximum_fusion.1), channel_id=1, source_target_pairs={{4,8},{8,12},{5,9},{9,13},{6,10},{10,14},{7,11},{11,15},{20,24},{2... | collective-permute-start | bytes 995336 | tf_op jit(solution)/shard_map/ppermute | solution.py:570
  40.8 10.6 %copy-start.1 = (s32[1024]{0:T(1024)S(1)}, s32[1024]{0:T(1024)}, u32[]{:S(2)}) copy-start(s32[1024]{0:T(1024)} %docs_ref.11) | copy-start | bytes 12292
  40.9 7.0 %collective-permute-start.4 = (f32[648,128]{1,0:T(8,128)S(1)}, f32[648,128]{1,0:T(8,128)S(1)}, u32[]{:S(2)}, u32[]{:S(2)}) collective-permute-start(f32[648,128]{1,0:T(8,128)S(1)} %pad_maximum_fusion), channel_id=1, source_target_pairs={{8,12},{9,13},{10,14},{11,15},{24,28},{25,29},{26,30},{27,31}} | collective-permute-start | bytes 995336 | tf_op jit(solution)/shard_map/ppermute | solution.py:570
  48.2 26.7 %collective-permute-start.5 = (f32[20,64,128]{2,1,0:T(8,128)S(1)}, f32[20,64,128]{2,1,0:T(8,128)S(1)}, u32[]{:S(2)}, u32[]{:S(2)}) collective-permute-start(f32[20,64,128]{2,1,0:T(8,128)S(1)} %get-tuple-element.45), channel_id=1, source_target_pairs={{0,1},{1,0},{2,3},{3,2},{4,5},{5,4},{6,7},{7,6},{8,9},{9,8},{10,11... | collective-permute-start | bytes 1966088 | tf_op jit(solution)/shard_map/ppermute | solution.py:583
  68.7 6.2 %copy-start = (bf16[1024,128]{1,0:T(8,128)(2,1)S(1)}, bf16[1024,128]{1,0:T(8,128)(2,1)}, u32[]{:S(2)}) copy-start(bf16[1024,128]{1,0:T(8,128)(2,1)} %c_ref.11) | copy-start | bytes 786436
  74.9 4.5 %copy-start.2 = (f32[2560]{0:T(1024)S(1)}, f32[2560]{0:T(1024)}, u32[]{:S(2)}) copy-start(f32[2560]{0:T(1024)} %param.22) | copy-start | bytes 30724
  78.1 2.5 %collective-permute-start.6 = (f32[1,1024]{1,0:T(1,128)S(1)}, f32[1,1024]{1,0:T(1,128)S(1)}, u32[]{:S(2)}, u32[]{:S(2)}) collective-permute-start(f32[1,1024]{1,0:T(1,128)S(1)} %get-tuple-element.39.square_ref), channel_id=1, source_target_pairs={{0,2},{2,0},{1,3},{3,1},{4,6},{6,4},{5,7},{7,5},{8,10},{10,8},{9,1... | collective-permute-start | bytes 12296 | tf_op jit(solution)/shard_map/ppermute | solution.py:534

commit v6 on v5

--- a/solution.py
+++ b/solution.py
@@ -247,7 +247,7 @@
             z = z_ref[:, cols].astype(F32)
             gate = z / (1.0 + jnp.exp2(-LOG2E * z))
             y_ref[:, cols] = y * gate
-            f_ref[:, cols] = (enter * gate * passed[:, cols]).astype(BF16)
+            f_ref[:, cols] = enter * gate * passed[:, cols]
 
 
 def join_kernel(spot_ref, own_ref, other_ref, c_ref, *refs):
@@ -272,7 +272,7 @@
             for r in range(0, length, BLOCK):
                 rows = slice(r, r + BLOCK)
                 outer = dot(c_ref[rows, :], carry)
-                gated = y_ref[rows, c : c + wide] + f_ref[rows, c : c + wide].astype(F32) * outer
+                gated = y_ref[rows, c : c + wide] + f_ref[rows, c : c + wide] * outer
                 gated_ref[rows, tile * LANES : tile * LANES + wide] = gated
                 square = total[rows, :]
                 for j in range(0, wide, LANES):
@@ -287,17 +287,12 @@
     start = pl.multiple_of(pl.program_id(0) * rows, rows)
     row = lax.rsqrt((square_ref[...] + more_ref[...]) / channels_all + 1e-05)
     scale[...] = jnp.broadcast_to(row, (LANES, rows)).T
-
-    def strip(i, rest):
-        at = pl.multiple_of(i * 32, 32)
-        part = scale[pl.ds(at, 32), :]
+    for r in range(0, rows, 16):
+        part = scale[r : r + 16, :]
         for j in range(gated_ref.shape[1] // LANES):
             cols = slice(j * LANES, (j + 1) * LANES)
-            gated = gated_ref[pl.ds(start + at, 32), cols]
-            out_ref[pl.ds(at, 32), cols] = (gated * gain_ref[:, cols] * part).astype(BF16)
-        return rest
-
-    lax.fori_loop(0, rows // 32, strip, 0)
+            gated = gated_ref[pl.ds(start + r, 16), cols]
+            out_ref[r : r + 16, cols] = (gated * part * gain_ref[:, cols]).astype(BF16)
 
 
 def chunk_of(total, most):
@@ -475,7 +470,7 @@
             out_specs=[pl.BlockSpec((BLOCK, wide), lambda k: (k, 0))] * 2,
             out_shape=[
                 jax.ShapeDtypeStruct((length, wide), F32),
-                jax.ShapeDtypeStruct((length, wide), BF16),
+                jax.ShapeDtypeStruct((length, wide), F32),
             ],
             cost_estimate=pl.CostEstimate(
                 flops=length * wide * 1200,
@@ -506,16 +501,16 @@
     squares, more = summed(squares, "head")
     return pl.pallas_call(
         functools.partial(norm_kernel, channels * lax.axis_size("head")),
-        grid=(count,),
+        grid=(length // LANES,),
         in_specs=[
-            pl.BlockSpec((1, BLOCK), lambda k: (0, k)),
-            pl.BlockSpec((1, BLOCK), lambda k: (0, k)),
+            pl.BlockSpec((1, LANES), lambda k: (0, k)),
+            pl.BlockSpec((1, LANES), lambda k: (0, k)),
             whole((1, channels)),
             VMEM,
         ],
-        out_specs=pl.BlockSpec((BLOCK, channels), lambda k: (k, 0)),
+        out_specs=pl.BlockSpec((LANES, channels), lambda k: (k, 0)),
         out_shape=jax.ShapeDtypeStruct((length, channels), BF16),
-        scratch_shapes=[pltpu.VMEM((BLOCK, LANES), F32)],
+        scratch_shapes=[pltpu.VMEM((LANES, LANES), F32)],
         compiler_params=pltpu.CompilerParams(vmem_limit_bytes=16 << 20),
         name="norm",
     )(squares, more, norm_gain.reshape(1, channels), gated)

time: 84.6 us -> 85.2 us (level)
    pallas_call x1, Pallas kernels: 3.48 us -> 4.54 us  [on_device(): pl.pallas_call(functools.partial(norm_kernel, channels * lax.axis_size('h...]
where the time goes in v6:
time: 85.2 us; the launch traced here: 84.7 us
  Pallas kernels  38 us (45%)
  waiting for transfers between devices  33.2 us (39%)
  starting transfers between devices  11.4 us (13%)
  other arithmetic  0.97 us (1%)
  between operations  0.97 us (1%)
    ppermute x4, waiting for transfers between devices, carry_in(): got = lax.ppermute(send, 'seq', pairs)  30.1 us
    pallas_call x4, Pallas kernels, on_device(): pl.pallas_call(functools.partial(inner_kernel, width, at, group, count),...  21.8 us
    pallas_call x1, Pallas kernels, on_device(): pl.pallas_call(functools.partial(state_kernel, heads), grid=(channels //...  7.35 us
    ppermute x4, starting transfers between devices, carry_in(): got = lax.ppermute(send, 'seq', pairs)  6.11 us
    pallas_call x1, Pallas kernels, on_device(): pl.pallas_call(functools.partial(norm_kernel, channels * lax.axis_size('h...  4.54 us
    ppermute x1, starting transfers between devices, carry_in(): lax.ppermute(jnp.where(second, entering, onward), 'sub', [(0, 1), (1, 0)])  3.3 us
    pallas_call x1, Pallas kernels, on_device(): pl.pallas_call(join_kernel, in_specs=[SMEM] + [VMEM] * (3 + 2 * len(piece...  2.81 us
    ppermute x1, waiting for transfers between devices, carry_in(): got = lax.ppermute(sent, 'sub', [(0, 1), (1, 0)])  1.83 us
  transfers between devices with their start and end apart: 7, of which 5 were waited for; matrix products, arithmetic and copies ran while one was open for 0% of the time, Pallas kernels for 28%

profile of v6, /device:TPU:17, one launch (start us, length us, event | category | flops | bytes accessed | tf_op | source)
XLA Modules:
  0.0 84.7 jit_solution(17638104558163621409)
XLA Ops:
  0.7 0.1 pad_add_fusion.spot_ref
  0.7 7.3 %shard_state.1 = (f32[40,1024]{1,0:T(8,128)S(1)}, f32[1024,128]{1,0:T(8,128)S(1)}, bf16[4,128,2560]{2,1,0:T(8,128)(2,1)S(1)}, f32[20,72,128]{2,1,0:T(8,128)S(1)}...) custom-call(s32[1]{0:T(128)S(6)} %copy.31.live_ref, s32[1024]{0:T(1024)} %docs_ref.11, s32[2]{0:T(128)S(1)} %pad_add_fusion.spot_ref, ...), custom_call_target="tpu_custom_call" | custom-call | tf_op jit(solution)/shard_map/shard_state/pallas_call | solution.py:362
  8.1 0.7 collective-permute-start
  8.8 1.8 %collective-permute-done = f32[20,72,128]{2,1,0:T(8,128)S(1)} collective-permute-done((f32[20,72,128]{2,1,0:T(8,128)S(1)}, f32[20,72,128]{2,1,0:T(8,128)S(1)}, u32[]{:S(2)}, u32[]{:S(2)}) %collective-permute-start) | collective-permute-done | bytes 737312 | tf_op jit(solution)/shard_map/ppermute | solution.py:538
  10.7 0.1 broadcast_select_fusion
  10.9 0.1 slice_add_fusion
  11.0 0.7 collective-permute-start.1
  11.7 0.0 collective-permute-done.1
  11.8 0.1 select_add_fusion.2
  11.9 1.3 %collective-permute-start.2 = (f32[648,128]{1,0:T(8,128)S(1)}, f32[648,128]{1,0:T(8,128)S(1)}, u32[]{:S(2)}, u32[]{:S(2)}) collective-permute-start(f32[648,128]{1,0:T(8,128)S(1)} %pad_maximum_fusion.2), channel_id=1, source_target_pairs={{0,4},{4,8},{1,5},{5,9},{2,6},{6,10},{3,7},{7,11},{16,20},{20,24},... | collective-permute-start | bytes 995336 | tf_op jit(solution)/shard_map/ppermute | solution.py:565
  13.2 17.9 %collective-permute-done.2 = f32[648,128]{1,0:T(8,128)S(1)} collective-permute-done((f32[648,128]{1,0:T(8,128)S(1)}, f32[648,128]{1,0:T(8,128)S(1)}, u32[]{:S(2)}, u32[]{:S(2)}) %collective-permute-start.2) | collective-permute-done | bytes 331808 | tf_op jit(solution)/shard_map/ppermute | solution.py:565
  31.1 0.1 select_add_fusion.1
  31.2 1.9 %collective-permute-start.3 = (f32[648,128]{1,0:T(8,128)S(1)}, f32[648,128]{1,0:T(8,128)S(1)}, u32[]{:S(2)}, u32[]{:S(2)}) collective-permute-start(f32[648,128]{1,0:T(8,128)S(1)} %pad_maximum_fusion.1), channel_id=1, source_target_pairs={{4,8},{8,12},{5,9},{9,13},{6,10},{10,14},{7,11},{11,15},{20,24},{2... | collective-permute-start | bytes 995336 | tf_op jit(solution)/shard_map/ppermute | solution.py:565
  33.2 7.5 %collective-permute-done.3 = f32[648,128]{1,0:T(8,128)S(1)} collective-permute-done((f32[648,128]{1,0:T(8,128)S(1)}, f32[648,128]{1,0:T(8,128)S(1)}, u32[]{:S(2)}, u32[]{:S(2)}) %collective-permute-start.3) | collective-permute-done | bytes 331808 | tf_op jit(solution)/shard_map/ppermute | solution.py:565
  40.7 0.1 select_add_fusion
  40.8 0.0 copy-start.1
  40.8 2.2 %collective-permute-start.4 = (f32[648,128]{1,0:T(8,128)S(1)}, f32[648,128]{1,0:T(8,128)S(1)}, u32[]{:S(2)}, u32[]{:S(2)}) collective-permute-start(f32[648,128]{1,0:T(8,128)S(1)} %pad_maximum_fusion), channel_id=1, source_target_pairs={{8,12},{9,13},{10,14},{11,15},{24,28},{25,29},{26,30},{27,31}} | collective-permute-start | bytes 995336 | tf_op jit(solution)/shard_map/ppermute | solution.py:565
  43.0 4.7 %collective-permute-done.4 = f32[648,128]{1,0:T(8,128)S(1)} collective-permute-done((f32[648,128]{1,0:T(8,128)S(1)}, f32[648,128]{1,0:T(8,128)S(1)}, u32[]{:S(2)}, u32[]{:S(2)}) %collective-permute-start.4) | collective-permute-done | bytes 331808 | tf_op jit(solution)/shard_map/ppermute | solution.py:565
  47.8 0.1 select_select_fusion.1
  47.9 0.2 fusion
  48.1 3.3 %collective-permute-start.5 = (f32[20,64,128]{2,1,0:T(8,128)S(1)}, f32[20,64,128]{2,1,0:T(8,128)S(1)}, u32[]{:S(2)}, u32[]{:S(2)}) collective-permute-start(f32[20,64,128]{2,1,0:T(8,128)S(1)} %get-tuple-element.45), channel_id=1, source_target_pairs={{0,1},{1,0},{2,3},{3,2},{4,5},{5,4},{6,7},{7,6},{8,9},{9,8},{10,11... | collective-permute-start | bytes 1966088 | tf_op jit(solution)/shard_map/ppermute | solution.py:578
  51.4 0.0 copy-done.1
  51.4 1.6 %prepare.1 = (f32[4,256,256]{2,1,0:T(8,128)S(1)}, bf16[1024,256]{1,0:T(8,128)(2,1)S(1)}) custom-call(s32[1024]{0:T(1024)S(1)} %copy-done.1, bf16[1024,128]{1,0:T(8,128)(2,1)} %b_ref.3, bf16[1024,128]{1,0:T(8,128)(2,1)} %c_ref.11, f32[1024,128]{1,0:T(8,128)S(1)} %get-tuple-element.26.col_ref, s32[1,1024]{1,0:T(1,128)S(1)} %bitcast.75), custom_call_target="tpu_custom_call" | custom-call | tf_op jit(solution)/shard_map/prepare/pallas_call | solution.py:424
  53.0 4.8 %shard_map.139 = (f32[1024,512]{1,0:T(8,128)S(1)}, f32[1024,512]{1,0:T(8,128)S(1)}) custom-call(s32[1]{0:T(128)S(6)} %copy.31.live_ref, s32[1024]{0:T(1024)S(1)} %copy-done.1, bf16[1024,2560]{1,0:T(8,128)(2,1)} %x_ref.9, bf16[1024,2560]{1,0:T(8,128)(2,1)} %z_ref.7, bf16[1024,128]{1,0:T(8,128)(2,1)} %c_ref.11, f32[40,1024]{1,0:T(8,128)S(1)} %get-tuple-element.25.g_ref, ...), custom_call_target="tpu_custom_call" | custom-call | flops 629145600 | bytes 5242880 | tf_op jit(solution)/shard_map/pallas_call | solution.py:453
  57.8 4.8 %shard_map.138 = (f32[1024,512]{1,0:T(8,128)S(1)}, f32[1024,512]{1,0:T(8,128)S(1)}) custom-call(s32[1]{0:T(128)S(6)} %copy.31.live_ref, s32[1024]{0:T(1024)S(1)} %copy-done.1, bf16[1024,2560]{1,0:T(8,128)(2,1)} %x_ref.9, bf16[1024,2560]{1,0:T(8,128)(2,1)} %z_ref.7, bf16[1024,128]{1,0:T(8,128)(2,1)} %c_ref.11, f32[40,1024]{1,0:T(8,128)S(1)} %get-tuple-element.25.g_ref, ...), custom_call_target="tpu_custom_call" | custom-call | flops 629145600 | bytes 5242880 | tf_op jit(solution)/shard_map/pallas_call | solution.py:453
  62.6 6.1 %shard_map.137 = (f32[1024,768]{1,0:T(8,128)S(1)}, f32[1024,768]{1,0:T(8,128)S(1)}) custom-call(s32[1]{0:T(128)S(6)} %copy.31.live_ref, s32[1024]{0:T(1024)S(1)} %copy-done.1, bf16[1024,2560]{1,0:T(8,128)(2,1)} %x_ref.9, bf16[1024,2560]{1,0:T(8,128)(2,1)} %z_ref.7, bf16[1024,128]{1,0:T(8,128)(2,1)} %c_ref.11, f32[40,1024]{1,0:T(8,128)S(1)} %get-tuple-element.25.g_ref, ...), custom_call_target="tpu_custom_call" | custom-call | flops 943718400 | bytes 7864320 | tf_op jit(solution)/shard_map/pallas_call | solution.py:453
  68.7 0.0 copy-start
  68.7 6.1 %shard_map.136 = (f32[1024,768]{1,0:T(8,128)S(1)}, f32[1024,768]{1,0:T(8,128)S(1)}) custom-call(s32[1]{0:T(128)S(6)} %copy.31.live_ref, s32[1024]{0:T(1024)S(1)} %copy-done.1, bf16[1024,2560]{1,0:T(8,128)(2,1)} %x_ref.9, bf16[1024,2560]{1,0:T(8,128)(2,1)} %z_ref.7, bf16[1024,128]{1,0:T(8,128)(2,1)} %c_ref.11, f32[40,1024]{1,0:T(8,128)S(1)} %get-tuple-element.25.g_ref, ...), custom_call_target="tpu_custom_call" | custom-call | flops 943718400 | bytes 7864320 | tf_op jit(solution)/shard_map/pallas_call | solution.py:453
  74.8 0.0 collective-permute-done.5.other_ref
  74.8 0.0 copy-done
  74.8 0.0 copy-start.2
  74.9 2.8 %join.1 = (f32[1024,2560]{1,0:T(8,128)S(1)}, f32[1,1024]{1,0:T(1,128)S(1)}) custom-call(s32[2]{0:T(128)S(1)} %pad_add_fusion.spot_ref, f32[20,64,128]{2,1,0:T(8,128)S(1)} %get-tuple-element.46.own_ref, f32[20,64,128]{2,1,0:T(8,128)S(1)} %collective-permute-done.5.other_ref, bf16[1024,128]{1,0:T(8,128)(2,1)S(1)} %copy-done, ...), custom_call_target="tpu_custom_call" | custom-call | tf_op jit(solution)/shard_map/join/pallas_call | solution.py:488
  77.7 1.3 %collective-permute-start.6 = (f32[1,1024]{1,0:T(1,128)S(1)}, f32[1,1024]{1,0:T(1,128)S(1)}, u32[]{:S(2)}, u32[]{:S(2)}) collective-permute-start(f32[1,1024]{1,0:T(1,128)S(1)} %get-tuple-element.39.square_ref), channel_id=1, source_target_pairs={{0,2},{2,0},{1,3},{3,1},{4,6},{6,4},{5,7},{7,5},{8,10},{10,8},{9,1... | collective-permute-start | bytes 12296 | tf_op jit(solution)/shard_map/ppermute | solution.py:529
  78.9 0.0 copy-done.2
  78.9 1.3 %collective-permute-done.6.more_ref = f32[1,1024]{1,0:T(1,128)S(1)} collective-permute-done((f32[1,1024]{1,0:T(1,128)S(1)}, f32[1,1024]{1,0:T(1,128)S(1)}, u32[]{:S(2)}, u32[]{:S(2)}) %collective-permute-start.6) | collective-permute-done | bytes 4128 | tf_op jit(solution)/shard_map/ppermute | solution.py:529
  80.2 4.5 %norm.1 = bf16[1024,2560]{1,0:T(8,128)(2,1)} custom-call(f32[1,1024]{1,0:T(1,128)S(1)} %get-tuple-element.39.square_ref, f32[1,1024]{1,0:T(1,128)S(1)} %collective-permute-done.6.more_ref, f32[1,2560]{1,0:T(1,128)S(1)} %reshape.78.gain_ref, f32[1024,2560]{1,0:T(8,128)S(1)} %get-tuple-element.40.gated_ref), custom_call_target="tpu_custom_call" | custom-call | tf_op jit(solution)/shard_map/norm/pallas_call | solution.py:502
  (24 shorter events, 0.3 us)
Async XLA Ops:
  8.1 2.6 %collective-permute-start = (f32[20,72,128]{2,1,0:T(8,128)S(1)}, f32[20,72,128]{2,1,0:T(8,128)S(1)}, u32[]{:S(2)}, u32[]{:S(2)}) collective-permute-start(f32[20,72,128]{2,1,0:T(8,128)S(1)} %get-tuple-element.24), channel_id=1, source_target_pairs={{0,1},{1,0},{2,3},{3,2},{4,5},{5,4},{6,7},{7,6},{8,9},{9,8},{10,11... | collective-permute-start | bytes 2211848 | tf_op jit(solution)/shard_map/ppermute | solution.py:538
  11.0 0.7 collective-permute-start.1
  11.9 19.2 %collective-permute-start.2 = (f32[648,128]{1,0:T(8,128)S(1)}, f32[648,128]{1,0:T(8,128)S(1)}, u32[]{:S(2)}, u32[]{:S(2)}) collective-permute-start(f32[648,128]{1,0:T(8,128)S(1)} %pad_maximum_fusion.2), channel_id=1, source_target_pairs={{0,4},{4,8},{1,5},{5,9},{2,6},{6,10},{3,7},{7,11},{16,20},{20,24},... | collective-permute-start | bytes 995336 | tf_op jit(solution)/shard_map/ppermute | solution.py:565
  31.2 9.4 %collective-permute-start.3 = (f32[648,128]{1,0:T(8,128)S(1)}, f32[648,128]{1,0:T(8,128)S(1)}, u32[]{:S(2)}, u32[]{:S(2)}) collective-permute-start(f32[648,128]{1,0:T(8,128)S(1)} %pad_maximum_fusion.1), channel_id=1, source_target_pairs={{4,8},{8,12},{5,9},{9,13},{6,10},{10,14},{7,11},{11,15},{20,24},{2... | collective-permute-start | bytes 995336 | tf_op jit(solution)/shard_map/ppermute | solution.py:565
  40.8 10.6 %copy-start.1 = (s32[1024]{0:T(1024)S(1)}, s32[1024]{0:T(1024)}, u32[]{:S(2)}) copy-start(s32[1024]{0:T(1024)} %docs_ref.11) | copy-start | bytes 12292
  40.8 7.0 %collective-permute-start.4 = (f32[648,128]{1,0:T(8,128)S(1)}, f32[648,128]{1,0:T(8,128)S(1)}, u32[]{:S(2)}, u32[]{:S(2)}) collective-permute-start(f32[648,128]{1,0:T(8,128)S(1)} %pad_maximum_fusion), channel_id=1, source_target_pairs={{8,12},{9,13},{10,14},{11,15},{24,28},{25,29},{26,30},{27,31}} | collective-permute-start | bytes 995336 | tf_op jit(solution)/shard_map/ppermute | solution.py:565
  48.1 26.7 %collective-permute-start.5 = (f32[20,64,128]{2,1,0:T(8,128)S(1)}, f32[20,64,128]{2,1,0:T(8,128)S(1)}, u32[]{:S(2)}, u32[]{:S(2)}) collective-permute-start(f32[20,64,128]{2,1,0:T(8,128)S(1)} %get-tuple-element.45), channel_id=1, source_target_pairs={{0,1},{1,0},{2,3},{3,2},{4,5},{5,4},{6,7},{7,6},{8,9},{9,8},{10,11... | collective-permute-start | bytes 1966088 | tf_op jit(solution)/shard_map/ppermute | solution.py:578
  68.7 6.2 %copy-start = (bf16[1024,128]{1,0:T(8,128)(2,1)S(1)}, bf16[1024,128]{1,0:T(8,128)(2,1)}, u32[]{:S(2)}) copy-start(bf16[1024,128]{1,0:T(8,128)(2,1)} %c_ref.11) | copy-start | bytes 786436
  74.8 4.1 %copy-start.2 = (f32[2560]{0:T(1024)S(1)}, f32[2560]{0:T(1024)}, u32[]{:S(2)}) copy-start(f32[2560]{0:T(1024)} %param.22) | copy-start | bytes 30724
  77.7 2.5 %collective-permute-start.6 = (f32[1,1024]{1,0:T(1,128)S(1)}, f32[1,1024]{1,0:T(1,128)S(1)}, u32[]{:S(2)}, u32[]{:S(2)}) collective-permute-start(f32[1,1024]{1,0:T(1,128)S(1)} %get-tuple-element.39.square_ref), channel_id=1, source_target_pairs={{0,2},{2,0},{1,3},{3,1},{4,6},{6,4},{5,7},{7,5},{8,10},{10,8},{9,1... | collective-permute-start | bytes 12296 | tf_op jit(solution)/shard_map/ppermute | solution.py:529

commit v7 on v6

--- a/solution.py
+++ b/solution.py
@@ -12,7 +12,8 @@
 BLOCK = 256
 LANES = 128
 LOG2E = math.log2(math.e)
-INNER_VMEM = 24 << 20
+CHUNKS = 3
+INNER_VMEM = 16 << 20
 EARLY_VMEM = 32 << 20
 F32 = jnp.float32
 BF16 = jnp.bfloat16
@@ -282,17 +283,23 @@
     square_ref[...] = jnp.sum(total[...].T, axis=0, keepdims=True)
 
 
-def norm_kernel(channels_all, square_ref, more_ref, gain_ref, gated_ref, out_ref, scale):
+def gain_kernel(gain_ref, gated_ref, out_ref):
+    for r in range(0, gated_ref.shape[0], BLOCK):
+        for j in range(0, gated_ref.shape[1], LANES):
+            piece = (slice(r, r + BLOCK), slice(j, j + LANES))
+            out_ref[piece] = gated_ref[piece] * gain_ref[:, j : j + LANES]
+
+
+def norm_kernel(channels_all, square_ref, more_ref, gained_ref, out_ref, scale):
     rows = out_ref.shape[0]
     start = pl.multiple_of(pl.program_id(0) * rows, rows)
     row = lax.rsqrt((square_ref[...] + more_ref[...]) / channels_all + 1e-05)
     scale[...] = jnp.broadcast_to(row, (LANES, rows)).T
     for r in range(0, rows, 16):
         part = scale[r : r + 16, :]
-        for j in range(gated_ref.shape[1] // LANES):
-            cols = slice(j * LANES, (j + 1) * LANES)
-            gated = gated_ref[pl.ds(start + r, 16), cols]
-            out_ref[r : r + 16, cols] = (gated * part * gain_ref[:, cols]).astype(BF16)
+        for j in range(0, gained_ref.shape[1], LANES):
+            gained = gained_ref[pl.ds(start + r, 16), j : j + LANES]
+            out_ref[r : r + 16, j : j + LANES] = (gained * part).astype(BF16)
 
 
 def chunk_of(total, most):
@@ -315,11 +322,11 @@
 
 
 def plan(chips, tiles):
-    chunks = 2 if tiles % 2 == 0 else 1
-    pieces = (tiles,)
-    if tiles % 10 == 0:
-        pieces = (3 * tiles // 10,) * 2 + (tiles // 5,) * 2
-    return chunks, chunks + chips - 2, pieces
+    chunks = min(CHUNKS, tiles)
+    size = -(-tiles // chunks)
+    starts = tuple(min(c * size, tiles - size) for c in range(chunks))
+    pieces = (tiles // 5,) * 5 if tiles % 10 == 0 else (tiles,)
+    return starts, size, chunks + chips - 2, pieces
 
 
 def on_device(
@@ -443,7 +450,7 @@
         name="prepare",
     )(document_ids, *in_hbm(state_input, state_readout), col, doc_row)
 
-    pieces = plan(lax.axis_size("seq"), tiles)[2]
+    pieces = plan(lax.axis_size("seq"), tiles)[3]
     group = 2 if tiles % 2 == 0 else 1
     ys, fs, at = [], [], 0
     x, z, readout, heads_hot = in_hbm(token_values, gate_values, state_readout, hot)
@@ -499,21 +506,29 @@
     )(spot, own, other, state_readout, *ys, *fs)
 
     squares, more = summed(squares, "head")
+    gained = pl.pallas_call(
+        gain_kernel,
+        in_specs=[VMEM, VMEM],
+        out_specs=VMEM,
+        out_shape=jax.ShapeDtypeStruct((length, channels), F32),
+        input_output_aliases={1: 0},
+        compiler_params=pltpu.CompilerParams(vmem_limit_bytes=16 << 20),
+        name="gain",
+    )(norm_gain.reshape(1, channels), gated)
     return pl.pallas_call(
         functools.partial(norm_kernel, channels * lax.axis_size("head")),
-        grid=(length // LANES,),
+        grid=(count,),
         in_specs=[
-            pl.BlockSpec((1, LANES), lambda k: (0, k)),
-            pl.BlockSpec((1, LANES), lambda k: (0, k)),
-            whole((1, channels)),
+            pl.BlockSpec((1, BLOCK), lambda k: (0, k)),
+            pl.BlockSpec((1, BLOCK), lambda k: (0, k)),
             VMEM,
         ],
-        out_specs=pl.BlockSpec((LANES, channels), lambda k: (k, 0)),
+        out_specs=pl.BlockSpec((BLOCK, channels), lambda k: (k, 0)),
         out_shape=jax.ShapeDtypeStruct((length, channels), BF16),
-        scratch_shapes=[pltpu.VMEM((LANES, LANES), F32)],
+        scratch_shapes=[pltpu.VMEM((BLOCK, LANES), F32)],
         compiler_params=pltpu.CompilerParams(vmem_limit_bytes=16 << 20),
         name="norm",
-    )(squares, more, norm_gain.reshape(1, channels), gated)
+    )(squares, more, gained)
 
 
 def summed(value, axis):
@@ -545,15 +560,14 @@
     chip_state = late_decay * early + late
     chip_decay = late_decay * early_decay
 
-    chunks, hops = plan(chips, tiles)[:2]
-    size = tiles // chunks
+    starts, size, hops, _ = plan(chips, tiles)
     rows = size * half
     tail = jnp.broadcast_to(last, (8, LANES))
 
     def at(array, t):
-        part = array[:size]
-        for c in range(1, chunks):
-            part = jnp.where(place <= t - c, array[c * size : (c + 1) * size], part)
+        part = array[starts[0] : starts[0] + size]
+        for c in range(1, len(starts)):
+            part = jnp.where(place <= t - c, array[starts[c] : starts[c] + size], part)
         return part
 
     carry = jnp.zeros((size, half, LANES), F32)
@@ -561,17 +575,18 @@
     for t in range(hops):
         send = at(chip_decay, t) * carry + at(chip_state, t)
         send = jnp.concatenate([send.reshape(rows, LANES), tail], axis=0)
-        pairs = [(z, z + 1) for z in range(chips - 1) if 0 <= t - z < chunks]
+        pairs = [(z, z + 1) for z in range(chips - 1) if 0 <= t - z < len(starts)]
         got = lax.ppermute(send, "seq", pairs)
         joined = jnp.where(got[rows] == first, 1.0, 0.0)
         carry = joined * got[:rows].reshape(size, half, LANES)
         received.append(carry)
-    parts = []
-    for c in range(chunks):
+    parts, done = [], 0
+    for c, start in enumerate(starts):
         part = jnp.zeros((size, half, LANES), F32)
         for z in range(1, chips):
             part = jnp.where(place == z, received[c + z - 1], part)
-        parts.append(part)
+        parts.append(part[done - start :])
+        done = start + size
     entering = jnp.concatenate(parts, axis=0)
     onward = link * (early_decay * entering + early)
     mine = jnp.where(second, onward, entering)

time: 85.2 us -> 87.1 us (1.022)
  waiting for transfers between devices: 33.2 us -> 28.3 us
  starting transfers between devices: 11.4 us -> 15 us
  Pallas kernels: 38 us -> 41 us
    ppermute x4 -> x5, waiting for transfers between devices: 30.1 us -> 26.4 us  [carry_in(): got = lax.ppermute(send, 'seq', pairs)]
    ppermute x4 -> x5, starting transfers between devices: 6.11 us -> 8.48 us  [carry_in(): got = lax.ppermute(send, 'seq', pairs)]
    pallas_call x0 -> x1, Pallas kernels: none -> 2.25 us  [on_device(): pl.pallas_call(gain_kernel, in_specs=[VMEM, VMEM], out_specs=VMEM, out_sh...]
    pallas_call x4 -> x5, Pallas kernels: 21.8 us -> 23.9 us  [on_device(): pl.pallas_call(functools.partial(inner_kernel, width, at, group, count),...]
    pallas_call x1, Pallas kernels: 4.54 us -> 3.15 us  [on_device(): pl.pallas_call(functools.partial(norm_kernel, channels * lax.axis_size('h...]
    ppermute x1, waiting for transfers between devices: 1.25 us -> 0.01 us  [summed(): more = lax.ppermute(value, axis, [(i, i ^ shift) for i in range(size)])]
    ppermute x1, starting transfers between devices: 3.3 us -> 4.45 us  [carry_in(): lax.ppermute(jnp.where(second, entering, onward), 'sub', [(0, 1), (1, 0)])]
  transfers between devices with their start and end apart: 7 -> 8, of which waited for: 5 -> 5; matrix products, arithmetic and copies ran while one was open for 0% -> 0% of each run, Pallas kernels for 28% -> 32%
where the time goes in v7:
time: 87.1 us; the launch traced here: 86.5 us
  Pallas kernels  41 us (47%)
  waiting for transfers between devices  28.3 us (32%)
  starting transfers between devices  15 us (17%)
  other arithmetic  1.06 us (1%)
  between operations  1.04 us (1%)
    ppermute x5, waiting for transfers between devices, carry_in(): got = lax.ppermute(send, 'seq', pairs)  26.4 us
    pallas_call x5, Pallas kernels, on_device(): pl.pallas_call(functools.partial(inner_kernel, width, at, group, count),...  23.9 us
    ppermute x5, starting transfers between devices, carry_in(): got = lax.ppermute(send, 'seq', pairs)  8.48 us
    pallas_call x1, Pallas kernels, on_device(): pl.pallas_call(functools.partial(state_kernel, heads), grid=(channels //...  7.33 us
    ppermute x1, starting transfers between devices, carry_in(): lax.ppermute(jnp.where(second, entering, onward), 'sub', [(0, 1), (1, 0)])  4.45 us
    pallas_call x1, Pallas kernels, on_device(): pl.pallas_call(functools.partial(norm_kernel, channels * lax.axis_size('h...  3.15 us
    pallas_call x1, Pallas kernels, on_device(): pl.pallas_call(join_kernel, in_specs=[SMEM] + [VMEM] * (3 + 2 * len(piece...  2.8 us
    pallas_call x1, Pallas kernels, on_device(): pl.pallas_call(gain_kernel, in_specs=[VMEM, VMEM], out_specs=VMEM, out_sh...  2.25 us
  transfers between devices with their start and end apart: 8, of which 5 were waited for; matrix products, arithmetic and copies ran while one was open for 0% of the time, Pallas kernels for 32%

profile of v7, /device:TPU:17, one launch (start us, length us, event | category | flops | bytes accessed | tf_op | source)
XLA Modules:
  0.0 86.5 jit_solution(10808717656911171805)
XLA Ops:
  0.7 0.1 pad_add_fusion.spot_ref
  0.7 7.3 %shard_state.1 = (f32[40,1024]{1,0:T(8,128)S(1)}, f32[1024,128]{1,0:T(8,128)S(1)}, bf16[4,128,2560]{2,1,0:T(8,128)(2,1)S(1)}, f32[20,72,128]{2,1,0:T(8,128)S(1)}...) custom-call(s32[1]{0:T(128)S(6)} %copy.36.live_ref, s32[1024]{0:T(1024)} %docs_ref.13, s32[2]{0:T(128)S(1)} %pad_add_fusion.spot_ref, ...), custom_call_target="tpu_custom_call" | custom-call | tf_op jit(solution)/shard_map/shard_state/pallas_call | solution.py:369
  8.1 0.7 collective-permute-start
  8.8 1.8 %collective-permute-done = f32[20,72,128]{2,1,0:T(8,128)S(1)} collective-permute-done((f32[20,72,128]{2,1,0:T(8,128)S(1)}, f32[20,72,128]{2,1,0:T(8,128)S(1)}, u32[]{:S(2)}, u32[]{:S(2)}) %collective-permute-start) | collective-permute-done | bytes 737312 | tf_op jit(solution)/shard_map/ppermute | solution.py:553
  10.6 0.1 broadcast_select_fusion
  10.8 0.1 slice_add_fusion
  11.0 0.7 collective-permute-start.1
  11.7 0.0 collective-permute-done.1
  11.8 0.1 select_add_fusion.3
  11.9 1.3 %collective-permute-start.2 = (f32[456,128]{1,0:T(8,128)S(1)}, f32[456,128]{1,0:T(8,128)S(1)}, u32[]{:S(2)}, u32[]{:S(2)}) collective-permute-start(f32[456,128]{1,0:T(8,128)S(1)} %pad_maximum_fusion.4), channel_id=1, source_target_pairs={{0,4},{4,8},{1,5},{5,9},{2,6},{6,10},{3,7},{7,11},{16,20},{20,24},... | collective-permute-start | bytes 700424 | tf_op jit(solution)/shard_map/ppermute | solution.py:579
  13.2 13.6 %collective-permute-done.2 = f32[456,128]{1,0:T(8,128)S(1)} collective-permute-done((f32[456,128]{1,0:T(8,128)S(1)}, f32[456,128]{1,0:T(8,128)S(1)}, u32[]{:S(2)}, u32[]{:S(2)}) %collective-permute-start.2) | collective-permute-done | bytes 233504 | tf_op jit(solution)/shard_map/ppermute | solution.py:579
  26.8 0.1 select_add_fusion.2
  26.9 1.9 %collective-permute-start.3 = (f32[456,128]{1,0:T(8,128)S(1)}, f32[456,128]{1,0:T(8,128)S(1)}, u32[]{:S(2)}, u32[]{:S(2)}) collective-permute-start(f32[456,128]{1,0:T(8,128)S(1)} %pad_maximum_fusion.3), channel_id=1, source_target_pairs={{0,4},{4,8},{8,12},{1,5},{5,9},{9,13},{2,6},{6,10},{10,14},{3,7},{... | collective-permute-start | bytes 700424 | tf_op jit(solution)/shard_map/ppermute | solution.py:579
  28.9 5.4 %collective-permute-done.3 = f32[456,128]{1,0:T(8,128)S(1)} collective-permute-done((f32[456,128]{1,0:T(8,128)S(1)}, f32[456,128]{1,0:T(8,128)S(1)}, u32[]{:S(2)}, u32[]{:S(2)}) %collective-permute-start.3) | collective-permute-done | bytes 233504 | tf_op jit(solution)/shard_map/ppermute | solution.py:579
  34.3 0.1 select_select_fusion.1
  34.4 0.1 select_add_fusion.1
  34.5 2.2 %collective-permute-start.4 = (f32[456,128]{1,0:T(8,128)S(1)}, f32[456,128]{1,0:T(8,128)S(1)}, u32[]{:S(2)}, u32[]{:S(2)}) collective-permute-start(f32[456,128]{1,0:T(8,128)S(1)} %pad_maximum_fusion.2), channel_id=1, source_target_pairs={{4,8},{8,12},{5,9},{9,13},{6,10},{10,14},{7,11},{11,15},{20,24},{2... | collective-permute-start | bytes 700424 | tf_op jit(solution)/shard_map/ppermute | solution.py:579
  36.7 4.6 %collective-permute-done.4 = f32[456,128]{1,0:T(8,128)S(1)} collective-permute-done((f32[456,128]{1,0:T(8,128)S(1)}, f32[456,128]{1,0:T(8,128)S(1)}, u32[]{:S(2)}, u32[]{:S(2)}) %collective-permute-start.4) | collective-permute-done | bytes 233504 | tf_op jit(solution)/shard_map/ppermute | solution.py:579
  41.3 0.1 select_select_fusion
  41.4 0.1 select_add_fusion
  41.4 0.0 copy-start.1
  41.5 2.4 %collective-permute-start.5 = (f32[456,128]{1,0:T(8,128)S(1)}, f32[456,128]{1,0:T(8,128)S(1)}, u32[]{:S(2)}, u32[]{:S(2)}) collective-permute-start(f32[456,128]{1,0:T(8,128)S(1)} %pad_maximum_fusion.1), channel_id=1, source_target_pairs={{8,12},{9,13},{10,14},{11,15},{24,28},{25,29},{26,30},{27,31}} | collective-permute-start | bytes 700424 | tf_op jit(solution)/shard_map/ppermute | solution.py:579
  43.9 2.8 %collective-permute-done.5 = f32[456,128]{1,0:T(8,128)S(1)} collective-permute-done((f32[456,128]{1,0:T(8,128)S(1)}, f32[456,128]{1,0:T(8,128)S(1)}, u32[]{:S(2)}, u32[]{:S(2)}) %collective-permute-start.5) | collective-permute-done | bytes 233504 | tf_op jit(solution)/shard_map/ppermute | solution.py:579
  46.7 0.2 fusion
  46.9 4.4 %collective-permute-start.6 = (f32[20,64,128]{2,1,0:T(8,128)S(1)}, f32[20,64,128]{2,1,0:T(8,128)S(1)}, u32[]{:S(2)}, u32[]{:S(2)}) collective-permute-start(f32[20,64,128]{2,1,0:T(8,128)S(1)} %get-tuple-element.53), channel_id=1, source_target_pairs={{0,1},{1,0},{2,3},{3,2},{4,5},{5,4},{6,7},{7,6},{8,9},{9,8},{10,11... | collective-permute-start | bytes 1966088 | tf_op jit(solution)/shard_map/ppermute | solution.py:593
  51.3 0.0 copy-done.1
  51.4 1.6 %prepare.1 = (f32[4,256,256]{2,1,0:T(8,128)S(1)}, bf16[1024,256]{1,0:T(8,128)(2,1)S(1)}) custom-call(s32[1024]{0:T(1024)S(1)} %copy-done.1, bf16[1024,128]{1,0:T(8,128)(2,1)} %b_ref.3, bf16[1024,128]{1,0:T(8,128)(2,1)} %c_ref.13, f32[1024,128]{1,0:T(8,128)S(1)} %get-tuple-element.28.col_ref, s32[1,1024]{1,0:T(1,128)S(1)} %bitcast.90), custom_call_target="tpu_custom_call" | custom-call | tf_op jit(solution)/shard_map/prepare/pallas_call | solution.py:431
  52.9 4.8 %shard_map.140 = (f32[1024,512]{1,0:T(8,128)S(1)}, f32[1024,512]{1,0:T(8,128)S(1)}) custom-call(s32[1]{0:T(128)S(6)} %copy.36.live_ref, s32[1024]{0:T(1024)S(1)} %copy-done.1, bf16[1024,2560]{1,0:T(8,128)(2,1)} %x_ref.11, bf16[1024,2560]{1,0:T(8,128)(2,1)} %z_ref.9, bf16[1024,128]{1,0:T(8,128)(2,1)} %c_ref.13, f32[40,1024]{1,0:T(8,128)S(1)} %get-tuple-element.27.g_ref, ...), custom_call_target="tpu_custom_call" | custom-call | flops 629145600 | bytes 5242880 | tf_op jit(solution)/shard_map/pallas_call | solution.py:460
  57.7 4.8 %shard_map.139 = (f32[1024,512]{1,0:T(8,128)S(1)}, f32[1024,512]{1,0:T(8,128)S(1)}) custom-call(s32[1]{0:T(128)S(6)} %copy.36.live_ref, s32[1024]{0:T(1024)S(1)} %copy-done.1, bf16[1024,2560]{1,0:T(8,128)(2,1)} %x_ref.11, bf16[1024,2560]{1,0:T(8,128)(2,1)} %z_ref.9, bf16[1024,128]{1,0:T(8,128)(2,1)} %c_ref.13, f32[40,1024]{1,0:T(8,128)S(1)} %get-tuple-element.27.g_ref, ...), custom_call_target="tpu_custom_call" | custom-call | flops 629145600 | bytes 5242880 | tf_op jit(solution)/shard_map/pallas_call | solution.py:460
  62.5 4.8 %shard_map.138 = (f32[1024,512]{1,0:T(8,128)S(1)}, f32[1024,512]{1,0:T(8,128)S(1)}) custom-call(s32[1]{0:T(128)S(6)} %copy.36.live_ref, s32[1024]{0:T(1024)S(1)} %copy-done.1, bf16[1024,2560]{1,0:T(8,128)(2,1)} %x_ref.11, bf16[1024,2560]{1,0:T(8,128)(2,1)} %z_ref.9, bf16[1024,128]{1,0:T(8,128)(2,1)} %c_ref.13, f32[40,1024]{1,0:T(8,128)S(1)} %get-tuple-element.27.g_ref, ...), custom_call_target="tpu_custom_call" | custom-call | flops 629145600 | bytes 5242880 | tf_op jit(solution)/shard_map/pallas_call | solution.py:460
  67.3 4.8 %shard_map.137 = (f32[1024,512]{1,0:T(8,128)S(1)}, f32[1024,512]{1,0:T(8,128)S(1)}) custom-call(s32[1]{0:T(128)S(6)} %copy.36.live_ref, s32[1024]{0:T(1024)S(1)} %copy-done.1, bf16[1024,2560]{1,0:T(8,128)(2,1)} %x_ref.11, bf16[1024,2560]{1,0:T(8,128)(2,1)} %z_ref.9, bf16[1024,128]{1,0:T(8,128)(2,1)} %c_ref.13, f32[40,1024]{1,0:T(8,128)S(1)} %get-tuple-element.27.g_ref, ...), custom_call_target="tpu_custom_call" | custom-call | flops 629145600 | bytes 5242880 | tf_op jit(solution)/shard_map/pallas_call | solution.py:460
  72.1 0.0 copy-start
  72.1 4.8 %shard_map.136 = (f32[1024,512]{1,0:T(8,128)S(1)}, f32[1024,512]{1,0:T(8,128)S(1)}) custom-call(s32[1]{0:T(128)S(6)} %copy.36.live_ref, s32[1024]{0:T(1024)S(1)} %copy-done.1, bf16[1024,2560]{1,0:T(8,128)(2,1)} %x_ref.11, bf16[1024,2560]{1,0:T(8,128)(2,1)} %z_ref.9, bf16[1024,128]{1,0:T(8,128)(2,1)} %c_ref.13, f32[40,1024]{1,0:T(8,128)S(1)} %get-tuple-element.27.g_ref, ...), custom_call_target="tpu_custom_call" | custom-call | flops 629145600 | bytes 5242880 | tf_op jit(solution)/shard_map/pallas_call | solution.py:460
  76.9 0.0 collective-permute-done.6.other_ref
  76.9 0.0 copy-done
  76.9 0.0 copy-start.2
  76.9 2.8 %join.1 = (f32[1024,2560]{1,0:T(8,128)S(1)}, f32[1,1024]{1,0:T(1,128)S(1)}) custom-call(s32[2]{0:T(128)S(1)} %pad_add_fusion.spot_ref, f32[20,64,128]{2,1,0:T(8,128)S(1)} %get-tuple-element.54.own_ref, f32[20,64,128]{2,1,0:T(8,128)S(1)} %collective-permute-done.6.other_ref, bf16[1024,128]{1,0:T(8,128)(2,1)S(1)} %copy-done, ...), custom_call_target="tpu_custom_call" | custom-call | tf_op jit(solution)/shard_map/join/pallas_call | solution.py:495
  79.7 1.3 %collective-permute-start.7 = (f32[1,1024]{1,0:T(1,128)S(1)}, f32[1,1024]{1,0:T(1,128)S(1)}, u32[]{:S(2)}, u32[]{:S(2)}) collective-permute-start(f32[1,1024]{1,0:T(1,128)S(1)} %get-tuple-element.43.square_ref), channel_id=1, source_target_pairs={{0,2},{2,0},{1,3},{3,1},{4,6},{6,4},{5,7},{7,5},{8,10},{10,8},{9,1... | collective-permute-start | bytes 12296 | tf_op jit(solution)/shard_map/ppermute | solution.py:544
  81.0 0.0 copy-done.2
  81.0 2.3 %gain.1.gained_ref = f32[1024,2560]{1,0:T(8,128)S(1)} custom-call(f32[1,2560]{1,0:T(1,128)S(1)} %reshape.91.gain_ref, f32[1024,2560]{1,0:T(8,128)S(1)} %get-tuple-element.44.gated_ref), custom_call_target="tpu_custom_call", output_to_operand_aliasing={{}: (1, {})} | custom-call | tf_op jit(solution)/shard_map/gain/pallas_call | solution.py:509
  83.3 0.0 collective-permute-done.7.more_ref
  83.3 3.2 %norm.1 = bf16[1024,2560]{1,0:T(8,128)(2,1)} custom-call(f32[1,1024]{1,0:T(1,128)S(1)} %get-tuple-element.43.square_ref, f32[1,1024]{1,0:T(1,128)S(1)} %collective-permute-done.7.more_ref, f32[1024,2560]{1,0:T(8,128)S(1)} %gain.1.gained_ref), custom_call_target="tpu_custom_call" | custom-call | tf_op jit(solution)/shard_map/norm/pallas_call | solution.py:518
  (30 shorter events, 0.4 us)
Async XLA Ops:
  8.1 2.6 %collective-permute-start = (f32[20,72,128]{2,1,0:T(8,128)S(1)}, f32[20,72,128]{2,1,0:T(8,128)S(1)}, u32[]{:S(2)}, u32[]{:S(2)}) collective-permute-start(f32[20,72,128]{2,1,0:T(8,128)S(1)} %get-tuple-element.26), channel_id=1, source_target_pairs={{0,1},{1,0},{2,3},{3,2},{4,5},{5,4},{6,7},{7,6},{8,9},{9,8},{10,11... | collective-permute-start | bytes 2211848 | tf_op jit(solution)/shard_map/ppermute | solution.py:553
  11.0 0.7 collective-permute-start.1
  11.9 14.9 %collective-permute-start.2 = (f32[456,128]{1,0:T(8,128)S(1)}, f32[456,128]{1,0:T(8,128)S(1)}, u32[]{:S(2)}, u32[]{:S(2)}) collective-permute-start(f32[456,128]{1,0:T(8,128)S(1)} %pad_maximum_fusion.4), channel_id=1, source_target_pairs={{0,4},{4,8},{1,5},{5,9},{2,6},{6,10},{3,7},{7,11},{16,20},{20,24},... | collective-permute-start | bytes 700424 | tf_op jit(solution)/shard_map/ppermute | solution.py:579
  26.9 7.3 %collective-permute-start.3 = (f32[456,128]{1,0:T(8,128)S(1)}, f32[456,128]{1,0:T(8,128)S(1)}, u32[]{:S(2)}, u32[]{:S(2)}) collective-permute-start(f32[456,128]{1,0:T(8,128)S(1)} %pad_maximum_fusion.3), channel_id=1, source_target_pairs={{0,4},{4,8},{8,12},{1,5},{5,9},{9,13},{2,6},{6,10},{10,14},{3,7},{... | collective-permute-start | bytes 700424 | tf_op jit(solution)/shard_map/ppermute | solution.py:579
  34.5 6.8 %collective-permute-start.4 = (f32[456,128]{1,0:T(8,128)S(1)}, f32[456,128]{1,0:T(8,128)S(1)}, u32[]{:S(2)}, u32[]{:S(2)}) collective-permute-start(f32[456,128]{1,0:T(8,128)S(1)} %pad_maximum_fusion.2), channel_id=1, source_target_pairs={{4,8},{8,12},{5,9},{9,13},{6,10},{10,14},{7,11},{11,15},{20,24},{2... | collective-permute-start | bytes 700424 | tf_op jit(solution)/shard_map/ppermute | solution.py:579
  41.4 9.9 %copy-start.1 = (s32[1024]{0:T(1024)S(1)}, s32[1024]{0:T(1024)}, u32[]{:S(2)}) copy-start(s32[1024]{0:T(1024)} %docs_ref.13) | copy-start | bytes 12292
  41.5 5.2 %collective-permute-start.5 = (f32[456,128]{1,0:T(8,128)S(1)}, f32[456,128]{1,0:T(8,128)S(1)}, u32[]{:S(2)}, u32[]{:S(2)}) collective-permute-start(f32[456,128]{1,0:T(8,128)S(1)} %pad_maximum_fusion.1), channel_id=1, source_target_pairs={{8,12},{9,13},{10,14},{11,15},{24,28},{25,29},{26,30},{27,31}} | collective-permute-start | bytes 700424 | tf_op jit(solution)/shard_map/ppermute | solution.py:579
  46.9 30.0 %collective-permute-start.6 = (f32[20,64,128]{2,1,0:T(8,128)S(1)}, f32[20,64,128]{2,1,0:T(8,128)S(1)}, u32[]{:S(2)}, u32[]{:S(2)}) collective-permute-start(f32[20,64,128]{2,1,0:T(8,128)S(1)} %get-tuple-element.53), channel_id=1, source_target_pairs={{0,1},{1,0},{2,3},{3,2},{4,5},{5,4},{6,7},{7,6},{8,9},{9,8},{10,11... | collective-permute-start | bytes 1966088 | tf_op jit(solution)/shard_map/ppermute | solution.py:593
  72.1 4.8 %copy-start = (bf16[1024,128]{1,0:T(8,128)(2,1)S(1)}, bf16[1024,128]{1,0:T(8,128)(2,1)}, u32[]{:S(2)}) copy-start(bf16[1024,128]{1,0:T(8,128)(2,1)} %c_ref.13) | copy-start | bytes 786436
  76.9 4.1 %copy-start.2 = (f32[2560]{0:T(1024)S(1)}, f32[2560]{0:T(1024)}, u32[]{:S(2)}) copy-start(f32[2560]{0:T(1024)} %param.22) | copy-start | bytes 30724
  79.7 3.6 %collective-permute-start.7 = (f32[1,1024]{1,0:T(1,128)S(1)}, f32[1,1024]{1,0:T(1,128)S(1)}, u32[]{:S(2)}, u32[]{:S(2)}) collective-permute-start(f32[1,1024]{1,0:T(1,128)S(1)} %get-tuple-element.43.square_ref), channel_id=1, source_target_pairs={{0,2},{2,0},{1,3},{3,1},{4,6},{6,4},{5,7},{7,5},{8,10},{10,8},{9,1... | collective-permute-start | bytes 12296 | tf_op jit(solution)/shard_map/ppermute | solution.py:544

commit v8 on v7

--- a/solution.py
+++ b/solution.py
@@ -12,7 +12,7 @@
 BLOCK = 256
 LANES = 128
 LOG2E = math.log2(math.e)
-CHUNKS = 3
+CHUNKS = 2
 INNER_VMEM = 16 << 20
 EARLY_VMEM = 32 << 20
 F32 = jnp.float32
@@ -61,7 +61,8 @@
     hot_low_ref,
     x_ref,
     b_ref,
-    g_ref,
+    cum_ref,
+    step_ref,
     col_ref,
     enter_ref,
     own_ref,
@@ -93,11 +94,11 @@
         high, _ = two_parts(rate)
         middle, low = two_parts(rate - high.astype(F32))
         tri = tri_ref[...]
-        logs = jnp.where(step > 0.0, LOG2E * jnp.log(step), -1e30)
+        step_ref[...] = step
         for j in range(count):
             piece = slice(j * BLOCK, (j + 1) * BLOCK)
             cum = dot(high[:, piece], tri) + (dot(middle[:, piece], tri) + dot(low[:, piece], tri))
-            g_ref[:, piece] = cum - logs[:, piece]
+            cum_ref[:, piece] = cum
             same = doc_row_ref[:, piece] == ends[j]
             pack[0:rows, piece] = cum
             pack[rows : 2 * rows, piece] = jnp.where(
@@ -186,7 +187,8 @@
     x_ref,
     z_ref,
     c_ref,
-    g_ref,
+    cum_ref,
+    step_ref,
     col_ref,
     affinity_ref,
     entry_ref,
@@ -221,13 +223,14 @@
                 for i in range(per_tile):
                     h = (first_tile + q * group + u) * per_tile + i
                     cum = jnp.broadcast_to(col_ref[:, h : h + 1], (BLOCK, LANES))
-                    left, right = g_ref[h : h + 1, :half], g_ref[h : h + 1, half:]
-                    top = jnp.exp2(jnp.minimum(cum[:half] - left, 64.0))
-                    bottom = jnp.exp2(cum[half:] - left)
-                    corner = jnp.exp2(jnp.minimum(cum[half:] - right, 64.0))
-                    tops.append((top * affinity_ref[0, :half, :half]).astype(BF16))
-                    bottoms.append((bottom * affinity_ref[0, half:, :half]).astype(BF16))
-                    bottoms.append((corner * affinity_ref[0, half:, half:]).astype(BF16))
+                    left, right = cum_ref[h : h + 1, :half], cum_ref[h : h + 1, half:]
+                    early, late = step_ref[h : h + 1, :half], step_ref[h : h + 1, half:]
+                    top = jnp.exp2(jnp.minimum(cum[:half] - left, 0.0))
+                    bottom = jnp.exp2(jnp.minimum(cum[half:] - left, 0.0))
+                    corner = jnp.exp2(jnp.minimum(cum[half:] - right, 0.0))
+                    tops.append((affinity_ref[0, :half, :half] * top * early).astype(BF16))
+                    bottoms.append((affinity_ref[0, half:, :half] * bottom * early).astype(BF16))
+                    bottoms.append((affinity_ref[0, half:, half:] * corner * late).astype(BF16))
                     mine = (lane >= i * width) & (lane < (i + 1) * width)
                     kept = part * jnp.where(mine, 1.0, 0.0).astype(BF16)
                     masked.append(
@@ -283,23 +286,15 @@
     square_ref[...] = jnp.sum(total[...].T, axis=0, keepdims=True)
 
 
-def gain_kernel(gain_ref, gated_ref, out_ref):
-    for r in range(0, gated_ref.shape[0], BLOCK):
-        for j in range(0, gated_ref.shape[1], LANES):
-            piece = (slice(r, r + BLOCK), slice(j, j + LANES))
-            out_ref[piece] = gated_ref[piece] * gain_ref[:, j : j + LANES]
-
-
-def norm_kernel(channels_all, square_ref, more_ref, gained_ref, out_ref, scale):
+def norm_kernel(channels_all, square_ref, more_ref, gain_ref, gated_ref, out_ref):
     rows = out_ref.shape[0]
     start = pl.multiple_of(pl.program_id(0) * rows, rows)
-    row = lax.rsqrt((square_ref[...] + more_ref[...]) / channels_all + 1e-05)
-    scale[...] = jnp.broadcast_to(row, (LANES, rows)).T
-    for r in range(0, rows, 16):
-        part = scale[r : r + 16, :]
-        for j in range(0, gained_ref.shape[1], LANES):
-            gained = gained_ref[pl.ds(start + r, 16), j : j + LANES]
-            out_ref[r : r + 16, j : j + LANES] = (gained * part).astype(BF16)
+    scale = lax.rsqrt((square_ref[...] + more_ref[...]) / channels_all + 1e-05)
+    scale = jnp.broadcast_to(scale, (LANES, rows)).T
+    for j in range(gated_ref.shape[1] // LANES):
+        cols = slice(j * LANES, (j + 1) * LANES)
+        gated = gated_ref[pl.ds(start, rows), cols]
+        out_ref[:, cols] = (gated * gain_ref[:, cols] * scale).astype(BF16)
 
 
 def chunk_of(total, most):
@@ -325,7 +320,9 @@
     chunks = min(CHUNKS, tiles)
     size = -(-tiles // chunks)
     starts = tuple(min(c * size, tiles - size) for c in range(chunks))
-    pieces = (tiles // 5,) * 5 if tiles % 10 == 0 else (tiles,)
+    pieces = (tiles,)
+    if tiles % 10 == 0:
+        pieces = (3 * tiles // 10,) * 2 + (tiles // 5,) * 2
     return starts, size, chunks + chips - 2, pieces
 
 
@@ -366,7 +363,7 @@
 
     chunk = chunk_of(channels, 512)
     per_chunk = chunk // LANES
-    g, col, enter, own, sent, row = pl.pallas_call(
+    cum, step, col, enter, own, sent, row = pl.pallas_call(
         functools.partial(state_kernel, heads),
         grid=(channels // chunk,),
         in_specs=[
@@ -386,6 +383,7 @@
         ],
         out_specs=[
             whole((rows, length)),
+            whole((rows, length)),
             whole((length, LANES)),
             pl.BlockSpec((count, states, chunk), lambda c: (0, 0, c)),
             pl.BlockSpec((per_chunk, half + 8, LANES), lambda c: (c, 0, 0)),
@@ -393,6 +391,7 @@
             pl.BlockSpec((scalars, chunk), lambda c: (0, c)),
         ],
         out_shape=[
+            jax.ShapeDtypeStruct((rows, length), F32),
             jax.ShapeDtypeStruct((rows, length), F32),
             jax.ShapeDtypeStruct((length, LANES), F32),
             jax.ShapeDtypeStruct((count, states, channels), BF16),
@@ -454,7 +453,7 @@
     group = 2 if tiles % 2 == 0 else 1
     ys, fs, at = [], [], 0
     x, z, readout, heads_hot = in_hbm(token_values, gate_values, state_readout, hot)
-    inputs = (x, z, readout, g, col, affinity, entry, enter, row, heads_hot)
+    inputs = (x, z, readout, cum, step, col, affinity, entry, enter, row, heads_hot)
     for size in pieces:
         wide, first = size * LANES, at // size
         y, f = pl.pallas_call(
@@ -466,6 +465,7 @@
                 pl.BlockSpec((BLOCK, wide), lambda k, q=first: (k, q)),
                 pl.BlockSpec((BLOCK, wide), lambda k, q=first: (k, q)),
                 pl.BlockSpec((BLOCK, states), lambda k: (k, 0)),
+                pl.BlockSpec((rows, BLOCK), lambda k: (0, k)),
                 pl.BlockSpec((rows, BLOCK), lambda k: (0, k)),
                 pl.BlockSpec((BLOCK, LANES), lambda k: (k, 0)),
                 pl.BlockSpec((1, BLOCK, BLOCK), lambda k: (k, 0, 0)),
@@ -506,29 +506,20 @@
     )(spot, own, other, state_readout, *ys, *fs)
 
     squares, more = summed(squares, "head")
-    gained = pl.pallas_call(
-        gain_kernel,
-        in_specs=[VMEM, VMEM],
-        out_specs=VMEM,
-        out_shape=jax.ShapeDtypeStruct((length, channels), F32),
-        input_output_aliases={1: 0},
-        compiler_params=pltpu.CompilerParams(vmem_limit_bytes=16 << 20),
-        name="gain",
-    )(norm_gain.reshape(1, channels), gated)
     return pl.pallas_call(
         functools.partial(norm_kernel, channels * lax.axis_size("head")),
         grid=(count,),
         in_specs=[
             pl.BlockSpec((1, BLOCK), lambda k: (0, k)),
             pl.BlockSpec((1, BLOCK), lambda k: (0, k)),
+            whole((1, channels)),
             VMEM,
         ],
         out_specs=pl.BlockSpec((BLOCK, channels), lambda k: (k, 0)),
         out_shape=jax.ShapeDtypeStruct((length, channels), BF16),
-        scratch_shapes=[pltpu.VMEM((BLOCK, LANES), F32)],
         compiler_params=pltpu.CompilerParams(vmem_limit_bytes=16 << 20),
         name="norm",
-    )(squares, more, gained)
+    )(squares, more, norm_gain.reshape(1, channels), gated)
 
 
 def summed(value, axis):

time: 87.1 us -> 84.6 us (0.971)
  waiting for transfers between devices: 28.3 us -> 33.2 us
  starting transfers between devices: 15 us -> 11.4 us
  Pallas kernels: 41 us -> 37.5 us
    ppermute x5 -> x4, waiting for transfers between devices: 26.4 us -> 30.1 us  [carry_in(): got = lax.ppermute(send, 'seq', pairs)]
    ppermute x5 -> x4, starting transfers between devices: 8.48 us -> 6.11 us  [carry_in(): got = lax.ppermute(send, 'seq', pairs)]
    pallas_call x1 -> x0, Pallas kernels: 2.25 us -> none  [on_device(): pl.pallas_call(gain_kernel, in_specs=[VMEM, VMEM], out_specs=VMEM, out_sh...]
    pallas_call x5 -> x4, Pallas kernels: 23.9 us -> 22.6 us  [on_device(): pl.pallas_call(functools.partial(inner_kernel, width, at, group, count),...]
    ppermute x1, waiting for transfers between devices: 0.01 us -> 1.24 us  [summed(): more = lax.ppermute(value, axis, [(i, i ^ shift) for i in range(size)])]
    ppermute x1, starting transfers between devices: 4.45 us -> 3.3 us  [carry_in(): lax.ppermute(jnp.where(second, entering, onward), 'sub', [(0, 1), (1, 0)])]
  transfers between devices with their start and end apart: 8 -> 7, of which waited for: 5 -> 5; matrix products, arithmetic and copies ran while one was open for 0% -> 0% of each run, Pallas kernels for 32% -> 29%
where the time goes in v8:
time: 84.6 us; the launch traced here: 84.2 us
  Pallas kernels  37.5 us (44%)
  waiting for transfers between devices  33.2 us (39%)
  starting transfers between devices  11.4 us (13%)
  other arithmetic  1 us (1%)
  between operations  0.97 us (1%)
    ppermute x4, waiting for transfers between devices, carry_in(): got = lax.ppermute(send, 'seq', pairs)  30.1 us
    pallas_call x4, Pallas kernels, on_device(): pl.pallas_call(functools.partial(inner_kernel, width, at, group, count),...  22.6 us
    pallas_call x1, Pallas kernels, on_device(): pl.pallas_call(functools.partial(state_kernel, heads), grid=(channels //...  7.28 us
    ppermute x4, starting transfers between devices, carry_in(): got = lax.ppermute(send, 'seq', pairs)  6.11 us
    ppermute x1, starting transfers between devices, carry_in(): lax.ppermute(jnp.where(second, entering, onward), 'sub', [(0, 1), (1, 0)])  3.3 us
    pallas_call x1, Pallas kernels, on_device(): pl.pallas_call(functools.partial(norm_kernel, channels * lax.axis_size('h...  3.27 us
    pallas_call x1, Pallas kernels, on_device(): pl.pallas_call(join_kernel, in_specs=[SMEM] + [VMEM] * (3 + 2 * len(piece...  2.8 us
    ppermute x1, waiting for transfers between devices, carry_in(): got = lax.ppermute(sent, 'sub', [(0, 1), (1, 0)])  1.83 us
  transfers between devices with their start and end apart: 7, of which 5 were waited for; matrix products, arithmetic and copies ran while one was open for 0% of the time, Pallas kernels for 29%

profile of v8, /device:TPU:17, one launch (start us, length us, event | category | flops | bytes accessed | tf_op | source)
XLA Modules:
  0.0 84.2 jit_solution(11061491508430584760)
XLA Ops:
  0.7 0.1 pad_add_fusion.spot_ref
  0.7 7.3 %shard_state.1 = (f32[40,1024]{1,0:T(8,128)S(1)}, f32[40,1024]{1,0:T(8,128)S(1)}, f32[1024,128]{1,0:T(8,128)S(1)}, bf16[4,128,2560]{2,1,0:T(8,128)(2,1)S(1)}, f3...) custom-call(s32[1]{0:T(128)S(6)} %copy.31.live_ref, s32[1024]{0:T(1024)} %docs_ref.11, ...), custom_call_target="tpu_custom_call" | custom-call | tf_op jit(solution)/shard_map/shard_state/pallas_call | solution.py:366
  8.0 0.8 collective-permute-start
  8.8 1.8 %collective-permute-done = f32[20,72,128]{2,1,0:T(8,128)S(1)} collective-permute-done((f32[20,72,128]{2,1,0:T(8,128)S(1)}, f32[20,72,128]{2,1,0:T(8,128)S(1)}, u32[]{:S(2)}, u32[]{:S(2)}) %collective-permute-start) | collective-permute-done | bytes 737312 | tf_op jit(solution)/shard_map/ppermute | solution.py:544
  10.6 0.1 broadcast_select_fusion
  10.8 0.1 slice_add_fusion
  11.0 0.7 collective-permute-start.1
  11.7 0.0 collective-permute-done.1
  11.8 0.1 select_add_fusion.2
  11.9 1.3 %collective-permute-start.2 = (f32[648,128]{1,0:T(8,128)S(1)}, f32[648,128]{1,0:T(8,128)S(1)}, u32[]{:S(2)}, u32[]{:S(2)}) collective-permute-start(f32[648,128]{1,0:T(8,128)S(1)} %pad_maximum_fusion.2), channel_id=1, source_target_pairs={{0,4},{4,8},{1,5},{5,9},{2,6},{6,10},{3,7},{7,11},{16,20},{20,24},... | collective-permute-start | bytes 995336 | tf_op jit(solution)/shard_map/ppermute | solution.py:570
  13.2 17.9 %collective-permute-done.2 = f32[648,128]{1,0:T(8,128)S(1)} collective-permute-done((f32[648,128]{1,0:T(8,128)S(1)}, f32[648,128]{1,0:T(8,128)S(1)}, u32[]{:S(2)}, u32[]{:S(2)}) %collective-permute-start.2) | collective-permute-done | bytes 331808 | tf_op jit(solution)/shard_map/ppermute | solution.py:570
  31.1 0.1 select_add_fusion.1
  31.2 1.9 %collective-permute-start.3 = (f32[648,128]{1,0:T(8,128)S(1)}, f32[648,128]{1,0:T(8,128)S(1)}, u32[]{:S(2)}, u32[]{:S(2)}) collective-permute-start(f32[648,128]{1,0:T(8,128)S(1)} %pad_maximum_fusion.1), channel_id=1, source_target_pairs={{4,8},{8,12},{5,9},{9,13},{6,10},{10,14},{7,11},{11,15},{20,24},{2... | collective-permute-start | bytes 995336 | tf_op jit(solution)/shard_map/ppermute | solution.py:570
  33.1 7.5 %collective-permute-done.3 = f32[648,128]{1,0:T(8,128)S(1)} collective-permute-done((f32[648,128]{1,0:T(8,128)S(1)}, f32[648,128]{1,0:T(8,128)S(1)}, u32[]{:S(2)}, u32[]{:S(2)}) %collective-permute-start.3) | collective-permute-done | bytes 331808 | tf_op jit(solution)/shard_map/ppermute | solution.py:570
  40.6 0.1 select_add_fusion
  40.7 0.0 copy-start.1
  40.8 2.2 %collective-permute-start.4 = (f32[648,128]{1,0:T(8,128)S(1)}, f32[648,128]{1,0:T(8,128)S(1)}, u32[]{:S(2)}, u32[]{:S(2)}) collective-permute-start(f32[648,128]{1,0:T(8,128)S(1)} %pad_maximum_fusion), channel_id=1, source_target_pairs={{8,12},{9,13},{10,14},{11,15},{24,28},{25,29},{26,30},{27,31}} | collective-permute-start | bytes 995336 | tf_op jit(solution)/shard_map/ppermute | solution.py:570
  43.0 4.7 %collective-permute-done.4 = f32[648,128]{1,0:T(8,128)S(1)} collective-permute-done((f32[648,128]{1,0:T(8,128)S(1)}, f32[648,128]{1,0:T(8,128)S(1)}, u32[]{:S(2)}, u32[]{:S(2)}) %collective-permute-start.4) | collective-permute-done | bytes 331808 | tf_op jit(solution)/shard_map/ppermute | solution.py:570
  47.8 0.2 select_select_fusion.1
  47.9 0.2 fusion
  48.1 3.3 %collective-permute-start.5 = (f32[20,64,128]{2,1,0:T(8,128)S(1)}, f32[20,64,128]{2,1,0:T(8,128)S(1)}, u32[]{:S(2)}, u32[]{:S(2)}) collective-permute-start(f32[20,64,128]{2,1,0:T(8,128)S(1)} %get-tuple-element.47), channel_id=1, source_target_pairs={{0,1},{1,0},{2,3},{3,2},{4,5},{5,4},{6,7},{7,6},{8,9},{9,8},{10,11... | collective-permute-start | bytes 1966088 | tf_op jit(solution)/shard_map/ppermute | solution.py:584
  51.4 0.0 copy-done.1
  51.4 1.6 %prepare.1 = (f32[4,256,256]{2,1,0:T(8,128)S(1)}, bf16[1024,256]{1,0:T(8,128)(2,1)S(1)}) custom-call(s32[1024]{0:T(1024)S(1)} %copy-done.1, bf16[1024,128]{1,0:T(8,128)(2,1)} %b_ref.3, bf16[1024,128]{1,0:T(8,128)(2,1)} %c_ref.11, f32[1024,128]{1,0:T(8,128)S(1)} %get-tuple-element.28.col_ref, s32[1,1024]{1,0:T(1,128)S(1)} %bitcast.75), custom_call_target="tpu_custom_call" | custom-call | tf_op jit(solution)/shard_map/prepare/pallas_call | solution.py:430
  53.0 4.9 %shard_map.139 = (f32[1024,512]{1,0:T(8,128)S(1)}, f32[1024,512]{1,0:T(8,128)S(1)}) custom-call(s32[1]{0:T(128)S(6)} %copy.31.live_ref, s32[1024]{0:T(1024)S(1)} %copy-done.1, bf16[1024,2560]{1,0:T(8,128)(2,1)} %x_ref.9, bf16[1024,2560]{1,0:T(8,128)(2,1)} %z_ref.7, bf16[1024,128]{1,0:T(8,128)(2,1)} %c_ref.11, f32[40,1024]{1,0:T(8,128)S(1)} %get-tuple-element.26.cum_ref, ...), custom_call_target="tpu_custom_call" | custom-call | flops 629145600 | bytes 5242880 | tf_op jit(solution)/shard_map/pallas_call | solution.py:459
  57.8 4.9 %shard_map.138 = (f32[1024,512]{1,0:T(8,128)S(1)}, f32[1024,512]{1,0:T(8,128)S(1)}) custom-call(s32[1]{0:T(128)S(6)} %copy.31.live_ref, s32[1024]{0:T(1024)S(1)} %copy-done.1, bf16[1024,2560]{1,0:T(8,128)(2,1)} %x_ref.9, bf16[1024,2560]{1,0:T(8,128)(2,1)} %z_ref.7, bf16[1024,128]{1,0:T(8,128)(2,1)} %c_ref.11, f32[40,1024]{1,0:T(8,128)S(1)} %get-tuple-element.26.cum_ref, ...), custom_call_target="tpu_custom_call" | custom-call | flops 629145600 | bytes 5242880 | tf_op jit(solution)/shard_map/pallas_call | solution.py:459
  62.7 6.4 %shard_map.137 = (f32[1024,768]{1,0:T(8,128)S(1)}, f32[1024,768]{1,0:T(8,128)S(1)}) custom-call(s32[1]{0:T(128)S(6)} %copy.31.live_ref, s32[1024]{0:T(1024)S(1)} %copy-done.1, bf16[1024,2560]{1,0:T(8,128)(2,1)} %x_ref.9, bf16[1024,2560]{1,0:T(8,128)(2,1)} %z_ref.7, bf16[1024,128]{1,0:T(8,128)(2,1)} %c_ref.11, f32[40,1024]{1,0:T(8,128)S(1)} %get-tuple-element.26.cum_ref, ...), custom_call_target="tpu_custom_call" | custom-call | flops 943718400 | bytes 7864320 | tf_op jit(solution)/shard_map/pallas_call | solution.py:459
  69.1 0.0 copy-start
  69.1 6.4 %shard_map.136 = (f32[1024,768]{1,0:T(8,128)S(1)}, f32[1024,768]{1,0:T(8,128)S(1)}) custom-call(s32[1]{0:T(128)S(6)} %copy.31.live_ref, s32[1024]{0:T(1024)S(1)} %copy-done.1, bf16[1024,2560]{1,0:T(8,128)(2,1)} %x_ref.9, bf16[1024,2560]{1,0:T(8,128)(2,1)} %z_ref.7, bf16[1024,128]{1,0:T(8,128)(2,1)} %c_ref.11, f32[40,1024]{1,0:T(8,128)S(1)} %get-tuple-element.26.cum_ref, ...), custom_call_target="tpu_custom_call" | custom-call | flops 943718400 | bytes 7864320 | tf_op jit(solution)/shard_map/pallas_call | solution.py:459
  75.6 0.0 collective-permute-done.5.other_ref
  75.6 0.0 copy-done
  75.6 0.0 copy-start.2
  75.6 2.8 %join.1 = (f32[1024,2560]{1,0:T(8,128)S(1)}, f32[1,1024]{1,0:T(1,128)S(1)}) custom-call(s32[2]{0:T(128)S(1)} %pad_add_fusion.spot_ref, f32[20,64,128]{2,1,0:T(8,128)S(1)} %get-tuple-element.48.own_ref, f32[20,64,128]{2,1,0:T(8,128)S(1)} %collective-permute-done.5.other_ref, bf16[1024,128]{1,0:T(8,128)(2,1)S(1)} %copy-done, ...), custom_call_target="tpu_custom_call" | custom-call | tf_op jit(solution)/shard_map/join/pallas_call | solution.py:495
  78.4 1.3 %collective-permute-start.6 = (f32[1,1024]{1,0:T(1,128)S(1)}, f32[1,1024]{1,0:T(1,128)S(1)}, u32[]{:S(2)}, u32[]{:S(2)}) collective-permute-start(f32[1,1024]{1,0:T(1,128)S(1)} %get-tuple-element.41.square_ref), channel_id=1, source_target_pairs={{0,2},{2,0},{1,3},{3,1},{4,6},{6,4},{5,7},{7,5},{8,10},{10,8},{9,1... | collective-permute-start | bytes 12296 | tf_op jit(solution)/shard_map/ppermute | solution.py:535
  79.7 0.0 copy-done.2
  79.7 1.2 %collective-permute-done.6.more_ref = f32[1,1024]{1,0:T(1,128)S(1)} collective-permute-done((f32[1,1024]{1,0:T(1,128)S(1)}, f32[1,1024]{1,0:T(1,128)S(1)}, u32[]{:S(2)}, u32[]{:S(2)}) %collective-permute-start.6) | collective-permute-done | bytes 4128 | tf_op jit(solution)/shard_map/ppermute | solution.py:535
  80.9 3.3 %norm.1 = bf16[1024,2560]{1,0:T(8,128)(2,1)} custom-call(f32[1,1024]{1,0:T(1,128)S(1)} %get-tuple-element.41.square_ref, f32[1,1024]{1,0:T(1,128)S(1)} %collective-permute-done.6.more_ref, f32[1,2560]{1,0:T(1,128)S(1)} %reshape.78.gain_ref, f32[1024,2560]{1,0:T(8,128)S(1)} %get-tuple-element.42.gated_ref), custom_call_target="tpu_custom_call" | custom-call | tf_op jit(solution)/shard_map/norm/pallas_call | solution.py:509
  (24 shorter events, 0.3 us)
Async XLA Ops:
  8.0 2.6 %collective-permute-start = (f32[20,72,128]{2,1,0:T(8,128)S(1)}, f32[20,72,128]{2,1,0:T(8,128)S(1)}, u32[]{:S(2)}, u32[]{:S(2)}) collective-permute-start(f32[20,72,128]{2,1,0:T(8,128)S(1)} %get-tuple-element.25), channel_id=1, source_target_pairs={{0,1},{1,0},{2,3},{3,2},{4,5},{5,4},{6,7},{7,6},{8,9},{9,8},{10,11... | collective-permute-start | bytes 2211848 | tf_op jit(solution)/shard_map/ppermute | solution.py:544
  11.0 0.7 collective-permute-start.1
  11.9 19.2 %collective-permute-start.2 = (f32[648,128]{1,0:T(8,128)S(1)}, f32[648,128]{1,0:T(8,128)S(1)}, u32[]{:S(2)}, u32[]{:S(2)}) collective-permute-start(f32[648,128]{1,0:T(8,128)S(1)} %pad_maximum_fusion.2), channel_id=1, source_target_pairs={{0,4},{4,8},{1,5},{5,9},{2,6},{6,10},{3,7},{7,11},{16,20},{20,24},... | collective-permute-start | bytes 995336 | tf_op jit(solution)/shard_map/ppermute | solution.py:570
  31.2 9.4 %collective-permute-start.3 = (f32[648,128]{1,0:T(8,128)S(1)}, f32[648,128]{1,0:T(8,128)S(1)}, u32[]{:S(2)}, u32[]{:S(2)}) collective-permute-start(f32[648,128]{1,0:T(8,128)S(1)} %pad_maximum_fusion.1), channel_id=1, source_target_pairs={{4,8},{8,12},{5,9},{9,13},{6,10},{10,14},{7,11},{11,15},{20,24},{2... | collective-permute-start | bytes 995336 | tf_op jit(solution)/shard_map/ppermute | solution.py:570
  40.7 10.7 %copy-start.1 = (s32[1024]{0:T(1024)S(1)}, s32[1024]{0:T(1024)}, u32[]{:S(2)}) copy-start(s32[1024]{0:T(1024)} %docs_ref.11) | copy-start | bytes 12292
  40.8 7.0 %collective-permute-start.4 = (f32[648,128]{1,0:T(8,128)S(1)}, f32[648,128]{1,0:T(8,128)S(1)}, u32[]{:S(2)}, u32[]{:S(2)}) collective-permute-start(f32[648,128]{1,0:T(8,128)S(1)} %pad_maximum_fusion), channel_id=1, source_target_pairs={{8,12},{9,13},{10,14},{11,15},{24,28},{25,29},{26,30},{27,31}} | collective-permute-start | bytes 995336 | tf_op jit(solution)/shard_map/ppermute | solution.py:570
  48.1 27.5 %collective-permute-start.5 = (f32[20,64,128]{2,1,0:T(8,128)S(1)}, f32[20,64,128]{2,1,0:T(8,128)S(1)}, u32[]{:S(2)}, u32[]{:S(2)}) collective-permute-start(f32[20,64,128]{2,1,0:T(8,128)S(1)} %get-tuple-element.47), channel_id=1, source_target_pairs={{0,1},{1,0},{2,3},{3,2},{4,5},{5,4},{6,7},{7,6},{8,9},{9,8},{10,11... | collective-permute-start | bytes 1966088 | tf_op jit(solution)/shard_map/ppermute | solution.py:584
  69.1 6.4 %copy-start = (bf16[1024,128]{1,0:T(8,128)(2,1)S(1)}, bf16[1024,128]{1,0:T(8,128)(2,1)}, u32[]{:S(2)}) copy-start(bf16[1024,128]{1,0:T(8,128)(2,1)} %c_ref.11) | copy-start | bytes 786436
  75.6 4.1 %copy-start.2 = (f32[2560]{0:T(1024)S(1)}, f32[2560]{0:T(1024)}, u32[]{:S(2)}) copy-start(f32[2560]{0:T(1024)} %param.22) | copy-start | bytes 30724
  78.4 2.5 %collective-permute-start.6 = (f32[1,1024]{1,0:T(1,128)S(1)}, f32[1,1024]{1,0:T(1,128)S(1)}, u32[]{:S(2)}, u32[]{:S(2)}) collective-permute-start(f32[1,1024]{1,0:T(1,128)S(1)} %get-tuple-element.41.square_ref), channel_id=1, source_target_pairs={{0,2},{2,0},{1,3},{3,1},{4,6},{6,4},{5,7},{7,5},{8,10},{10,8},{9,1... | collective-permute-start | bytes 12296 | tf_op jit(solution)/shard_map/ppermute | solution.py:535

commit v9 on v8

--- a/solution.py
+++ b/solution.py
@@ -73,11 +73,22 @@
     inputs_t,
     state,
     scal,
+    x_parts,
+    x_sems,
 ):
-    length = raw_ref.shape[0 + 1]
-    rows = raw_ref.shape[0]
+    rows, length = raw_ref.shape
     count = length // BLOCK
-    wide = x_ref.shape[1]
+    wide = hot_ref.shape[1]
+    step_at, slot = pl.program_id(0), lax.rem(pl.program_id(0), 2)
+
+    def fetch(at, into):
+        cols = pl.ds(pl.multiple_of(at * wide, LANES), wide)
+        return pltpu.make_async_copy(x_ref.at[:, cols], x_parts.at[into], x_sems.at[into])
+
+    @pl.when(step_at == 0)
+    def _():
+        fetch(0, 0).start()
+
     ends = [docs_ref[j * BLOCK + BLOCK - 1] for j in range(count)]
 
     @pl.when(pl.program_id(0) == 0)
@@ -123,13 +134,18 @@
         scal[2 * count : 2 * count + 1, :] = jnp.where(head_lane, jnp.exp2(before), 0.0)
         scal[2 * count + 1 : 2 * count + 2, 0:heads] = skip_ref[...]
 
+    @pl.when(step_at + 1 < pl.num_programs(0))
+    def _():
+        fetch(step_at + 1, 1 - slot).start()
+
     hot = hot_ref[...]
     high, low = two_parts(scal[...])
     row = dot(high, hot) + dot(low, hot)
     row_ref[...] = row
     hot_low = jnp.concatenate([hot_low_ref[...]] * 2, axis=0)
     state[...] = jnp.zeros_like(state)
-    scaled = (x_ref[...].astype(F32) * dot(col_parts[...], hot_low)).astype(BF16)
+    fetch(step_at, slot).wait()
+    scaled = (x_parts[slot].astype(F32) * dot(col_parts[...], hot_low)).astype(BF16)
     for j in range(count):
         piece = slice(j * BLOCK, (j + 1) * BLOCK)
         prior = docs_ref[max(j * BLOCK - 1, 0)]
@@ -286,15 +302,25 @@
     square_ref[...] = jnp.sum(total[...].T, axis=0, keepdims=True)
 
 
-def norm_kernel(channels_all, square_ref, more_ref, gain_ref, gated_ref, out_ref):
-    rows = out_ref.shape[0]
-    start = pl.multiple_of(pl.program_id(0) * rows, rows)
-    scale = lax.rsqrt((square_ref[...] + more_ref[...]) / channels_all + 1e-05)
-    scale = jnp.broadcast_to(scale, (LANES, rows)).T
-    for j in range(gated_ref.shape[1] // LANES):
-        cols = slice(j * LANES, (j + 1) * LANES)
-        gated = gated_ref[pl.ds(start, rows), cols]
-        out_ref[:, cols] = (gated * gain_ref[:, cols] * scale).astype(BF16)
+def norm_kernel(
+    channels_all, square_ref, more_ref, gain_ref, gated_ref, out_ref, stage, scale, sems
+):
+    length = gated_ref.shape[0]
+    row = lax.rsqrt((square_ref[...] + more_ref[...]) / channels_all + 1e-05)
+    copies = []
+    for b in range(length // LANES):
+        block = slice(b * LANES, (b + 1) * LANES)
+        scale[...] = jnp.broadcast_to(row[:, block], (LANES, LANES)).T
+        for r in range(0, LANES, 16):
+            rows = slice(b * LANES + r, b * LANES + r + 16)
+            part = scale[r : r + 16, :]
+            for j in range(0, gated_ref.shape[1], LANES):
+                cols = slice(j, j + LANES)
+                stage[rows, cols] = (gated_ref[rows, cols] * gain_ref[:, cols] * part).astype(BF16)
+        copies.append(pltpu.make_async_copy(stage.at[block], out_ref.at[block], sems.at[b]))
+        copies[-1].start()
+    for copy in copies:
+        copy.wait()
 
 
 def chunk_of(total, most):
@@ -378,7 +404,7 @@
             whole((BLOCK, BLOCK)),
             pl.BlockSpec((LANES, chunk), lambda c: (0, c)),
             pl.BlockSpec((LANES, chunk), lambda c: (0, c)),
-            pl.BlockSpec((length, chunk), lambda c: (0, c)),
+            pl.BlockSpec(memory_space=pl.ANY),
             whole((length, states)),
         ],
         out_specs=[
@@ -405,6 +431,8 @@
             pltpu.VMEM((states, length), BF16),
             pltpu.VMEM((states, chunk), F32),
             pltpu.VMEM((scalars, LANES), F32),
+            pltpu.VMEM((2, length, chunk), BF16),
+            pltpu.SemaphoreType.DMA((2,)),
         ],
         compiler_params=pltpu.CompilerParams(vmem_limit_bytes=EARLY_VMEM),
         name="shard_state",
@@ -508,15 +536,14 @@
     squares, more = summed(squares, "head")
     return pl.pallas_call(
         functools.partial(norm_kernel, channels * lax.axis_size("head")),
-        grid=(count,),
-        in_specs=[
-            pl.BlockSpec((1, BLOCK), lambda k: (0, k)),
-            pl.BlockSpec((1, BLOCK), lambda k: (0, k)),
-            whole((1, channels)),
-            VMEM,
-        ],
-        out_specs=pl.BlockSpec((BLOCK, channels), lambda k: (k, 0)),
+        in_specs=[VMEM] * 4,
+        out_specs=pl.BlockSpec(memory_space=pl.ANY),
         out_shape=jax.ShapeDtypeStruct((length, channels), BF16),
+        scratch_shapes=[
+            pltpu.VMEM((length, channels), BF16),
+            pltpu.VMEM((LANES, LANES), F32),
+            pltpu.SemaphoreType.DMA((length // LANES,)),
+        ],
         compiler_params=pltpu.CompilerParams(vmem_limit_bytes=16 << 20),
         name="norm",
     )(squares, more, norm_gain.reshape(1, channels), gated)

time: 84.6 us -> 84.3 us (level)
  the two profiles are of different devices: /device:TPU:17 before, /device:TPU:19 now
where the time goes in v9:
time: 84.3 us; the launch traced here: 83.8 us
  Pallas kernels  37 us (44%)
  waiting for transfers between devices  34.1 us (40%)
  starting transfers between devices  10.5 us (12%)
  other arithmetic  1 us (1%)
  between operations  0.97 us (1%)
    ppermute x4, waiting for transfers between devices, carry_in(): got = lax.ppermute(send, 'seq', pairs)  30.1 us
    pallas_call x4, Pallas kernels, on_device(): pl.pallas_call(functools.partial(inner_kernel, width, at, group, count),...  22.6 us
    pallas_call x1, Pallas kernels, on_device(): pl.pallas_call(functools.partial(state_kernel, heads), grid=(channels //...  7.39 us
    ppermute x4, starting transfers between devices, carry_in(): got = lax.ppermute(send, 'seq', pairs)  6.11 us
    ppermute x1, starting transfers between devices, carry_in(): lax.ppermute(jnp.where(second, entering, onward), 'sub', [(0, 1), (1, 0)])  3.3 us
    pallas_call x1, Pallas kernels, on_device(): pl.pallas_call(join_kernel, in_specs=[SMEM] + [VMEM] * (3 + 2 * len(piece...  2.8 us
    pallas_call x1, Pallas kernels, on_device(): pl.pallas_call(functools.partial(norm_kernel, channels * lax.axis_size('h...  2.74 us
    ppermute x1, waiting for transfers between devices, summed(): more = lax.ppermute(value, axis, [(i, i ^ shift) for i in range(size)])  2.19 us
  transfers between devices with their start and end apart: 7, of which 5 were waited for; matrix products, arithmetic and copies ran while one was open for 0% of the time, Pallas kernels for 29%

profile of v9, /device:TPU:19, one launch (start us, length us, event | category | flops | bytes accessed | tf_op | source)
XLA Modules:
  0.0 83.8 jit_solution(11359749423610035605)
XLA Ops:
  0.7 0.1 pad_add_fusion.spot_ref
  0.7 7.4 %shard_state.1 = (f32[40,1024]{1,0:T(8,128)S(1)}, f32[40,1024]{1,0:T(8,128)S(1)}, f32[1024,128]{1,0:T(8,128)S(1)}, bf16[4,128,2560]{2,1,0:T(8,128)(2,1)S(1)}, f3...) custom-call(s32[1]{0:T(128)S(6)} %copy.31.live_ref, s32[1024]{0:T(1024)} %docs_ref.11, ...), custom_call_target="tpu_custom_call" | custom-call | tf_op jit(solution)/shard_map/shard_state/pallas_call | solution.py:392
  8.1 0.7 collective-permute-start
  8.9 1.8 %collective-permute-done = f32[20,72,128]{2,1,0:T(8,128)S(1)} collective-permute-done((f32[20,72,128]{2,1,0:T(8,128)S(1)}, f32[20,72,128]{2,1,0:T(8,128)S(1)}, u32[]{:S(2)}, u32[]{:S(2)}) %collective-permute-start) | collective-permute-done | bytes 737312 | tf_op jit(solution)/shard_map/ppermute | solution.py:571
  10.7 0.1 broadcast_select_fusion
  10.9 0.1 slice_add_fusion
  11.1 0.7 collective-permute-start.1
  11.8 0.0 collective-permute-done.1
  11.9 0.1 select_add_fusion.2
  12.0 1.3 %collective-permute-start.2 = (f32[648,128]{1,0:T(8,128)S(1)}, f32[648,128]{1,0:T(8,128)S(1)}, u32[]{:S(2)}, u32[]{:S(2)}) collective-permute-start(f32[648,128]{1,0:T(8,128)S(1)} %pad_maximum_fusion.2), channel_id=1, source_target_pairs={{0,4},{4,8},{1,5},{5,9},{2,6},{6,10},{3,7},{7,11},{16,20},{20,24},... | collective-permute-start | bytes 995336 | tf_op jit(solution)/shard_map/ppermute | solution.py:597
  13.3 17.9 %collective-permute-done.2 = f32[648,128]{1,0:T(8,128)S(1)} collective-permute-done((f32[648,128]{1,0:T(8,128)S(1)}, f32[648,128]{1,0:T(8,128)S(1)}, u32[]{:S(2)}, u32[]{:S(2)}) %collective-permute-start.2) | collective-permute-done | bytes 331808 | tf_op jit(solution)/shard_map/ppermute | solution.py:597
  31.2 0.1 select_add_fusion.1
  31.3 1.9 %collective-permute-start.3 = (f32[648,128]{1,0:T(8,128)S(1)}, f32[648,128]{1,0:T(8,128)S(1)}, u32[]{:S(2)}, u32[]{:S(2)}) collective-permute-start(f32[648,128]{1,0:T(8,128)S(1)} %pad_maximum_fusion.1), channel_id=1, source_target_pairs={{4,8},{8,12},{5,9},{9,13},{6,10},{10,14},{7,11},{11,15},{20,24},{2... | collective-permute-start | bytes 995336 | tf_op jit(solution)/shard_map/ppermute | solution.py:597
  33.2 7.5 %collective-permute-done.3 = f32[648,128]{1,0:T(8,128)S(1)} collective-permute-done((f32[648,128]{1,0:T(8,128)S(1)}, f32[648,128]{1,0:T(8,128)S(1)}, u32[]{:S(2)}, u32[]{:S(2)}) %collective-permute-start.3) | collective-permute-done | bytes 331808 | tf_op jit(solution)/shard_map/ppermute | solution.py:597
  40.8 0.1 select_add_fusion
  40.8 0.0 copy-start.1
  40.9 2.2 %collective-permute-start.4 = (f32[648,128]{1,0:T(8,128)S(1)}, f32[648,128]{1,0:T(8,128)S(1)}, u32[]{:S(2)}, u32[]{:S(2)}) collective-permute-start(f32[648,128]{1,0:T(8,128)S(1)} %pad_maximum_fusion), channel_id=1, source_target_pairs={{8,12},{9,13},{10,14},{11,15},{24,28},{25,29},{26,30},{27,31}} | collective-permute-start | bytes 995336 | tf_op jit(solution)/shard_map/ppermute | solution.py:597
  43.1 4.7 %collective-permute-done.4 = f32[648,128]{1,0:T(8,128)S(1)} collective-permute-done((f32[648,128]{1,0:T(8,128)S(1)}, f32[648,128]{1,0:T(8,128)S(1)}, u32[]{:S(2)}, u32[]{:S(2)}) %collective-permute-start.4) | collective-permute-done | bytes 331808 | tf_op jit(solution)/shard_map/ppermute | solution.py:597
  47.9 0.2 select_select_fusion.1
  48.0 0.2 fusion
  48.2 3.3 %collective-permute-start.5 = (f32[20,64,128]{2,1,0:T(8,128)S(1)}, f32[20,64,128]{2,1,0:T(8,128)S(1)}, u32[]{:S(2)}, u32[]{:S(2)}) collective-permute-start(f32[20,64,128]{2,1,0:T(8,128)S(1)} %get-tuple-element.47), channel_id=1, source_target_pairs={{0,1},{1,0},{2,3},{3,2},{4,5},{5,4},{6,7},{7,6},{8,9},{9,8},{10,11... | collective-permute-start | bytes 1966088 | tf_op jit(solution)/shard_map/ppermute | solution.py:611
  51.5 0.0 copy-done.1
  51.5 1.6 %prepare.1 = (f32[4,256,256]{2,1,0:T(8,128)S(1)}, bf16[1024,256]{1,0:T(8,128)(2,1)S(1)}) custom-call(s32[1024]{0:T(1024)S(1)} %copy-done.1, bf16[1024,128]{1,0:T(8,128)(2,1)} %b_ref.3, bf16[1024,128]{1,0:T(8,128)(2,1)} %c_ref.11, f32[1024,128]{1,0:T(8,128)S(1)} %get-tuple-element.28.col_ref, s32[1,1024]{1,0:T(1,128)S(1)} %bitcast.75), custom_call_target="tpu_custom_call" | custom-call | tf_op jit(solution)/shard_map/prepare/pallas_call | solution.py:458
  53.1 4.9 %shard_map.139 = (f32[1024,512]{1,0:T(8,128)S(1)}, f32[1024,512]{1,0:T(8,128)S(1)}) custom-call(s32[1]{0:T(128)S(6)} %copy.31.live_ref, s32[1024]{0:T(1024)S(1)} %copy-done.1, bf16[1024,2560]{1,0:T(8,128)(2,1)} %x_ref.9, bf16[1024,2560]{1,0:T(8,128)(2,1)} %z_ref.7, bf16[1024,128]{1,0:T(8,128)(2,1)} %c_ref.11, f32[40,1024]{1,0:T(8,128)S(1)} %get-tuple-element.26.cum_ref, ...), custom_call_target="tpu_custom_call" | custom-call | flops 629145600 | bytes 5242880 | tf_op jit(solution)/shard_map/pallas_call | solution.py:487
  57.9 4.9 %shard_map.138 = (f32[1024,512]{1,0:T(8,128)S(1)}, f32[1024,512]{1,0:T(8,128)S(1)}) custom-call(s32[1]{0:T(128)S(6)} %copy.31.live_ref, s32[1024]{0:T(1024)S(1)} %copy-done.1, bf16[1024,2560]{1,0:T(8,128)(2,1)} %x_ref.9, bf16[1024,2560]{1,0:T(8,128)(2,1)} %z_ref.7, bf16[1024,128]{1,0:T(8,128)(2,1)} %c_ref.11, f32[40,1024]{1,0:T(8,128)S(1)} %get-tuple-element.26.cum_ref, ...), custom_call_target="tpu_custom_call" | custom-call | flops 629145600 | bytes 5242880 | tf_op jit(solution)/shard_map/pallas_call | solution.py:487
  62.8 6.4 %shard_map.137 = (f32[1024,768]{1,0:T(8,128)S(1)}, f32[1024,768]{1,0:T(8,128)S(1)}) custom-call(s32[1]{0:T(128)S(6)} %copy.31.live_ref, s32[1024]{0:T(1024)S(1)} %copy-done.1, bf16[1024,2560]{1,0:T(8,128)(2,1)} %x_ref.9, bf16[1024,2560]{1,0:T(8,128)(2,1)} %z_ref.7, bf16[1024,128]{1,0:T(8,128)(2,1)} %c_ref.11, f32[40,1024]{1,0:T(8,128)S(1)} %get-tuple-element.26.cum_ref, ...), custom_call_target="tpu_custom_call" | custom-call | flops 943718400 | bytes 7864320 | tf_op jit(solution)/shard_map/pallas_call | solution.py:487
  69.2 0.0 copy-start
  69.2 6.4 %shard_map.136 = (f32[1024,768]{1,0:T(8,128)S(1)}, f32[1024,768]{1,0:T(8,128)S(1)}) custom-call(s32[1]{0:T(128)S(6)} %copy.31.live_ref, s32[1024]{0:T(1024)S(1)} %copy-done.1, bf16[1024,2560]{1,0:T(8,128)(2,1)} %x_ref.9, bf16[1024,2560]{1,0:T(8,128)(2,1)} %z_ref.7, bf16[1024,128]{1,0:T(8,128)(2,1)} %c_ref.11, f32[40,1024]{1,0:T(8,128)S(1)} %get-tuple-element.26.cum_ref, ...), custom_call_target="tpu_custom_call" | custom-call | flops 943718400 | bytes 7864320 | tf_op jit(solution)/shard_map/pallas_call | solution.py:487
  75.7 0.0 collective-permute-done.5.other_ref
  75.7 0.0 copy-done
  75.7 0.0 copy-start.2
  75.7 2.8 %join.1 = (f32[1024,2560]{1,0:T(8,128)S(1)}, f32[1,1024]{1,0:T(1,128)S(1)}) custom-call(s32[2]{0:T(128)S(1)} %pad_add_fusion.spot_ref, f32[20,64,128]{2,1,0:T(8,128)S(1)} %get-tuple-element.48.own_ref, f32[20,64,128]{2,1,0:T(8,128)S(1)} %collective-permute-done.5.other_ref, bf16[1024,128]{1,0:T(8,128)(2,1)S(1)} %copy-done, ...), custom_call_target="tpu_custom_call" | custom-call | tf_op jit(solution)/shard_map/join/pallas_call | solution.py:523
  78.5 0.3 collective-permute-start.6
  78.8 0.0 copy-done.2
  78.8 2.2 %collective-permute-done.6.more_ref = f32[1,1024]{1,0:T(1,128)S(1)} collective-permute-done((f32[1,1024]{1,0:T(1,128)S(1)}, f32[1,1024]{1,0:T(1,128)S(1)}, u32[]{:S(2)}, u32[]{:S(2)}) %collective-permute-start.6) | collective-permute-done | bytes 4128 | tf_op jit(solution)/shard_map/ppermute | solution.py:562
  81.0 2.7 %norm.1 = bf16[1024,2560]{1,0:T(8,128)(2,1)} custom-call(f32[1,1024]{1,0:T(1,128)S(1)} %get-tuple-element.41.square_ref, f32[1,1024]{1,0:T(1,128)S(1)} %collective-permute-done.6.more_ref, f32[1,2560]{1,0:T(1,128)S(1)} %reshape.78.gain_ref, f32[1024,2560]{1,0:T(8,128)S(1)} %get-tuple-element.42.gated_ref), custom_call_target="tpu_custom_call" | custom-call | tf_op jit(solution)/shard_map/norm/pallas_call | solution.py:537
  (24 shorter events, 0.3 us)
Async XLA Ops:
  8.1 2.6 %collective-permute-start = (f32[20,72,128]{2,1,0:T(8,128)S(1)}, f32[20,72,128]{2,1,0:T(8,128)S(1)}, u32[]{:S(2)}, u32[]{:S(2)}) collective-permute-start(f32[20,72,128]{2,1,0:T(8,128)S(1)} %get-tuple-element.25), channel_id=1, source_target_pairs={{0,1},{1,0},{2,3},{3,2},{4,5},{5,4},{6,7},{7,6},{8,9},{9,8},{10,11... | collective-permute-start | bytes 2211848 | tf_op jit(solution)/shard_map/ppermute | solution.py:571
  11.1 0.7 collective-permute-start.1
  12.0 19.2 %collective-permute-start.2 = (f32[648,128]{1,0:T(8,128)S(1)}, f32[648,128]{1,0:T(8,128)S(1)}, u32[]{:S(2)}, u32[]{:S(2)}) collective-permute-start(f32[648,128]{1,0:T(8,128)S(1)} %pad_maximum_fusion.2), channel_id=1, source_target_pairs={{0,4},{4,8},{1,5},{5,9},{2,6},{6,10},{3,7},{7,11},{16,20},{20,24},... | collective-permute-start | bytes 995336 | tf_op jit(solution)/shard_map/ppermute | solution.py:597
  31.3 9.4 %collective-permute-start.3 = (f32[648,128]{1,0:T(8,128)S(1)}, f32[648,128]{1,0:T(8,128)S(1)}, u32[]{:S(2)}, u32[]{:S(2)}) collective-permute-start(f32[648,128]{1,0:T(8,128)S(1)} %pad_maximum_fusion.1), channel_id=1, source_target_pairs={{4,8},{8,12},{5,9},{9,13},{6,10},{10,14},{7,11},{11,15},{20,24},{2... | collective-permute-start | bytes 995336 | tf_op jit(solution)/shard_map/ppermute | solution.py:597
  40.8 10.7 %copy-start.1 = (s32[1024]{0:T(1024)S(1)}, s32[1024]{0:T(1024)}, u32[]{:S(2)}) copy-start(s32[1024]{0:T(1024)} %docs_ref.11) | copy-start | bytes 12292
  40.9 7.0 %collective-permute-start.4 = (f32[648,128]{1,0:T(8,128)S(1)}, f32[648,128]{1,0:T(8,128)S(1)}, u32[]{:S(2)}, u32[]{:S(2)}) collective-permute-start(f32[648,128]{1,0:T(8,128)S(1)} %pad_maximum_fusion), channel_id=1, source_target_pairs={{8,12},{9,13},{10,14},{11,15},{24,28},{25,29},{26,30},{27,31}} | collective-permute-start | bytes 995336 | tf_op jit(solution)/shard_map/ppermute | solution.py:597
  48.2 27.5 %collective-permute-start.5 = (f32[20,64,128]{2,1,0:T(8,128)S(1)}, f32[20,64,128]{2,1,0:T(8,128)S(1)}, u32[]{:S(2)}, u32[]{:S(2)}) collective-permute-start(f32[20,64,128]{2,1,0:T(8,128)S(1)} %get-tuple-element.47), channel_id=1, source_target_pairs={{0,1},{1,0},{2,3},{3,2},{4,5},{5,4},{6,7},{7,6},{8,9},{9,8},{10,11... | collective-permute-start | bytes 1966088 | tf_op jit(solution)/shard_map/ppermute | solution.py:611
  69.2 6.4 %copy-start = (bf16[1024,128]{1,0:T(8,128)(2,1)S(1)}, bf16[1024,128]{1,0:T(8,128)(2,1)}, u32[]{:S(2)}) copy-start(bf16[1024,128]{1,0:T(8,128)(2,1)} %c_ref.11) | copy-start | bytes 786436
  75.7 3.1 %copy-start.2 = (f32[2560]{0:T(1024)S(1)}, f32[2560]{0:T(1024)}, u32[]{:S(2)}) copy-start(f32[2560]{0:T(1024)} %param.22) | copy-start | bytes 30724
  78.5 2.5 %collective-permute-start.6 = (f32[1,1024]{1,0:T(1,128)S(1)}, f32[1,1024]{1,0:T(1,128)S(1)}, u32[]{:S(2)}, u32[]{:S(2)}) collective-permute-start(f32[1,1024]{1,0:T(1,128)S(1)} %get-tuple-element.41.square_ref), channel_id=1, source_target_pairs={{0,2},{2,0},{1,3},{3,1},{4,6},{6,4},{5,7},{7,5},{8,10},{10,8},{9,1... | collective-permute-start | bytes 12296 | tf_op jit(solution)/shard_map/ppermute | solution.py:562

commit v10 on v9

--- a/solution.py
+++ b/solution.py
@@ -73,22 +73,11 @@
     inputs_t,
     state,
     scal,
-    x_parts,
-    x_sems,
 ):
-    rows, length = raw_ref.shape
+    length = raw_ref.shape[0 + 1]
+    rows = raw_ref.shape[0]
     count = length // BLOCK
-    wide = hot_ref.shape[1]
-    step_at, slot = pl.program_id(0), lax.rem(pl.program_id(0), 2)
-
-    def fetch(at, into):
-        cols = pl.ds(pl.multiple_of(at * wide, LANES), wide)
-        return pltpu.make_async_copy(x_ref.at[:, cols], x_parts.at[into], x_sems.at[into])
-
-    @pl.when(step_at == 0)
-    def _():
-        fetch(0, 0).start()
-
+    wide = x_ref.shape[1]
     ends = [docs_ref[j * BLOCK + BLOCK - 1] for j in range(count)]
 
     @pl.when(pl.program_id(0) == 0)
@@ -134,18 +123,13 @@
         scal[2 * count : 2 * count + 1, :] = jnp.where(head_lane, jnp.exp2(before), 0.0)
         scal[2 * count + 1 : 2 * count + 2, 0:heads] = skip_ref[...]
 
-    @pl.when(step_at + 1 < pl.num_programs(0))
-    def _():
-        fetch(step_at + 1, 1 - slot).start()
-
     hot = hot_ref[...]
     high, low = two_parts(scal[...])
     row = dot(high, hot) + dot(low, hot)
     row_ref[...] = row
     hot_low = jnp.concatenate([hot_low_ref[...]] * 2, axis=0)
     state[...] = jnp.zeros_like(state)
-    fetch(step_at, slot).wait()
-    scaled = (x_parts[slot].astype(F32) * dot(col_parts[...], hot_low)).astype(BF16)
+    scaled = (x_ref[...].astype(F32) * dot(col_parts[...], hot_low)).astype(BF16)
     for j in range(count):
         piece = slice(j * BLOCK, (j + 1) * BLOCK)
         prior = docs_ref[max(j * BLOCK - 1, 0)]
@@ -273,12 +257,11 @@
 def join_kernel(spot_ref, own_ref, other_ref, c_ref, *refs):
     pieces = (len(refs) - 3) // 2
     gated_ref, square_ref, total = refs[2 * pieces :]
-    length = c_ref.shape[0]
     second = spot_ref[0] == 1
     total[...] = jnp.zeros_like(total)
     tile = 0
     for y_ref, f_ref in zip(refs[:pieces], refs[pieces : 2 * pieces]):
-        wide = chunk_of(y_ref.shape[1], 4 * LANES)
+        wide = chunk_of(y_ref.shape[1], 2 * LANES)
         for c in range(0, y_ref.shape[1], wide):
             parts = []
             for j in range(tile, tile + wide // LANES):
@@ -288,16 +271,13 @@
                         [jnp.where(second, other, own), jnp.where(second, own, other)], axis=0
                     )
                 )
-            carry = jnp.concatenate(parts, axis=1)
-            for r in range(0, length, BLOCK):
-                rows = slice(r, r + BLOCK)
-                outer = dot(c_ref[rows, :], carry)
-                gated = y_ref[rows, c : c + wide] + f_ref[rows, c : c + wide] * outer
-                gated_ref[rows, tile * LANES : tile * LANES + wide] = gated
-                square = total[rows, :]
-                for j in range(0, wide, LANES):
-                    square = square + gated[:, j : j + LANES] * gated[:, j : j + LANES]
-                total[rows, :] = square
+            outer = dot(c_ref[...], jnp.concatenate(parts, axis=1))
+            gated = y_ref[:, c : c + wide] + f_ref[:, c : c + wide] * outer
+            gated_ref[:, tile * LANES : tile * LANES + wide] = gated
+            square = total[...]
+            for j in range(0, wide, LANES):
+                square = square + gated[:, j : j + LANES] * gated[:, j : j + LANES]
+            total[...] = square
             tile += wide // LANES
     square_ref[...] = jnp.sum(total[...].T, axis=0, keepdims=True)
 
@@ -404,7 +384,7 @@
             whole((BLOCK, BLOCK)),
             pl.BlockSpec((LANES, chunk), lambda c: (0, c)),
             pl.BlockSpec((LANES, chunk), lambda c: (0, c)),
-            pl.BlockSpec(memory_space=pl.ANY),
+            pl.BlockSpec((length, chunk), lambda c: (0, c)),
             whole((length, states)),
         ],
         out_specs=[
@@ -431,8 +411,6 @@
             pltpu.VMEM((states, length), BF16),
             pltpu.VMEM((states, chunk), F32),
             pltpu.VMEM((scalars, LANES), F32),
-            pltpu.VMEM((2, length, chunk), BF16),
-            pltpu.SemaphoreType.DMA((2,)),
         ],
         compiler_params=pltpu.CompilerParams(vmem_limit_bytes=EARLY_VMEM),
         name="shard_state",

time: 84.3 us -> 84 us (level)
  no operation moved by 1% of the time
where the time goes in v10:
time: 84 us; the launch traced here: 83.5 us
  Pallas kernels  36.8 us (44%)
  waiting for transfers between devices  34.1 us (41%)
  starting transfers between devices  10.5 us (12%)
  other arithmetic  1 us (1%)
  between operations  0.97 us (1%)
    ppermute x4, waiting for transfers between devices, carry_in(): got = lax.ppermute(send, 'seq', pairs)  30.1 us
    pallas_call x4, Pallas kernels, on_device(): pl.pallas_call(functools.partial(inner_kernel, width, at, group, count),...  22.6 us
    pallas_call x1, Pallas kernels, on_device(): pl.pallas_call(functools.partial(state_kernel, heads), grid=(channels //...  7.29 us
    ppermute x4, starting transfers between devices, carry_in(): got = lax.ppermute(send, 'seq', pairs)  6.11 us
    ppermute x1, starting transfers between devices, carry_in(): lax.ppermute(jnp.where(second, entering, onward), 'sub', [(0, 1), (1, 0)])  3.3 us
    pallas_call x1, Pallas kernels, on_device(): pl.pallas_call(functools.partial(norm_kernel, channels * lax.axis_size('h...  2.74 us
    pallas_call x1, Pallas kernels, on_device(): pl.pallas_call(join_kernel, in_specs=[SMEM] + [VMEM] * (3 + 2 * len(piece...  2.65 us
    ppermute x1, waiting for transfers between devices, summed(): more = lax.ppermute(value, axis, [(i, i ^ shift) for i in range(size)])  2.19 us
  transfers between devices with their start and end apart: 7, of which 5 were waited for; matrix products, arithmetic and copies ran while one was open for 0% of the time, Pallas kernels for 29%

profile of v10, /device:TPU:19, one launch (start us, length us, event | category | flops | bytes accessed | tf_op | source)
XLA Modules:
  0.0 83.5 jit_solution(4572868212663112121)
XLA Ops:
  0.7 0.1 pad_add_fusion.spot_ref
  0.7 7.3 %shard_state.1 = (f32[40,1024]{1,0:T(8,128)S(1)}, f32[40,1024]{1,0:T(8,128)S(1)}, f32[1024,128]{1,0:T(8,128)S(1)}, bf16[4,128,2560]{2,1,0:T(8,128)(2,1)S(1)}, f3...) custom-call(s32[1]{0:T(128)S(6)} %copy.31.live_ref, s32[1024]{0:T(1024)} %docs_ref.11, ...), custom_call_target="tpu_custom_call" | custom-call | tf_op jit(solution)/shard_map/shard_state/pallas_call | solution.py:372
  8.0 0.7 collective-permute-start
  8.8 1.8 %collective-permute-done = f32[20,72,128]{2,1,0:T(8,128)S(1)} collective-permute-done((f32[20,72,128]{2,1,0:T(8,128)S(1)}, f32[20,72,128]{2,1,0:T(8,128)S(1)}, u32[]{:S(2)}, u32[]{:S(2)}) %collective-permute-start) | collective-permute-done | bytes 737312 | tf_op jit(solution)/shard_map/ppermute | solution.py:549
  10.6 0.1 broadcast_select_fusion
  10.8 0.1 slice_add_fusion
  11.0 0.7 collective-permute-start.1
  11.7 0.0 collective-permute-done.1
  11.7 0.1 select_add_fusion.2
  11.9 1.3 %collective-permute-start.2 = (f32[648,128]{1,0:T(8,128)S(1)}, f32[648,128]{1,0:T(8,128)S(1)}, u32[]{:S(2)}, u32[]{:S(2)}) collective-permute-start(f32[648,128]{1,0:T(8,128)S(1)} %pad_maximum_fusion.2), channel_id=1, source_target_pairs={{0,4},{4,8},{1,5},{5,9},{2,6},{6,10},{3,7},{7,11},{16,20},{20,24},... | collective-permute-start | bytes 995336 | tf_op jit(solution)/shard_map/ppermute | solution.py:575
  13.2 17.9 %collective-permute-done.2 = f32[648,128]{1,0:T(8,128)S(1)} collective-permute-done((f32[648,128]{1,0:T(8,128)S(1)}, f32[648,128]{1,0:T(8,128)S(1)}, u32[]{:S(2)}, u32[]{:S(2)}) %collective-permute-start.2) | collective-permute-done | bytes 331808 | tf_op jit(solution)/shard_map/ppermute | solution.py:575
  31.1 0.1 select_add_fusion.1
  31.2 1.9 %collective-permute-start.3 = (f32[648,128]{1,0:T(8,128)S(1)}, f32[648,128]{1,0:T(8,128)S(1)}, u32[]{:S(2)}, u32[]{:S(2)}) collective-permute-start(f32[648,128]{1,0:T(8,128)S(1)} %pad_maximum_fusion.1), channel_id=1, source_target_pairs={{4,8},{8,12},{5,9},{9,13},{6,10},{10,14},{7,11},{11,15},{20,24},{2... | collective-permute-start | bytes 995336 | tf_op jit(solution)/shard_map/ppermute | solution.py:575
  33.1 7.5 %collective-permute-done.3 = f32[648,128]{1,0:T(8,128)S(1)} collective-permute-done((f32[648,128]{1,0:T(8,128)S(1)}, f32[648,128]{1,0:T(8,128)S(1)}, u32[]{:S(2)}, u32[]{:S(2)}) %collective-permute-start.3) | collective-permute-done | bytes 331808 | tf_op jit(solution)/shard_map/ppermute | solution.py:575
  40.6 0.1 select_add_fusion
  40.7 0.0 copy-start.1
  40.8 2.2 %collective-permute-start.4 = (f32[648,128]{1,0:T(8,128)S(1)}, f32[648,128]{1,0:T(8,128)S(1)}, u32[]{:S(2)}, u32[]{:S(2)}) collective-permute-start(f32[648,128]{1,0:T(8,128)S(1)} %pad_maximum_fusion), channel_id=1, source_target_pairs={{8,12},{9,13},{10,14},{11,15},{24,28},{25,29},{26,30},{27,31}} | collective-permute-start | bytes 995336 | tf_op jit(solution)/shard_map/ppermute | solution.py:575
  43.0 4.7 %collective-permute-done.4 = f32[648,128]{1,0:T(8,128)S(1)} collective-permute-done((f32[648,128]{1,0:T(8,128)S(1)}, f32[648,128]{1,0:T(8,128)S(1)}, u32[]{:S(2)}, u32[]{:S(2)}) %collective-permute-start.4) | collective-permute-done | bytes 331808 | tf_op jit(solution)/shard_map/ppermute | solution.py:575
  47.8 0.2 select_select_fusion.1
  47.9 0.2 fusion
  48.1 3.3 %collective-permute-start.5 = (f32[20,64,128]{2,1,0:T(8,128)S(1)}, f32[20,64,128]{2,1,0:T(8,128)S(1)}, u32[]{:S(2)}, u32[]{:S(2)}) collective-permute-start(f32[20,64,128]{2,1,0:T(8,128)S(1)} %get-tuple-element.47), channel_id=1, source_target_pairs={{0,1},{1,0},{2,3},{3,2},{4,5},{5,4},{6,7},{7,6},{8,9},{9,8},{10,11... | collective-permute-start | bytes 1966088 | tf_op jit(solution)/shard_map/ppermute | solution.py:589
  51.4 0.0 copy-done.1
  51.4 1.6 %prepare.1 = (f32[4,256,256]{2,1,0:T(8,128)S(1)}, bf16[1024,256]{1,0:T(8,128)(2,1)S(1)}) custom-call(s32[1024]{0:T(1024)S(1)} %copy-done.1, bf16[1024,128]{1,0:T(8,128)(2,1)} %b_ref.3, bf16[1024,128]{1,0:T(8,128)(2,1)} %c_ref.11, f32[1024,128]{1,0:T(8,128)S(1)} %get-tuple-element.28.col_ref, s32[1,1024]{1,0:T(1,128)S(1)} %bitcast.75), custom_call_target="tpu_custom_call" | custom-call | tf_op jit(solution)/shard_map/prepare/pallas_call | solution.py:436
  52.9 4.9 %shard_map.139 = (f32[1024,512]{1,0:T(8,128)S(1)}, f32[1024,512]{1,0:T(8,128)S(1)}) custom-call(s32[1]{0:T(128)S(6)} %copy.31.live_ref, s32[1024]{0:T(1024)S(1)} %copy-done.1, bf16[1024,2560]{1,0:T(8,128)(2,1)} %x_ref.9, bf16[1024,2560]{1,0:T(8,128)(2,1)} %z_ref.7, bf16[1024,128]{1,0:T(8,128)(2,1)} %c_ref.11, f32[40,1024]{1,0:T(8,128)S(1)} %get-tuple-element.26.cum_ref, ...), custom_call_target="tpu_custom_call" | custom-call | flops 629145600 | bytes 5242880 | tf_op jit(solution)/shard_map/pallas_call | solution.py:465
  57.8 4.9 %shard_map.138 = (f32[1024,512]{1,0:T(8,128)S(1)}, f32[1024,512]{1,0:T(8,128)S(1)}) custom-call(s32[1]{0:T(128)S(6)} %copy.31.live_ref, s32[1024]{0:T(1024)S(1)} %copy-done.1, bf16[1024,2560]{1,0:T(8,128)(2,1)} %x_ref.9, bf16[1024,2560]{1,0:T(8,128)(2,1)} %z_ref.7, bf16[1024,128]{1,0:T(8,128)(2,1)} %c_ref.11, f32[40,1024]{1,0:T(8,128)S(1)} %get-tuple-element.26.cum_ref, ...), custom_call_target="tpu_custom_call" | custom-call | flops 629145600 | bytes 5242880 | tf_op jit(solution)/shard_map/pallas_call | solution.py:465
  62.7 6.4 %shard_map.137 = (f32[1024,768]{1,0:T(8,128)S(1)}, f32[1024,768]{1,0:T(8,128)S(1)}) custom-call(s32[1]{0:T(128)S(6)} %copy.31.live_ref, s32[1024]{0:T(1024)S(1)} %copy-done.1, bf16[1024,2560]{1,0:T(8,128)(2,1)} %x_ref.9, bf16[1024,2560]{1,0:T(8,128)(2,1)} %z_ref.7, bf16[1024,128]{1,0:T(8,128)(2,1)} %c_ref.11, f32[40,1024]{1,0:T(8,128)S(1)} %get-tuple-element.26.cum_ref, ...), custom_call_target="tpu_custom_call" | custom-call | flops 943718400 | bytes 7864320 | tf_op jit(solution)/shard_map/pallas_call | solution.py:465
  69.1 0.0 copy-start
  69.1 6.4 %shard_map.136 = (f32[1024,768]{1,0:T(8,128)S(1)}, f32[1024,768]{1,0:T(8,128)S(1)}) custom-call(s32[1]{0:T(128)S(6)} %copy.31.live_ref, s32[1024]{0:T(1024)S(1)} %copy-done.1, bf16[1024,2560]{1,0:T(8,128)(2,1)} %x_ref.9, bf16[1024,2560]{1,0:T(8,128)(2,1)} %z_ref.7, bf16[1024,128]{1,0:T(8,128)(2,1)} %c_ref.11, f32[40,1024]{1,0:T(8,128)S(1)} %get-tuple-element.26.cum_ref, ...), custom_call_target="tpu_custom_call" | custom-call | flops 943718400 | bytes 7864320 | tf_op jit(solution)/shard_map/pallas_call | solution.py:465
  75.6 0.0 collective-permute-done.5.other_ref
  75.6 0.0 copy-done
  75.6 0.0 copy-start.2
  75.6 2.7 %join.1 = (f32[1024,2560]{1,0:T(8,128)S(1)}, f32[1,1024]{1,0:T(1,128)S(1)}) custom-call(s32[2]{0:T(128)S(1)} %pad_add_fusion.spot_ref, f32[20,64,128]{2,1,0:T(8,128)S(1)} %get-tuple-element.48.own_ref, f32[20,64,128]{2,1,0:T(8,128)S(1)} %collective-permute-done.5.other_ref, bf16[1024,128]{1,0:T(8,128)(2,1)S(1)} %copy-done, ...), custom_call_target="tpu_custom_call" | custom-call | tf_op jit(solution)/shard_map/join/pallas_call | solution.py:501
  78.2 0.3 collective-permute-start.6
  78.6 0.0 copy-done.2
  78.6 2.2 %collective-permute-done.6.more_ref = f32[1,1024]{1,0:T(1,128)S(1)} collective-permute-done((f32[1,1024]{1,0:T(1,128)S(1)}, f32[1,1024]{1,0:T(1,128)S(1)}, u32[]{:S(2)}, u32[]{:S(2)}) %collective-permute-start.6) | collective-permute-done | bytes 4128 | tf_op jit(solution)/shard_map/ppermute | solution.py:540
  80.8 2.7 %norm.1 = bf16[1024,2560]{1,0:T(8,128)(2,1)} custom-call(f32[1,1024]{1,0:T(1,128)S(1)} %get-tuple-element.41.square_ref, f32[1,1024]{1,0:T(1,128)S(1)} %collective-permute-done.6.more_ref, f32[1,2560]{1,0:T(1,128)S(1)} %reshape.78.gain_ref, f32[1024,2560]{1,0:T(8,128)S(1)} %get-tuple-element.42.gated_ref), custom_call_target="tpu_custom_call" | custom-call | tf_op jit(solution)/shard_map/norm/pallas_call | solution.py:515
  (24 shorter events, 0.3 us)
Async XLA Ops:
  8.0 2.6 %collective-permute-start = (f32[20,72,128]{2,1,0:T(8,128)S(1)}, f32[20,72,128]{2,1,0:T(8,128)S(1)}, u32[]{:S(2)}, u32[]{:S(2)}) collective-permute-start(f32[20,72,128]{2,1,0:T(8,128)S(1)} %get-tuple-element.25), channel_id=1, source_target_pairs={{0,1},{1,0},{2,3},{3,2},{4,5},{5,4},{6,7},{7,6},{8,9},{9,8},{10,11... | collective-permute-start | bytes 2211848 | tf_op jit(solution)/shard_map/ppermute | solution.py:549
  11.0 0.7 collective-permute-start.1
  11.9 19.2 %collective-permute-start.2 = (f32[648,128]{1,0:T(8,128)S(1)}, f32[648,128]{1,0:T(8,128)S(1)}, u32[]{:S(2)}, u32[]{:S(2)}) collective-permute-start(f32[648,128]{1,0:T(8,128)S(1)} %pad_maximum_fusion.2), channel_id=1, source_target_pairs={{0,4},{4,8},{1,5},{5,9},{2,6},{6,10},{3,7},{7,11},{16,20},{20,24},... | collective-permute-start | bytes 995336 | tf_op jit(solution)/shard_map/ppermute | solution.py:575
  31.2 9.4 %collective-permute-start.3 = (f32[648,128]{1,0:T(8,128)S(1)}, f32[648,128]{1,0:T(8,128)S(1)}, u32[]{:S(2)}, u32[]{:S(2)}) collective-permute-start(f32[648,128]{1,0:T(8,128)S(1)} %pad_maximum_fusion.1), channel_id=1, source_target_pairs={{4,8},{8,12},{5,9},{9,13},{6,10},{10,14},{7,11},{11,15},{20,24},{2... | collective-permute-start | bytes 995336 | tf_op jit(solution)/shard_map/ppermute | solution.py:575
  40.7 10.7 %copy-start.1 = (s32[1024]{0:T(1024)S(1)}, s32[1024]{0:T(1024)}, u32[]{:S(2)}) copy-start(s32[1024]{0:T(1024)} %docs_ref.11) | copy-start | bytes 12292
  40.8 7.0 %collective-permute-start.4 = (f32[648,128]{1,0:T(8,128)S(1)}, f32[648,128]{1,0:T(8,128)S(1)}, u32[]{:S(2)}, u32[]{:S(2)}) collective-permute-start(f32[648,128]{1,0:T(8,128)S(1)} %pad_maximum_fusion), channel_id=1, source_target_pairs={{8,12},{9,13},{10,14},{11,15},{24,28},{25,29},{26,30},{27,31}} | collective-permute-start | bytes 995336 | tf_op jit(solution)/shard_map/ppermute | solution.py:575
  48.1 27.5 %collective-permute-start.5 = (f32[20,64,128]{2,1,0:T(8,128)S(1)}, f32[20,64,128]{2,1,0:T(8,128)S(1)}, u32[]{:S(2)}, u32[]{:S(2)}) collective-permute-start(f32[20,64,128]{2,1,0:T(8,128)S(1)} %get-tuple-element.47), channel_id=1, source_target_pairs={{0,1},{1,0},{2,3},{3,2},{4,5},{5,4},{6,7},{7,6},{8,9},{9,8},{10,11... | collective-permute-start | bytes 1966088 | tf_op jit(solution)/shard_map/ppermute | solution.py:589
  69.1 6.4 %copy-start = (bf16[1024,128]{1,0:T(8,128)(2,1)S(1)}, bf16[1024,128]{1,0:T(8,128)(2,1)}, u32[]{:S(2)}) copy-start(bf16[1024,128]{1,0:T(8,128)(2,1)} %c_ref.11) | copy-start | bytes 786436
  75.6 3.0 %copy-start.2 = (f32[2560]{0:T(1024)S(1)}, f32[2560]{0:T(1024)}, u32[]{:S(2)}) copy-start(f32[2560]{0:T(1024)} %param.22) | copy-start | bytes 30724
  78.2 2.5 %collective-permute-start.6 = (f32[1,1024]{1,0:T(1,128)S(1)}, f32[1,1024]{1,0:T(1,128)S(1)}, u32[]{:S(2)}, u32[]{:S(2)}) collective-permute-start(f32[1,1024]{1,0:T(1,128)S(1)} %get-tuple-element.41.square_ref), channel_id=1, source_target_pairs={{0,2},{2,0},{1,3},{3,1},{4,6},{6,4},{5,7},{7,5},{8,10},{10,8},{9,1... | collective-permute-start | bytes 12296 | tf_op jit(solution)/shard_map/ppermute | solution.py:540
